TPU v7x, 256 devices: a whole 4x4x8 slice. The times are simulated.
256 devices in a mesh: noise: 16 (over y_lo, z), tile: 16 (over y_hi, x, core).
Axes of the slice: x: 4, y: 4 (y_hi: 2, y_lo: 2; y = y_hi * 2 + y_lo), z: 8, core: 2. Of those that a mesh axis runs over, the one named last changes fastest.
Arguments:
- queue_state: float32 [64, 69, 16, 256], P('noise', None, 'tile'), may hold values from -6 to 6
- fresh_noise: float32 [2, 69, 16, 256], P(None, None, 'tile'), may hold values from -6 to 6
- plan: float32 [17], replicated, may hold values from 0.5 to 2
- levels: int32 [64], P('noise'), may hold values from 0 to 15
- neighbours: int32 [16, 4], replicated, may hold values from -1 to 15, as said below
- in_weight: bfloat16 [256, 69], replicated, may hold values from -0.75 to 0.75
- level_embed: float32 [256], replicated, may hold values from -3 to 3
- conv_weight: bfloat16 [9, 256, 256], replicated, may hold values from -0.125 to 0.125
- norm_gain: float32 [256], replicated, may hold values from 0.5 to 1.5
- query_weight: bfloat16 [256, 256], replicated, may hold values from -0.375 to 0.375
- memory_weight: bfloat16 [512, 256], replicated, may hold values from -0.375 to 0.375
- attend_out: bfloat16 [256, 256], replicated, may hold values from -0.375 to 0.375
- decode_weight: bfloat16 [69, 256], replicated, may hold values from -0.375 to 0.375
Outputs:
- queue_after: float32 [64, 69, 16, 256], P('noise', None, 'tile')
Inputs may be any that keep to these rules, and one draw needn't show every extreme that they name: The tiles fill a grid of 2 rows and 8 columns, each tile once, in an arrangement drawn per run; west and east neighbours run along a row, which closes into a loop; -1 stands for the missing north neighbour of the first row and south neighbour of the last row.
All inputs are finite; a program needn't handle non-finite values.
Results may differ from a plain program's by a relative error of at most 0.012.
Values may be sent and summed in bfloat16 or wider, within the bound.
No kernel may reach another device: no remote copies, remote signals or barrier semaphores. Data moves between devices by JAX's collectives and lax.ppermute only.
A program may use at most 64 MiB of HBM per device.

v0:
```python
import jax
import jax.numpy as jnp
from jax import lax
from jax.sharding import Mesh
from jax.sharding import PartitionSpec as P

FIELDS = 69
WIDTH = 256
HEADS = 8
TILE = 16
FR_DEV = 4
STEPS = 2
TILE_AXES = ("tile_0", "tile_1", "tile_2")


def copy_for_each(array, axis):
    copies = jnp.broadcast_to(array, (lax.axis_size(axis), *array.shape))
    return lax.all_to_all(copies, axis, split_axis=0, concat_axis=0, tiled=True)


def laid_out(tiles, dim):
    tiles = jnp.moveaxis(tiles, 0, dim)
    lengths = tiles.shape
    return tiles.reshape(*lengths[:dim], lengths[dim] * lengths[dim + 1], *lengths[dim + 2 :])


def gathered_by_axis(array, axes, dim):
    far, near = axes
    initial = copy_for_each(array, far)
    tiles = jnp.swapaxes(copy_for_each(initial, near), 0, 1)
    return laid_out(tiles.reshape(-1, *array.shape), dim)


def shortened(array):
    return jax.tree.map(lambda a: a.astype(jnp.bfloat16) if a.dtype == jnp.float32 else a, array)


def from_behind(block, axis, distance):
    devices = range(lax.axis_size(axis))
    route = [(i - distance, i) for i in devices if i - distance in devices]
    return lax.ppermute(block, axis, route)


def level_lookup(plan, levels):
    grid_ids = jnp.arange(plan.shape[0], dtype=jnp.int32)
    sigmas = jnp.sum(jnp.where(levels[:, None] == grid_ids[None, :], plan[None, :], 0.0), axis=1)
    sigmas_next = jnp.sum(
        jnp.where(levels[:, None] + 1 == grid_ids[None, :], plan[None, :], 0.0), axis=1
    )
    return (sigmas, sigmas_next)


def select_tile(gathered, tile_index):
    chosen = lax.dynamic_index_in_dim(gathered, jnp.maximum(tile_index, 0), 0, keepdims=False)
    return jnp.where(tile_index >= 0, chosen, jnp.zeros_like(chosen))


def pad_frames(lifted_low, neighbours):
    own_tile = lax.axis_index(TILE_AXES)
    beside_all = lax.dynamic_index_in_dim(neighbours, own_tile, 0, keepdims=False)
    rim_cells = jnp.stack(
        [
            lifted_low[:, :, :, 0],
            lifted_low[:, :, :, TILE - 1],
            lifted_low[:, :, 0, :],
            lifted_low[:, :, TILE - 1, :],
        ],
        axis=2,
    )[None]
    rim_cells = gathered_by_axis(rim_cells, (("tile_0", "tile_1"), "tile_2"), 0)
    west_col = select_tile(rim_cells, beside_all[0])[:, :, 1]
    east_col = select_tile(rim_cells, beside_all[1])[:, :, 0]
    middle = jnp.concatenate([west_col[..., None], lifted_low, east_col[..., None]], axis=3)
    north_around = lax.dynamic_index_in_dim(
        neighbours, jnp.maximum(beside_all[2], 0), 0, keepdims=False
    )
    south_around = lax.dynamic_index_in_dim(
        neighbours, jnp.maximum(beside_all[3], 0), 0, keepdims=False
    )
    north_west = select_tile(rim_cells, north_around[0])[:, :, 3, TILE - 1]
    north_east = select_tile(rim_cells, north_around[1])[:, :, 3, 0]
    south_west = select_tile(rim_cells, south_around[0])[:, :, 2, TILE - 1]
    south_east = select_tile(rim_cells, south_around[1])[:, :, 2, 0]
    north_line = select_tile(rim_cells, beside_all[2])[:, :, 3]
    south_line = select_tile(rim_cells, beside_all[3])[:, :, 2]
    north_row = jnp.concatenate([north_west[..., None], north_line, north_east[..., None]], axis=2)
    south_row = jnp.concatenate([south_west[..., None], south_line, south_east[..., None]], axis=2)
    north_row = jnp.where(beside_all[2] >= 0, north_row, jnp.zeros_like(north_row))
    south_row = jnp.where(beside_all[3] >= 0, south_row, jnp.zeros_like(south_row))
    return jnp.concatenate([north_row[:, :, None, :], middle, south_row[:, :, None, :]], axis=2)


def convolve(padded, conv_weight):
    frame_count = padded.shape[0]
    convolved = jnp.zeros((frame_count, WIDTH, TILE * TILE), jnp.float32)
    for offset in range(9):
        down_by = offset // 3
        right_by = offset % 3
        window = padded[:, :, down_by : down_by + TILE, right_by : right_by + TILE].reshape(
            frame_count, WIDTH, TILE * TILE
        )
        convolved = convolved + jnp.einsum(
            "oc,gcn->gon", conv_weight[offset], window, preferred_element_type=jnp.float32
        )
    return convolved


def project(weight, values):
    return jnp.einsum("oc,gcn->gon", weight, values, preferred_element_type=jnp.float32)


def frame_features(
    frames_now, sigmas_now, neighbours, in_weight, level_embed, conv_weight, norm_gain
):
    frame_count = frames_now.shape[0]
    in_scale = 1.0 / jnp.sqrt(sigmas_now * sigmas_now + 1.0)
    scaled = (in_scale[:, None, None] * frames_now).astype(jnp.bfloat16)
    lifted = (
        project(in_weight, scaled) + jnp.log(sigmas_now)[:, None, None] * level_embed[None, :, None]
    )
    lifted_low = lifted.astype(jnp.bfloat16)
    padded = pad_frames(lifted_low.reshape(frame_count, WIDTH, TILE, TILE), neighbours)
    convolved = convolve(padded, conv_weight)
    hidden = (lifted_low.astype(jnp.float32) + jax.nn.silu(convolved)).astype(jnp.bfloat16)
    widened = hidden.astype(jnp.float32)
    normed = (
        widened
        * lax.rsqrt(jnp.mean(widened * widened, axis=1, keepdims=True) + 1e-06)
        * norm_gain[None, :, None]
    ).astype(jnp.bfloat16)
    return (hidden, normed)


def attend(queries, memory, usable):
    cell_count = queries.shape[-1]
    head_size = WIDTH // HEADS
    query_heads = queries.reshape(FR_DEV, HEADS, head_size, cell_count)
    key_heads = memory[:, :WIDTH].reshape(2 * FR_DEV, HEADS, head_size, cell_count)
    value_heads = memory[:, WIDTH:].reshape(2 * FR_DEV, HEADS, head_size, cell_count)
    scores = jnp.einsum(
        "ihdn,jhdn->ijhn", query_heads, key_heads, preferred_element_type=jnp.float32
    ) * head_size ** (-0.5)
    scores = jnp.where(usable[None, :, None, None], scores, -jnp.inf)
    weights = jax.nn.softmax(scores, axis=1).astype(jnp.bfloat16)
    context = jnp.einsum(
        "ijhn,jhdn->ihdn", weights, value_heads, preferred_element_type=jnp.float32
    )
    return context.astype(jnp.bfloat16).reshape(FR_DEV, WIDTH, cell_count)


def take_front(queue_now, entering, is_last):
    incoming = from_behind(shortened(queue_now[0:1]), "noise", -1)
    return jnp.where(is_last, entering[None], incoming)


def rolling_step(
    queue_now,
    noise_frame,
    sigmas,
    sigmas_next,
    neighbours,
    in_weight,
    level_embed,
    conv_weight,
    norm_gain,
    query_weight,
    memory_weight,
    attend_out,
    decode_weight,
):
    position = lax.axis_index("noise")
    last_index = lax.axis_size("noise") - 1
    is_last = position == last_index
    entering = sigmas[FR_DEV - 1] * noise_frame
    shifted = jnp.concatenate([queue_now[1:], take_front(queue_now, entering, is_last)], axis=0)
    hidden, normed = frame_features(
        shifted, sigmas, neighbours, in_weight, level_embed, conv_weight, norm_gain
    )
    own_memory = project(memory_weight, normed).astype(jnp.bfloat16)
    next_memory = from_behind(own_memory, "noise", -1)
    memory = jnp.concatenate([own_memory, next_memory], axis=0)
    queries = project(query_weight, normed).astype(jnp.bfloat16)
    usable = jnp.logical_or(jnp.arange(2 * FR_DEV) < FR_DEV, jnp.logical_not(is_last))
    context = attend(queries, memory, usable)
    refined = (hidden.astype(jnp.float32) + project(attend_out, context)).astype(jnp.bfloat16)
    projected = project(decode_weight, refined)
    spread = sigmas * sigmas + 1.0
    denoised = (1.0 / spread)[:, None, None] * shifted + (sigmas / jnp.sqrt(spread))[
        :, None, None
    ] * projected
    return shifted + ((sigmas_next - sigmas) / sigmas)[:, None, None] * (shifted - denoised)


def shards(
    queue_state,
    fresh_noise,
    plan,
    levels,
    neighbours,
    in_weight,
    level_embed,
    conv_weight,
    norm_gain,
    query_weight,
    memory_weight,
    attend_out,
    decode_weight,
):
    cell_count = queue_state.shape[-1]
    queue_now = queue_state.reshape(FR_DEV, FIELDS, cell_count)
    noise_now = fresh_noise.reshape(STEPS, FIELDS, cell_count)
    sigmas, sigmas_next = level_lookup(plan, levels)
    for step_index in range(STEPS):
        queue_now = rolling_step(
            queue_now,
            noise_now[step_index],
            sigmas,
            sigmas_next,
            neighbours,
            in_weight,
            level_embed,
            conv_weight,
            norm_gain,
            query_weight,
            memory_weight,
            attend_out,
            decode_weight,
        )
    return queue_now.reshape(queue_state.shape)


def solution(mesh):
    split = Mesh(
        mesh.devices.reshape(mesh.shape["noise"], 2, 4, 2), ("noise", "tile_0", "tile_1", "tile_2")
    )
    placed = (
        P("noise", None, TILE_AXES, None),
        P(None, None, TILE_AXES, None),
        P(),
        P("noise"),
        P(),
        P(),
        P(),
        P(),
        P(),
        P(),
        P(),
        P(),
        P(),
    )
    return jax.shard_map(
        shards,
        mesh=split,
        in_specs=placed,
        out_specs=P("noise", None, TILE_AXES, None),
        check_vma=False,
    )
```

profile of v0, /device:TPU:8, one launch (start us, length us, event | category | flops | bytes accessed | tf_op | source)
XLA Modules:
  0.0 206.0 jit_solution(12198464280034061058)
XLA Ops:
  0.0 1.0 slice.331
  1.1 7.7 %collective-permute-start = (bf16[1,69,256]{2,1,0:T(8,128)(2,1)S(1)}, bf16[1,69,256]{2,1,0:T(8,128)(2,1)S(1)}, u32[]{:S(2)}, u32[]{:S(2)}) collective-permute-start(bf16[1,69,256]{2,1,0:T(8,128)(2,1)S(1)} %bitcast.358), channel_id=1, source_target_pairs={{16,0},{32,16},{48,32},{64,48},{80,64},{96,80},{112,96},{128,112},... | collective-permute-start | bytes 105992 | tf_op jit(solution)/shard_map/ppermute | solution.py:41
  8.7 0.7 broadcast_add_fusion
  9.4 1.0 fusion.118
  10.4 0.9 select_reduce_fusion
  11.3 0.6 subtract_divide_fusion
  11.9 0.7 broadcast_multiply_fusion
  12.7 0.6 slice.264
  13.3 1.1 slice.262
  14.5 0.7 fusion.97
  15.1 1.2 fusion.22
  16.5 1.1 broadcast_in_dim.42
  17.6 6.3 %all-to-all-start = ((bf16[8,1,4,256,4,16]{3,5,4,2,1,0:T(8,128)(2,1)}), bf16[8,1,4,256,4,16]{3,5,4,2,1,0:T(8,128)(2,1)S(1)}, u32[]{:S(2)}, u32[]{:S(2)}) async-start(bf16[8,1,4,256,4,16]{3,5,4,2,1,0:T(8,128)(2,1)} %broadcast_in_dim.42), calls=%async_computation | async-start | bytes 2097152 | tf_op jit(solution)/shard_map/all_to_all | solution.py:18
  26.0 0.6 fusion.119
  35.4 5.5 %all-to-all-done = bf16[8,1,4,256,4,16]{3,5,4,2,1,0:T(8,128)(2,1)S(1)} async-done(((bf16[8,1,4,256,4,16]{3,5,4,2,1,0:T(8,128)(2,1)}), bf16[8,1,4,256,4,16]{3,5,4,2,1,0:T(8,128)(2,1)S(1)}, u32[]{:S(2)}, u32[]{:S(2)}) %all-to-all-start) | async-done | bytes 1048608 | tf_op jit(solution)/shard_map/all_to_all | solution.py:18
  41.1 5.4 %all_to_all.26 = bf16[2,8,1,4,256,4,16]{4,6,5,3,1,2,0:T(8,128)(2,1)S(1)} all-to-all(bf16[2,8,1,4,256,4,16]{4,6,5,3,1,2,0:T(8,128)(2,1)S(1)} %broadcast_in_dim.43), channel_id=1, replica_groups=mesh['noise'=16,'tile_0'=2,'tile_1'=4,'tile_2'=2] {'tile_2'}, dimensions={0} | all-to-all | bytes 4194304 | tf_op jit(solution)/shard_map/all_to_all | solution.py:18
  47.7 0.7 pad_maximum_fusion.2
  48.8 0.9 copy-done.1
  52.8 0.7 fusion.32
  54.0 3.7 %collective-permute-start.1 = (bf16[4,512,256]{1,2,0:T(8,128)(2,1)S(1)}, bf16[4,512,256]{1,2,0:T(8,128)(2,1)}, u32[]{:S(2)}, u32[]{:S(2)}) collective-permute-start(bf16[4,512,256]{1,2,0:T(8,128)(2,1)S(1)} %fusion.18), channel_id=1, source_target_pairs={{16,0},{32,16},{48,32},{64,48},{80,64},{96,80},{112,96},{128,112},... | collective-permute-start | bytes 3145736 | tf_op jit(solution)/shard_map/ppermute | solution.py:41
  58.7 2.5 %copy.401 = bf16[4,8,32,256]{2,0,3,1:T(4,128)(2,1)} copy(bf16[4,8,32,256]{3,2,1,0:T(8,128)(2,1)S(1)} %bitcast.352) | data formatting | bytes 1048576 | tf_op jit(solution)/shard_map/reshape | solution.py:137
  61.2 20.0 %collective-permute-done.1 = bf16[4,512,256]{1,2,0:T(8,128)(2,1)} collective-permute-done((bf16[4,512,256]{1,2,0:T(8,128)(2,1)S(1)}, bf16[4,512,256]{1,2,0:T(8,128)(2,1)}, u32[]{:S(2)}, u32[]{:S(2)}) %collective-permute-start.1) | collective-permute-done | bytes 1048608 | tf_op jit(solution)/shard_map/ppermute | solution.py:41
  81.2 1.4 pad_maximum_fusion.1
  83.1 3.6 %copy.400 = bf16[8,8,32,256]{2,0,3,1:T(8,128)(2,1)} copy(bf16[8,8,32,256]{3,2,1,0:T(8,128)(2,1)S(1)} %bitcast.329) | data formatting | bytes 2097152 | tf_op jit(solution)/shard_map/reshape | solution.py:138
  87.3 3.5 %copy.402 = bf16[8,8,32,256]{2,0,3,1:T(8,128)(2,1)} copy(bf16[8,8,32,256]{3,2,1,0:T(8,128)(2,1)S(1)} %bitcast.330) | data formatting | bytes 2097152 | tf_op jit(solution)/shard_map/reshape | solution.py:139
  90.8 8.3 %fusion.122 = (f32[4,8,256]{0,2,1:T(8,128)}, f32[4,8,8,256]{1,0,3,2:T(4,128)}) fusion(pred[8]{0:T(512)(128)(4,1)} %compare_or_fusion, bf16[8,8,32,256]{2,0,3,1:T(8,128)(2,1)} %copy.400, bf16[4,8,32,256]{2,0,3,1:T(4,128)(2,1)S(1)} %copy-done.4), kind=kOutput, calls=%fused_computation.225 | convolution fusion | flops 4456455 | bytes 1867784 | tf_op jit(solution)/shard_map/sub | solution.py:144
  99.1 5.4 %convert_bitcast_fusion.1 = bf16[4,8,32,256]{2,0,3,1:T(4,128)(2,1)S(1)} fusion(bf16[8,8,32,256]{2,0,3,1:T(8,128)(2,1)} %copy.402, f32[4,8,8,256]{1,0,3,2:T(4,128)} %get-tuple-element.75, f32[4,8,256]{0,2,1:T(8,128)} %get-tuple-element.74), kind=kOutput, calls=%fused_computation.19 | convolution fusion | flops 4587520 | bytes 1867776 | tf_op jit(solution)/shard_map/ijhn,jhdn->ihdn/dot_general | solution.py:145
  104.5 2.2 %copy.403 = bf16[4,8,32,256]{3,2,1,0:T(8,128)(2,1)} copy(bf16[4,8,32,256]{2,0,3,1:T(4,128)(2,1)S(1)} %convert_bitcast_fusion.1) | data formatting | bytes 1048576 | tf_op jit(solution)/shard_map/convert_element_type | solution.py:148
  106.8 1.7 multiply_add_fusion
  108.5 5.6 %collective-permute-start.2 = (bf16[1,69,256]{2,1,0:T(8,128)(2,1)S(1)}, bf16[1,69,256]{2,1,0:T(8,128)(2,1)S(1)}, u32[]{:S(2)}, u32[]{:S(2)}) collective-permute-start(bf16[1,69,256]{2,1,0:T(8,128)(2,1)S(1)} %slice.463), channel_id=1, source_target_pairs={{16,0},{32,16},{48,32},{64,48},{80,64},{96,80},{112,96},{128,112},... | collective-permute-start | bytes 105992 | tf_op jit(solution)/shard_map/ppermute | solution.py:41
  114.2 1.6 collective-permute-done.2
  115.8 0.6 fusion.95
  117.2 18.5 %all_to_all.27 = bf16[8,1,4,256,4,16]{3,5,4,2,1,0:T(8,128)(2,1)S(1)} all-to-all(bf16[8,1,4,256,4,16]{3,5,4,2,1,0:T(8,128)(2,1)S(1)} %broadcast_in_dim.46), channel_id=1, replica_groups=mesh['noise'=16,'tile_0'=2,'tile_1'=4,'tile_2'=2] {'tile_0','tile_1'}, dimensions={0} | all-to-all | bytes 2097152 | tf_op jit(solution)/shard_map/all_to_all | solution.py:18
  136.0 5.4 %all_to_all.28 = bf16[2,8,1,4,256,4,16]{4,6,5,3,1,2,0:T(8,128)(2,1)S(1)} all-to-all(bf16[2,8,1,4,256,4,16]{4,6,5,3,1,2,0:T(8,128)(2,1)S(1)} %broadcast_in_dim.47), channel_id=1, replica_groups=mesh['noise'=16,'tile_0'=2,'tile_1'=4,'tile_2'=2] {'tile_2'}, dimensions={0} | all-to-all | bytes 4194304 | tf_op jit(solution)/shard_map/all_to_all | solution.py:18
  142.6 0.7 pad_maximum_fusion.3
  143.7 0.9 copy-done.2
  147.7 0.7 fusion.35
  148.9 6.0 %collective-permute-start.3 = (bf16[4,512,256]{1,2,0:T(8,128)(2,1)S(1)}, bf16[4,512,256]{1,2,0:T(8,128)(2,1)}, u32[]{:S(2)}, u32[]{:S(2)}) collective-permute-start(bf16[4,512,256]{1,2,0:T(8,128)(2,1)S(1)} %fusion.19), channel_id=1, source_target_pairs={{16,0},{32,16},{48,32},{64,48},{80,64},{96,80},{112,96},{128,112},... | collective-permute-start | bytes 3145736 | tf_op jit(solution)/shard_map/ppermute | solution.py:41
  155.3 2.5 %copy.436 = bf16[4,8,32,256]{2,0,3,1:T(4,128)(2,1)} copy(bf16[4,8,32,256]{3,2,1,0:T(8,128)(2,1)S(1)} %bitcast.353) | data formatting | bytes 1048576 | tf_op jit(solution)/shard_map/reshape | solution.py:137
  157.8 19.9 %collective-permute-done.3 = bf16[4,512,256]{1,2,0:T(8,128)(2,1)} collective-permute-done((bf16[4,512,256]{1,2,0:T(8,128)(2,1)S(1)}, bf16[4,512,256]{1,2,0:T(8,128)(2,1)}, u32[]{:S(2)}, u32[]{:S(2)}) %collective-permute-start.3) | collective-permute-done | bytes 1048608 | tf_op jit(solution)/shard_map/ppermute | solution.py:41
  177.7 1.4 pad_maximum_fusion
  179.6 3.6 %copy.435 = bf16[8,8,32,256]{2,0,3,1:T(8,128)(2,1)} copy(bf16[8,8,32,256]{3,2,1,0:T(8,128)(2,1)S(1)} %bitcast.332) | data formatting | bytes 2097152 | tf_op jit(solution)/shard_map/reshape | solution.py:138
  183.8 3.5 %copy.437 = bf16[8,8,32,256]{2,0,3,1:T(8,128)(2,1)} copy(bf16[8,8,32,256]{3,2,1,0:T(8,128)(2,1)S(1)} %bitcast.333) | data formatting | bytes 2097152 | tf_op jit(solution)/shard_map/reshape | solution.py:139
  187.3 8.3 %fusion.123 = (f32[4,8,256]{0,2,1:T(8,128)}, f32[4,8,8,256]{1,0,3,2:T(4,128)}) fusion(pred[8]{0:T(512)(128)(4,1)S(1)} %copy-done.28, bf16[8,8,32,256]{2,0,3,1:T(8,128)(2,1)} %copy.435, bf16[4,8,32,256]{2,0,3,1:T(4,128)(2,1)S(1)} %copy-done.3), kind=kOutput, calls=%fused_computation.226 | convolution fusion | flops 4456455 | bytes 1867784 | tf_op jit(solution)/shard_map/sub | solution.py:144
  195.6 5.4 %convert_bitcast_fusion = bf16[4,8,32,256]{2,0,3,1:T(4,128)(2,1)S(1)} fusion(bf16[8,8,32,256]{2,0,3,1:T(8,128)(2,1)} %copy.437, f32[4,8,8,256]{1,0,3,2:T(4,128)} %get-tuple-element.79, f32[4,8,256]{0,2,1:T(8,128)} %get-tuple-element.78), kind=kOutput, calls=%fused_computation.18 | convolution fusion | flops 4587520 | bytes 1867776 | tf_op jit(solution)/shard_map/ijhn,jhdn->ihdn/dot_general | solution.py:145
  201.1 2.2 %copy.438 = bf16[4,8,32,256]{3,2,1,0:T(8,128)(2,1)} copy(bf16[4,8,32,256]{2,0,3,1:T(4,128)(2,1)S(1)} %convert_bitcast_fusion) | data formatting | bytes 1048576 | tf_op jit(solution)/shard_map/convert_element_type | solution.py:148
  203.3 1.7 add_bitcast_fusion
  205.0 1.0 copy.441
  (139 shorter events, 15.6 us)
Async XLA Ops:
  0.0 53.5 %copy-start = (bf16[512,256]{1,0:T(8,128)(2,1)S(1)}, bf16[512,256]{1,0:T(8,128)(2,1)}, u32[]{:S(2)}) copy-start(bf16[512,256]{1,0:T(8,128)(2,1)} %param.23) | copy-start | bytes 786436
  1.1 13.4 %collective-permute-start = (bf16[1,69,256]{2,1,0:T(8,128)(2,1)S(1)}, bf16[1,69,256]{2,1,0:T(8,128)(2,1)S(1)}, u32[]{:S(2)}, u32[]{:S(2)}) collective-permute-start(bf16[1,69,256]{2,1,0:T(8,128)(2,1)S(1)} %bitcast.358), channel_id=1, source_target_pairs={{16,0},{32,16},{48,32},{64,48},{80,64},{96,80},{112,96},{128,112},... | collective-permute-start | bytes 105992 | tf_op jit(solution)/shard_map/ppermute | solution.py:41
  11.9 4.4 %copy-start.17 = (f32[4]{0:T(128)}, f32[4]{0:T(128)S(1)}, u32[]{:S(2)}) copy-start(f32[4]{0:T(128)S(1)} %get-tuple-element.68) | copy-start | bytes 52
  12.7 3.7 %copy-start.14 = (f32[4,256]{1,0:T(4,128)}, f32[4,256]{1,0:T(4,128)S(1)}, u32[]{:S(2)}) copy-start(f32[4,256]{1,0:T(4,128)S(1)} %broadcast_multiply_fusion) | copy-start | bytes 12292
  14.4 3.2 %copy-start.7 = (f32[3,69,1,256]{3,1,0,2:T(8,128)}, f32[3,69,1,256]{3,1,0,2:T(8,128)S(1)}, u32[]{:S(2)}) copy-start(f32[3,69,1,256]{3,1,0,2:T(8,128)S(1)} %copy.511) | copy-start | bytes 635908
  16.4 7.6 %copy-start.16 = (s32[16,4]{0,1:T(4,128)S(1)}, s32[16,4]{0,1:T(4,128)}, u32[]{:S(2)}) copy-start(s32[16,4]{0,1:T(4,128)} %param.17) | copy-start | bytes 772
  17.6 23.3 %all-to-all-start = ((bf16[8,1,4,256,4,16]{3,5,4,2,1,0:T(8,128)(2,1)}), bf16[8,1,4,256,4,16]{3,5,4,2,1,0:T(8,128)(2,1)S(1)}, u32[]{:S(2)}, u32[]{:S(2)}) async-start(bf16[8,1,4,256,4,16]{3,5,4,2,1,0:T(8,128)(2,1)} %broadcast_in_dim.42), calls=%async_computation | async-start | bytes 2097152 | tf_op jit(solution)/shard_map/all_to_all | solution.py:18
  48.5 1.3 copy-start.1
  52.8 0.7 copy-start.19
  52.8 5.5 %copy-start.25 = (bf16[256,256]{1,0:T(8,128)(2,1)S(1)}, bf16[256,256]{1,0:T(8,128)(2,1)}, u32[]{:S(2)}) copy-start(bf16[256,256]{1,0:T(8,128)(2,1)} %param.22) | copy-start | bytes 393220
  53.5 7.7 %copy-start.9 = (bf16[4,256,256]{1,2,0:T(8,128)(2,1)}, bf16[4,256,256]{1,2,0:T(8,128)(2,1)S(1)}, u32[]{:S(2)}) copy-start(bf16[4,256,256]{1,2,0:T(8,128)(2,1)S(1)} %get-tuple-element.73) | copy-start | bytes 1572868
  54.0 27.2 %collective-permute-start.1 = (bf16[4,512,256]{1,2,0:T(8,128)(2,1)S(1)}, bf16[4,512,256]{1,2,0:T(8,128)(2,1)}, u32[]{:S(2)}, u32[]{:S(2)}) collective-permute-start(bf16[4,512,256]{1,2,0:T(8,128)(2,1)S(1)} %fusion.18), channel_id=1, source_target_pairs={{16,0},{32,16},{48,32},{64,48},{80,64},{96,80},{112,96},{128,112},... | collective-permute-start | bytes 3145736 | tf_op jit(solution)/shard_map/ppermute | solution.py:41
  87.3 3.5 %copy-start.4 = (bf16[4,8,32,256]{2,0,3,1:T(4,128)(2,1)S(1)}, bf16[4,8,32,256]{2,0,3,1:T(4,128)(2,1)}, u32[]{:S(2)}) copy-start(bf16[4,8,32,256]{2,0,3,1:T(4,128)(2,1)} %copy.401) | copy-start | bytes 1572868
  104.5 2.3 %copy-start.8 = (f32[3,69,1,256]{3,1,0,2:T(8,128)S(1)}, f32[3,69,1,256]{3,1,0,2:T(8,128)}, u32[]{:S(2)}) copy-start(f32[3,69,1,256]{3,1,0,2:T(8,128)} %copy-done.7) | copy-start | bytes 635908
  104.5 2.2 %copy-start.10 = (bf16[4,256,256]{1,2,0:T(8,128)(2,1)S(1)}, bf16[4,256,256]{1,2,0:T(8,128)(2,1)}, u32[]{:S(2)}) copy-start(bf16[4,256,256]{1,2,0:T(8,128)(2,1)} %copy-done.9) | copy-start | bytes 1572868
  104.5 2.2 %copy-start.21 = (f32[4]{0:T(128)S(1)}, f32[4]{0:T(128)}, u32[]{:S(2)}) copy-start(f32[4]{0:T(128)} %get-tuple-element.67) | copy-start | bytes 52
  104.5 11.9 %copy-start.15 = (f32[4,256]{1,0:T(4,128)S(1)}, f32[4,256]{1,0:T(4,128)}, u32[]{:S(2)}) copy-start(f32[4,256]{1,0:T(4,128)} %copy-done.14) | copy-start | bytes 12292
  106.8 9.7 %copy-start.13 = (bf16[256,69]{0,1:T(8,128)(2,1)S(1)}, bf16[256,69]{0,1:T(8,128)(2,1)}, u32[]{:S(2)}) copy-start(bf16[256,69]{0,1:T(8,128)(2,1)} %param.18) | copy-start | bytes 105988
  106.8 9.7 %copy-start.18 = (f32[4]{0:T(128)S(1)}, f32[4]{0:T(128)}, u32[]{:S(2)}) copy-start(f32[4]{0:T(128)} %copy-done.17) | copy-start | bytes 52
  108.5 7.3 %collective-permute-start.2 = (bf16[1,69,256]{2,1,0:T(8,128)(2,1)S(1)}, bf16[1,69,256]{2,1,0:T(8,128)(2,1)S(1)}, u32[]{:S(2)}, u32[]{:S(2)}) collective-permute-start(bf16[1,69,256]{2,1,0:T(8,128)(2,1)S(1)} %slice.463), channel_id=1, source_target_pairs={{16,0},{32,16},{48,32},{64,48},{80,64},{96,80},{112,96},{128,112},... | collective-permute-start | bytes 105992 | tf_op jit(solution)/shard_map/ppermute | solution.py:41
  114.2 2.9 %copy-start.5 = (f32[3,69,256]{2,1,0:T(8,128)}, f32[3,69,256]{2,1,0:T(8,128)S(1)}, u32[]{:S(2)}) copy-start(f32[3,69,256]{2,1,0:T(8,128)S(1)} %slice.352) | copy-start | bytes 635908
  143.3 1.3 copy-start.2
  147.6 0.7 copy-start.20
  147.7 7.3 %copy-start.26 = (bf16[256,256]{1,0:T(8,128)(2,1)S(1)}, bf16[256,256]{1,0:T(8,128)(2,1)}, u32[]{:S(2)}) copy-start(bf16[256,256]{1,0:T(8,128)(2,1)} %param.22) | copy-start | bytes 393220
  148.3 6.6 %copy-start.11 = (bf16[4,256,256]{1,2,0:T(8,128)(2,1)}, bf16[4,256,256]{1,2,0:T(8,128)(2,1)S(1)}, u32[]{:S(2)}) copy-start(bf16[4,256,256]{1,2,0:T(8,128)(2,1)S(1)} %get-tuple-element.77) | copy-start | bytes 1572868
  148.9 28.8 %collective-permute-start.3 = (bf16[4,512,256]{1,2,0:T(8,128)(2,1)S(1)}, bf16[4,512,256]{1,2,0:T(8,128)(2,1)}, u32[]{:S(2)}, u32[]{:S(2)}) collective-permute-start(bf16[4,512,256]{1,2,0:T(8,128)(2,1)S(1)} %fusion.19), channel_id=1, source_target_pairs={{16,0},{32,16},{48,32},{64,48},{80,64},{96,80},{112,96},{128,112},... | collective-permute-start | bytes 3145736 | tf_op jit(solution)/shard_map/ppermute | solution.py:41
  183.8 3.5 %copy-start.3 = (bf16[4,8,32,256]{2,0,3,1:T(4,128)(2,1)S(1)}, bf16[4,8,32,256]{2,0,3,1:T(4,128)(2,1)}, u32[]{:S(2)}) copy-start(bf16[4,8,32,256]{2,0,3,1:T(4,128)(2,1)} %copy.436) | copy-start | bytes 1572868
  183.8 3.5 %copy-start.28 = (pred[8]{0:T(512)(128)(4,1)S(1)}, pred[8]{0:T(512)(128)(4,1)}, u32[]{:S(2)}) copy-start(pred[8]{0:T(512)(128)(4,1)} %compare_or_fusion) | copy-start | bytes 28
  201.0 2.3 %copy-start.6 = (f32[3,69,256]{2,1,0:T(8,128)S(1)}, f32[3,69,256]{2,1,0:T(8,128)}, u32[]{:S(2)}) copy-start(f32[3,69,256]{2,1,0:T(8,128)} %copy-done.5) | copy-start | bytes 635908
  201.0 2.3 %copy-start.12 = (bf16[4,256,256]{1,2,0:T(8,128)(2,1)S(1)}, bf16[4,256,256]{1,2,0:T(8,128)(2,1)}, u32[]{:S(2)}) copy-start(bf16[4,256,256]{1,2,0:T(8,128)(2,1)} %copy-done.11) | copy-start | bytes 1572868
  201.0 2.3 %copy-start.22 = (f32[4]{0:T(128)S(1)}, f32[4]{0:T(128)}, u32[]{:S(2)}) copy-start(f32[4]{0:T(128)} %get-tuple-element.67) | copy-start | bytes 52
  201.0 2.3 %copy-start.23 = (f32[4]{0:T(128)S(1)}, f32[4]{0:T(128)}, u32[]{:S(2)}) copy-start(f32[4]{0:T(128)} %get-tuple-element.69) | copy-start | bytes 52
  201.1 2.3 %copy-start.24 = (f32[4]{0:T(128)S(1)}, f32[4]{0:T(128)}, u32[]{:S(2)}) copy-start(f32[4]{0:T(128)} %get-tuple-element.70) | copy-start | bytes 52
  201.1 2.3 %copy-start.27 = (bf16[69,256]{1,0:T(8,128)(2,1)S(1)}, bf16[69,256]{1,0:T(8,128)(2,1)}, u32[]{:S(2)}) copy-start(bf16[69,256]{1,0:T(8,128)(2,1)} %param.25) | copy-start | bytes 105988
where the time goes:
time: 207 us; the launch traced here: 206 us
  waiting for transfers between devices  47 us (23%)
  matrix products  40.9 us (20%)
  local copies, waits for them, and re-layouts  38 us (18%)
  starting transfers between devices  29.4 us (14%)
  blocking collectives  29.3 us (14%)
  between operations  11.1 us (5%)
  other arithmetic  10.4 us (5%)
    ppermute x4, waiting for transfers between devices, from_behind(): return lax.ppermute(block, axis, route)  41.5 us
    all_to_all x3, blocking collectives, copy_for_each(): return lax.all_to_all(copies, axis, split_axis=0, concat_axis=0, tiled=True)  29.3 us
    ppermute x4, starting transfers between devices, from_behind(): return lax.ppermute(block, axis, route)  23 us
    sub x2, matrix products, attend(): weights = jax.nn.softmax(scores, axis=1).astype(jnp.bfloat16)  16.6 us
    dot_general x2, matrix products, attend(): jnp.einsum('ijhn,jhdn->ihdn', weights, value_heads, preferred_element_typ...  10.9 us
    reshape x2, local copies, waits for them, and re-layouts, attend(): memory[:, :WIDTH].reshape(2 * FR_DEV, HEADS, head_size, cell_count)  7.27 us
    reshape x2, local copies, waits for them, and re-layouts, attend(): memory[:, WIDTH:].reshape(2 * FR_DEV, HEADS, head_size, cell_count)  7.02 us
    dot_general x8, matrix products, project(): jnp.einsum('oc,gcn->gon', weight, values, preferred_element_type=jnp.floa...  6.85 us
  transfers between devices with their start and end apart: 5, of which 4 were waited for; matrix products, arithmetic and copies ran while one was open for 7% of the time, Pallas kernels for 0%

commit v1 on v0

v1 whole, which is shorter than its diff:
```python
import jax
import jax.numpy as jnp
from jax import lax
from jax.experimental import pallas as pl
from jax.experimental.pallas import tpu as pltpu
from jax.sharding import Mesh
from jax.sharding import PartitionSpec as P

FIELDS = 69
ROWS = 72
WIDTH = 256
HEADS = 8
HEAD = WIDTH // HEADS
TILE = 16
CELLS = TILE * TILE
TAPS = 9
FR_DEV = 4
STEPS = 2
NTILES = 16
TILE_AXES = ("tile_0", "tile_1", "tile_2")
BF = jnp.bfloat16
F32 = jnp.float32

VMEM = pl.BlockSpec(memory_space=pltpu.VMEM)
SMEM = pl.BlockSpec(memory_space=pltpu.SMEM)


def iota(shape, dim):
    return lax.broadcasted_iota(jnp.int32, shape, dim)


def mm(a, b):
    return jnp.dot(a, b, preferred_element_type=F32)


def mm_nt(a, b):
    return lax.dot_general(a, b, (((1,), (1,)), ((), ())), preferred_element_type=F32)


def split_hi_lo(v):
    hi = v.astype(BF).astype(F32)
    return hi, v - hi


def weights_kernel(
    in_ref, embed_ref, conv_ref, gain_ref, query_ref, memory_ref, out_ref, decode_ref,
    taps_out, lift_out, qkv_out, attend_out, decode_out, folded,
):
    rows = iota((ROWS, WIDTH), 0)
    weight = in_ref[...].astype(F32)
    unit = (iota((ROWS, FIELDS), 0) == iota((ROWS, FIELDS), 1)).astype(BF)
    lift_t = mm_nt(unit, weight.astype(BF))
    embed = jnp.broadcast_to(embed_ref[...], (ROWS, WIDTH))
    embed_hi, embed_lo = split_hi_lo(embed)
    stacked = jnp.where(
        rows == FIELDS, embed_hi, jnp.where(rows == FIELDS + 1, embed_lo, lift_t)
    ).astype(BF)
    lift_rows = jnp.where(
        rows >= FIELDS, jnp.where(rows == FIELDS + 2, embed_lo, embed_hi), lift_t
    )
    lift_out[...] = jnp.transpose(lift_rows).astype(BF)
    for tap in range(TAPS):
        both = mm_nt(stacked, conv_ref[tap])
        whole = jnp.broadcast_to(
            both[FIELDS : FIELDS + 1] + both[FIELDS + 1 : FIELDS + 2], (ROWS, WIDTH)
        )
        hi, lo = split_hi_lo(whole)
        folded[pl.ds(tap * ROWS, ROWS), :] = jnp.where(
            rows >= FIELDS, jnp.where(rows == FIELDS + 2, lo, hi), both
        )
    taps_out[...] = jnp.transpose(folded[...]).astype(BF)
    place = iota((WIDTH, WIDTH), 0)
    order = ((place % HEADS) * HEAD + place // HEADS == iota((WIDTH, WIDTH), 1)).astype(BF)
    gain = gain_ref[...]
    qkv_out[0:WIDTH, :] = (mm(order, query_ref[...]) * gain).astype(BF)
    for part in range(2):
        qkv_out[pl.ds((part + 1) * WIDTH, WIDTH), :] = (
            mm(order, memory_ref[pl.ds(part * WIDTH, WIDTH), :]) * gain
        ).astype(BF)
    attend_out[...] = mm_nt(out_ref[...], order).astype(BF)
    unit = (iota((ROWS, FIELDS), 0) == iota((ROWS, FIELDS), 1)).astype(BF)
    decode_out[...] = mm(unit, decode_ref[...]).astype(BF)


def prepare_weights(in_weight, embed, conv, gain, query, memory, attend, decode):
    return pl.pallas_call(
        weights_kernel,
        out_shape=(
            jax.ShapeDtypeStruct((WIDTH, TAPS * ROWS), BF),
            jax.ShapeDtypeStruct((WIDTH, ROWS), BF),
            jax.ShapeDtypeStruct((3 * WIDTH, WIDTH), BF),
            jax.ShapeDtypeStruct((WIDTH, WIDTH), BF),
            jax.ShapeDtypeStruct((ROWS, WIDTH), BF),
        ),
        in_specs=[VMEM] * 8,
        out_specs=(VMEM,) * 5,
        scratch_shapes=[pltpu.VMEM((TAPS * ROWS, WIDTH), F32)],
        name="weights",
    )(in_weight, embed.reshape(1, WIDTH), conv, gain.reshape(1, WIDTH), query, memory, attend, decode)


def border_kernel(place_ref, near_ref, queue_ref, fresh_ref, frames_out, slots_out, full, lines):
    me = place_ref[0]
    full[...] = jnp.zeros_like(full)
    for f in range(FR_DEV):
        full[pl.ds(f * ROWS, FIELDS), :] = queue_ref[f]
    full[pl.ds(FR_DEV * ROWS, FIELDS), :] = fresh_ref[0]
    frames = full[...].astype(BF)
    for f in range(FR_DEV):
        frames_out[f] = full[pl.ds(f * ROWS, ROWS), :].astype(BF)
    cell = iota((CELLS, 128), 0)
    want = iota((CELLS, 128), 1)
    line = want // TILE
    along = want % TILE
    source = jnp.where(
        line == 0,
        along * TILE + TILE - 1,
        jnp.where(
            line == 1,
            along * TILE,
            jnp.where(line == 2, (TILE - 1) * TILE + along, along),
        ),
    )
    pick = jnp.logical_and(cell == source, line < 4).astype(BF)
    found = mm(frames, pick)
    lane_block = iota((ROWS, 128), 1) // TILE
    for r in range(4):
        packed = jnp.zeros((ROWS, 128), F32)
        for f in range(FR_DEV + 1):
            one = found[f * ROWS : (f + 1) * ROWS]
            turn = (TILE * (f - r)) % 128
            if turn:
                one = pltpu.roll(one, turn, 1)
            packed = jnp.where(lane_block == f, one, packed)
        lines[r] = packed.astype(BF)
    for j in range(NTILES):
        north = near_ref[j, 2]
        beside = jnp.maximum(north, near_ref[j, 3])
        from_west = jnp.logical_or(near_ref[j, 0] == me, near_ref[beside, 0] == me)
        from_east = jnp.logical_or(near_ref[j, 1] == me, near_ref[beside, 1] == me)
        vertical = jnp.where(north >= 0, 2, 3)
        code = jnp.where(from_west, 0, jnp.where(from_east, 1, vertical))
        slots_out[j] = lines[code]


def border_lines(place, near, queue, fresh):
    return pl.pallas_call(
        border_kernel,
        out_shape=(
            jax.ShapeDtypeStruct((FR_DEV, ROWS, CELLS), BF),
            jax.ShapeDtypeStruct((NTILES, ROWS, 128), BF),
        ),
        in_specs=[SMEM, SMEM, VMEM, VMEM],
        out_specs=(VMEM, VMEM),
        scratch_shapes=[
            pltpu.VMEM(((FR_DEV + 1) * ROWS, CELLS), F32),
            pltpu.VMEM((4, ROWS, 128), BF),
        ],
        name="border",
    )(place, near, queue, fresh)


def ring_kernel(place_ref, near_ref, slots_ref, frames_ref, ring_out, near_out, far_out):
    me = place_ref[0]
    north = near_ref[me, 2]
    beside = jnp.maximum(north, near_ref[me, 3])
    west = slots_ref[near_ref[me, 0]].astype(F32)
    east = slots_ref[near_ref[me, 1]].astype(F32)
    line = slots_ref[beside].astype(F32)
    corner_west = slots_ref[near_ref[beside, 0]].astype(F32)
    corner_east = slots_ref[near_ref[beside, 1]].astype(F32)
    lane = iota((ROWS, 128), 1)
    below = north >= 0
    west_end = jnp.where(below, pltpu.roll(corner_west, 128 - (TILE - 1), 1), corner_west)
    east_end = jnp.where(below, pltpu.roll(corner_east, 128 - (TILE - 1), 1), corner_east)
    ends = jnp.where(lane % TILE == 0, west_end, pltpu.roll(east_end, 1, 1))
    sides = (west, east, line, ends)
    rings = []
    for f in range(FR_DEV + 1):
        ring = jnp.zeros((ROWS, 128), F32)
        for r in range(4):
            turn = (TILE * (r - f)) % 128
            one = pltpu.roll(sides[r], turn, 1) if turn else sides[r]
            keep = lane // TILE == r if r < 3 else jnp.logical_and(lane >= 48, lane < 50)
            ring = jnp.where(keep, one, ring)
        rings.append(ring)
        ring_out[f] = ring.astype(BF)
    for pair in range(2):
        near_out[pair] = jnp.where(
            lane < 64, rings[2 * pair], pltpu.roll(rings[2 * pair + 1], 64, 1)
        ).astype(BF)
    far_out[:, 0:CELLS] = frames_ref[0]
    far_out[:, CELLS : CELLS + 128] = rings[0].astype(BF)


def ring_cells(place, near, slots, frames):
    return pl.pallas_call(
        ring_kernel,
        out_shape=(
            jax.ShapeDtypeStruct((FR_DEV + 1, ROWS, 128), BF),
            jax.ShapeDtypeStruct((2, ROWS, 128), BF),
            jax.ShapeDtypeStruct((ROWS, CELLS + 128), BF),
        ),
        in_specs=[SMEM, SMEM, VMEM, VMEM],
        out_specs=(VMEM,) * 3,
        name="ring",
    )(place, near, slots, frames)


def with_log_rows(scaled, log_hi, log_lo, lanes):
    rows = iota((ROWS, lanes), 0)
    return jnp.where(
        rows >= FIELDS, jnp.where(rows == FIELDS + 1, log_lo, log_hi), scaled
    )


def step_kernel(
    place_ref, near_ref, plan_ref, level_ref, next_level_ref,
    queue_ref, fresh_ref, ring_ref, next_frames_ref, next_ring_ref, far_ref,
    taps_ref, lift_ref, qkv_ref, attend_ref, decode_ref,
    out_ref, states, rings, spread_ref, hidden_all, qkv_all, context_all,
):
    me = place_ref[0]
    group = place_ref[1]
    is_last = group == place_ref[2] - 1
    is_second_last = group == place_ref[2] - 2
    north_here = (near_ref[me, 2] >= 0).astype(F32)
    south_here = (near_ref[me, 3] >= 0).astype(F32)

    def sigma_at(p, lanes=128):
        level = jnp.where(p < FR_DEV, level_ref[p % FR_DEV], next_level_ref[p % FR_DEV])
        return jnp.full((1, lanes), plan_ref[level], F32)

    for p in range(FR_DEV - 1):
        states[p, 64:ROWS, :] = jnp.zeros((ROWS - 64, CELLS), F32)
        states[p, 0:FIELDS, :] = queue_ref[p + 1]
        rings[p] = ring_ref[p + 1].astype(F32)
    lane = iota((ROWS, 128), 1)
    for f in range(FR_DEV):
        states[FR_DEV - 1 + f] = next_frames_ref[f].astype(F32)
        pair = next_ring_ref[f // 2].astype(F32)
        rings[FR_DEV - 1 + f] = pair if f % 2 == 0 else pltpu.roll(pair, 64, 1)
    states[2 * FR_DEV - 1] = far_ref[:, 0:CELLS].astype(F32)
    rings[2 * FR_DEV - 1] = far_ref[:, CELLS : CELLS + 128].astype(F32)

    def enter(p):
        amount = sigma_at(p)
        states[p, 64:ROWS, :] = jnp.zeros((ROWS - 64, CELLS), F32)
        states[p, 0:FIELDS, :] = fresh_ref[0] * sigma_at(p, CELLS)
        rings[p] = ring_ref[FR_DEV].astype(F32) * amount

    @pl.when(is_last)
    def _():
        enter(FR_DEV - 1)

    @pl.when(is_second_last)
    def _():
        enter(2 * FR_DEV - 1)

    across = iota((ROWS, CELLS), 1) % TILE
    down = iota((ROWS, CELLS), 1) // TILE
    ring_row = iota((128, 4 * CELLS), 0)
    column = iota((128, 4 * CELLS), 1)
    shift = column // CELLS - 2
    cell_x = column % TILE
    cell_y = (column % CELLS) // TILE
    line_x = cell_x + shift
    from_line = jnp.where(
        line_x < 0, 3 * TILE, jnp.where(line_x >= TILE, 3 * TILE + 1, 2 * TILE + line_x)
    )
    from_side = jnp.where(cell_x == 0, cell_y, TILE + cell_y)
    spread_ref[...] = (ring_row == jnp.where(column < CELLS, from_side, from_line)).astype(BF)

    def features(p):
        sigma = sigma_at(p)
        scale = 1.0 / jnp.sqrt(sigma * sigma + 1.0)
        log_hi, log_lo = split_hi_lo(jnp.log(sigma))
        scale2 = jnp.concatenate([scale, scale], axis=1)
        log_hi2 = jnp.concatenate([log_hi, log_hi], axis=1)
        log_lo2 = jnp.concatenate([log_lo, log_lo], axis=1)
        inner = with_log_rows(states[p] * scale2, log_hi2, log_lo2, CELLS)
        ring = with_log_rows(rings[p] * scale, log_hi, log_lo, 128)
        inner_low = inner.astype(BF)
        inner = inner_low.astype(F32)
        image = mm(ring.astype(BF), spread_ref[...])
        sides = image[:, 0:CELLS]
        shifted = (
            jnp.where(across == 0, sides, pltpu.roll(inner, 1, 1)),
            inner,
            jnp.where(across == TILE - 1, sides, pltpu.roll(inner, CELLS - 1, 1)),
        )
        up = []
        low = []
        for b in range(3):
            line = image[:, (b + 1) * CELLS : (b + 2) * CELLS]
            up.append(jnp.where(down == 0, line * north_here, pltpu.roll(shifted[b], TILE, 1)))
            low.append(
                jnp.where(
                    down == TILE - 1, line * south_here, pltpu.roll(shifted[b], CELLS - TILE, 1)
                )
            )
        windows = jnp.concatenate([*up, *shifted, *low], axis=0).astype(BF)
        convolved = mm(taps_ref[...], windows)
        lifted = mm(lift_ref[...], inner_low)
        hidden = lifted + convolved / (1.0 + jnp.exp(-convolved))
        power = jnp.mean(hidden * hidden, axis=0, keepdims=True)
        return hidden, (hidden * lax.rsqrt(power + 1e-06)).astype(BF)

    def own(p, carry):
        hidden, normed = features(p)
        hidden_all[p] = hidden
        qkv_all[p] = mm(qkv_ref[...], normed).reshape(3 * HEAD, HEADS, CELLS)
        return carry

    def following(p, carry):
        _, normed = features(p)
        qkv_all[p, HEAD : 3 * HEAD] = mm(qkv_ref[WIDTH : 3 * WIDTH, :], normed).reshape(
            2 * HEAD, HEADS, CELLS
        )
        return carry

    lax.fori_loop(0, FR_DEV, own, 0)
    lax.fori_loop(FR_DEV, 2 * FR_DEV, following, 0)

    hide = jnp.where(is_last, -jnp.inf, 0.0)
    for half in range(2):
        lanes = slice(half * 128, half * 128 + 128)

        def score(d, sums):
            keys = qkv_all[:, HEAD + d, :, lanes]
            return tuple(
                sums[i] + qkv_all[i, d, :, lanes][None] * keys for i in range(FR_DEV)
            )

        zero = jnp.zeros((2 * FR_DEV, HEADS, 128), F32)
        sums = lax.fori_loop(0, HEAD, score, (zero,) * FR_DEV, unroll=4)
        later = iota((2 * FR_DEV, HEADS, 128), 0) >= FR_DEV
        weights = []
        for i in range(FR_DEV):
            scores = sums[i] * HEAD ** (-0.5) + jnp.where(later, hide, 0.0)
            top = jnp.max(scores, axis=0, keepdims=True)
            raised = jnp.exp(scores - top)
            weights.append(raised / jnp.sum(raised, axis=0, keepdims=True))

        def combine(d, carry):
            values = qkv_all[:, 2 * HEAD + d, :, lanes]
            for i in range(FR_DEV):
                context_all[i, d, :, lanes] = jnp.sum(weights[i] * values, axis=0)
            return carry

        lax.fori_loop(0, HEAD, combine, 0, unroll=4)

    def finish(p, carry):
        context = context_all[p].reshape(WIDTH, CELLS).astype(BF)
        refined = (hidden_all[p] + mm(attend_ref[...], context)).astype(BF)
        projected = mm(decode_ref[...], refined)
        sigma = sigma_at(p, CELLS)
        sigma_next = jnp.full((1, CELLS), plan_ref[level_ref[p] + 1], F32)
        spread = sigma * sigma + 1.0
        slope = (sigma_next - sigma) / sigma
        state = states[p]
        denoised = state / spread + sigma / jnp.sqrt(spread) * projected
        out_ref[p] = (state + slope * (state - denoised))[0:FIELDS]
        return carry

    lax.fori_loop(0, FR_DEV, finish, 0)


def rolling_step(place, near, plan, levels, next_levels, queue, fresh, weights):
    groups = lax.axis_size("noise")
    from_next = [(i + 1, i) for i in range(groups - 1)]
    from_second = [(i + 2, i) for i in range(groups - 2)]
    frames, slots = border_lines(place, near, queue, fresh)
    next_frames = lax.ppermute(frames, "noise", from_next)
    slots = lax.all_to_all(slots, TILE_AXES, split_axis=0, concat_axis=0, tiled=True)
    rings, pair_rings, far = ring_cells(place, near, slots, frames)
    next_rings = lax.ppermute(pair_rings, "noise", from_next)
    far = lax.ppermute(far, "noise", from_second)
    return pl.pallas_call(
        step_kernel,
        out_shape=jax.ShapeDtypeStruct((FR_DEV, FIELDS, CELLS), F32),
        in_specs=[SMEM] * 5 + [VMEM] * 11,
        out_specs=VMEM,
        scratch_shapes=[
            pltpu.VMEM((2 * FR_DEV, ROWS, CELLS), F32),
            pltpu.VMEM((2 * FR_DEV, ROWS, 128), F32),
            pltpu.VMEM((128, 4 * CELLS), BF),
            pltpu.VMEM((FR_DEV, WIDTH, CELLS), F32),
            pltpu.VMEM((2 * FR_DEV, 3 * HEAD, HEADS, CELLS), F32),
            pltpu.VMEM((FR_DEV, HEAD, HEADS, CELLS), F32),
        ],
        name="step",
    )(
        place, near, plan, levels, next_levels,
        queue, fresh, rings, next_frames, next_rings, far, *weights,
    )


def shards(
    queue_state, fresh_noise, plan, levels, neighbours, in_weight, level_embed, conv_weight,
    norm_gain, query_weight, memory_weight, attend_out, decode_weight,
):
    groups = lax.axis_size("noise")
    place = jnp.stack(
        [lax.axis_index(TILE_AXES), lax.axis_index("noise"), jnp.int32(groups)]
    ).astype(jnp.int32)
    next_levels = lax.ppermute(levels, "noise", [(i + 1, i) for i in range(groups - 1)])
    weights = prepare_weights(
        in_weight, level_embed, conv_weight, norm_gain, query_weight, memory_weight,
        attend_out, decode_weight,
    )
    queue = queue_state.reshape(FR_DEV, FIELDS, CELLS)
    noise = fresh_noise.reshape(STEPS, FIELDS, CELLS)
    for step in range(STEPS):
        queue = rolling_step(
            place, neighbours, plan, levels, next_levels, queue, noise[step : step + 1], weights
        )
    return queue.reshape(queue_state.shape)


def solution(mesh):
    split = Mesh(
        mesh.devices.reshape(mesh.shape["noise"], 2, 4, 2), ("noise", "tile_0", "tile_1", "tile_2")
    )
    placed = (
        P("noise", None, TILE_AXES, None),
        P(None, None, TILE_AXES, None),
        P(),
        P("noise"),
        P(),
        P(),
        P(),
        P(),
        P(),
        P(),
        P(),
        P(),
        P(),
    )
    return jax.shard_map(
        shards,
        mesh=split,
        in_specs=placed,
        out_specs=P("noise", None, TILE_AXES, None),
        check_vma=False,
    )
```

time: 207 us -> 102 us (0.49)
  matrix products: 40.9 us -> 0 us
  Pallas kernels: 0 us -> 37.3 us
  waiting for transfers between devices: 47 us -> 11.2 us
  blocking collectives: 29.3 us -> 0 us
  local copies, waits for them, and re-layouts: 38 us -> 10.7 us
  starting transfers between devices: 29.4 us -> 41.2 us
  between operations: 11.1 us -> 0.18 us
  other arithmetic: 10.4 us -> 0.6 us
    ppermute x4 -> x7, waiting for transfers between devices: 41.5 us -> 3.58 us  [the longest x2 3.56 us: rolling_step(): next_rings = lax.ppermute(pair_rings, 'noise', from_next)]
    pallas_call x0 -> x7, Pallas kernels: none -> 37.3 us  [the longest x2 26 us: rolling_step(): pl.pallas_call(step_kernel, out_shape=jax.ShapeDtypeStruct((FR_DEV, FIELD...]
    all_to_all x3 -> x0, blocking collectives: 29.3 us -> none  [copy_for_each(): return lax.all_to_all(copies, axis, split_axis=0, concat_axis=0, tiled=True)]
    dot_general x28 -> x0, matrix products: 24.3 us -> none  [the longest x2 10.9 us: attend(): jnp.einsum('ijhn,jhdn->ihdn', weights, value_heads, preferred_element_typ...]
    reshape x7 -> x1, local copies, waits for them, and re-layouts: 20.3 us -> 1.96 us  [shards(): return queue.reshape(queue_state.shape)]
    sub x2 -> x0, matrix products: 16.6 us -> none  [attend(): weights = jax.nn.softmax(scores, axis=1).astype(jnp.bfloat16)]
    ppermute x4 -> x7, starting transfers between devices: 23 us -> 31.5 us  [the longest x2 11.7 us: rolling_step(): next_frames = lax.ppermute(frames, 'noise', from_next)]
    slice x32 -> x1, local copies, waits for them, and re-layouts: 8.68 us -> 1.03 us  [shards(): noise[step:step + 1]]
  transfers between devices with their start and end apart: 5 -> 9, of which waited for: 4 -> 3; matrix products, arithmetic and copies ran while one was open for 7% -> 1% of each run, Pallas kernels for 0% -> 7%
where the time goes in v1:
time: 102 us; the launch traced here: 101 us
  starting transfers between devices  41.2 us (40%)
  Pallas kernels  37.3 us (37%)
  waiting for transfers between devices  11.2 us (11%)
  local copies, waits for them, and re-layouts  10.7 us (10%)
    pallas_call x2, Pallas kernels, rolling_step(): pl.pallas_call(step_kernel, out_shape=jax.ShapeDtypeStruct((FR_DEV, FIELD...  26 us
    ppermute x2, starting transfers between devices, rolling_step(): next_frames = lax.ppermute(frames, 'noise', from_next)  11.7 us
    ppermute x2, starting transfers between devices, rolling_step(): far = lax.ppermute(far, 'noise', from_second)  10.9 us
    all_to_all x2, starting transfers between devices, rolling_step(): lax.all_to_all(slots, TILE_AXES, split_axis=0, concat_axis=0, tiled=True)  9.68 us
    unnamed x27, local copies, waits for them, and re-layouts  7.75 us
    all_to_all x2, waiting for transfers between devices, rolling_step(): lax.all_to_all(slots, TILE_AXES, split_axis=0, concat_axis=0, tiled=True)  7.65 us
    ppermute x2, starting transfers between devices, rolling_step(): next_rings = lax.ppermute(pair_rings, 'noise', from_next)  6.02 us
    pallas_call x2, Pallas kernels, border_lines(): pl.pallas_call(border_kernel, out_shape=(jax.ShapeDtypeStruct((FR_DEV, RO...  4.23 us
  transfers between devices with their start and end apart: 9, of which 3 were waited for; matrix products, arithmetic and copies ran while one was open for 1% of the time, Pallas kernels for 7%

profile of v1, /device:TPU:8, one launch (start us, length us, event | category | flops | bytes accessed | tf_op | source)
XLA Modules:
  0.0 101.2 jit_solution(18345986788127417398)
XLA Ops:
  0.0 1.4 %copy.32.near_ref = s32[16,4]{1,0:T(8,128)} copy(s32[16,4]{0,1:T(4,128)} %param.17) | data formatting | bytes 512 | tf_op args[4]
  1.4 1.0 %fusion = (f32[1,69,1,256]{3,2,1,0:T(1,128)S(1)}, f32[1,69,1,256]{3,2,1,0:T(1,128)S(1)}) fusion(f32[2,69,1,256]{3,2,1,0:T(1,128)} %param.14), kind=kLoop, calls=%fused_computation.4 | loop fusion | bytes 282624 | tf_op jit(solution)/shard_map/slice | solution.py:416
  2.4 0.6 copy.42
  3.0 1.7 %copy.40 = f32[4,69,1,256]{3,1,2,0:T(8,128)} copy(f32[4,69,1,256]{3,2,1,0:T(1,128)} %param.13) | data formatting | bytes 565248
  4.7 0.6 pad_add_fusion.place_ref
  5.3 2.1 %border.2 = (bf16[4,72,256]{2,1,0:T(8,128)(2,1)}, bf16[16,72,128]{2,1,0:T(8,128)(2,1)}) custom-call(s32[3]{0:T(128)} %pad_add_fusion.place_ref, s32[16,4]{1,0:T(8,128)} %copy.32.near_ref, f32[4,69,256]{2,1,0:T(8,128)} %bitcast.14, f32[1,69,256]{2,1,0:T(8,128)} %bitcast.17), custom_call_target="tpu_custom_call" | custom-call | tf_op jit(solution)/shard_map/border/pallas_call | solution.py:147
  7.4 6.1 %all-to-all-start = ((bf16[16,72,128]{2,1,0:T(8,128)(2,1)}), bf16[16,72,128]{2,1,0:T(8,128)(2,1)S(1)}, u32[]{:S(2)}, u32[]{:S(2)}) async-start(bf16[16,72,128]{2,1,0:T(8,128)(2,1)} %get-tuple-element.20), calls=%async_computation | async-start | bytes 589824 | tf_op jit(solution)/shard_map/all_to_all | solution.py:375
  13.6 8.6 %collective-permute-start.1 = (bf16[4,72,256]{2,1,0:T(8,128)(2,1)}, bf16[4,72,256]{2,1,0:T(8,128)(2,1)S(1)}, u32[]{:S(2)}, u32[]{:S(2)}) collective-permute-start(bf16[4,72,256]{2,1,0:T(8,128)(2,1)} %get-tuple-element.21.frames_ref), channel_id=1, source_target_pairs={{16,0},{32,16},{48,32},{64,48},{80,64},{96,80},{112,96},{128,112},... | collective-permute-start | bytes 442376 | tf_op jit(solution)/shard_map/ppermute | solution.py:374
  22.1 1.1 %all-to-all-done.slots_ref = bf16[16,72,128]{2,1,0:T(8,128)(2,1)S(1)} async-done(((bf16[16,72,128]{2,1,0:T(8,128)(2,1)}), bf16[16,72,128]{2,1,0:T(8,128)(2,1)S(1)}, u32[]{:S(2)}, u32[]{:S(2)}) %all-to-all-start) | async-done | bytes 294944 | tf_op jit(solution)/shard_map/all_to_all | solution.py:375
  23.3 0.7 copy-done
  24.0 2.0 %ring.2 = (bf16[5,72,128]{2,1,0:T(8,128)(2,1)}, bf16[2,72,128]{2,1,0:T(8,128)(2,1)}, bf16[72,384]{1,0:T(8,128)(2,1)}) custom-call(s32[3]{0:T(128)} %pad_add_fusion.place_ref, s32[16,4]{1,0:T(8,128)} %copy.32.near_ref, bf16[16,72,128]{2,1,0:T(8,128)(2,1)} %copy-done, bf16[4,72,256]{2,1,0:T(8,128)(2,1)} %get-tuple-element.21.frames_ref), custom_call_target="tpu_custom_call" | custom-call | tf_op jit(solution)/shard_map/ring/pallas_call | solution.py:197
  26.0 9.0 %collective-permute-start.3 = (bf16[72,384]{1,0:T(8,128)(2,1)}, bf16[72,384]{1,0:T(8,128)(2,1)S(1)}, u32[]{:S(2)}, u32[]{:S(2)}) collective-permute-start(bf16[72,384]{1,0:T(8,128)(2,1)} %get-tuple-element.24), channel_id=1, source_target_pairs={{32,0},{48,16},{64,32},{80,48},{96,64},{112,80},{128,96},{144,112}... | collective-permute-start | bytes 165896 | tf_op jit(solution)/shard_map/ppermute | solution.py:378
  35.0 2.9 %collective-permute-start.2 = (bf16[2,72,128]{2,1,0:T(8,128)(2,1)}, bf16[2,72,128]{2,1,0:T(8,128)(2,1)S(1)}, u32[]{:S(2)}, u32[]{:S(2)}) collective-permute-start(bf16[2,72,128]{2,1,0:T(8,128)(2,1)} %get-tuple-element.23), channel_id=1, source_target_pairs={{16,0},{32,16},{48,32},{64,48},{80,64},{96,80},{112,96},{128,112},... | collective-permute-start | bytes 110600 | tf_op jit(solution)/shard_map/ppermute | solution.py:377
  37.9 0.0 copy-done.9
  37.9 2.9 %collective-permute-start = (s32[4]{0:T(128)S(1)}, s32[4]{0:T(128)S(1)}, u32[]{:S(2)}, u32[]{:S(2)}) collective-permute-start(s32[4]{0:T(128)S(1)} %copy-done.9), channel_id=1, source_target_pairs={{16,0},{32,16},{48,32},{64,48},{80,64},{96,80},{112,96},{128,112},... | collective-permute-start | bytes 56 | tf_op jit(solution)/shard_map/ppermute | solution.py:407
  40.8 0.0 copy-done.6
  40.8 0.7 copy.27.in_ref
  41.6 0.6 copy.41
  42.2 3.1 %weights.1 = (bf16[256,648]{1,0:T(8,128)(2,1)}, bf16[256,72]{1,0:T(8,128)(2,1)}, bf16[768,256]{1,0:T(8,128)(2,1)}, bf16[256,256]{1,0:T(8,128)(2,1)}, bf16[72,256]{1,0:T(8,128)(2,1)}) custom-call(bf16[256,69]{1,0:T(8,128)(2,1)} %copy.27.in_ref, f32[1,256]{1,0:T(1,128)} %bitcast.21, bf16[9,256,256]{2,1,0:T(8,128)(2,1)} %conv_ref.1, f32[1,256]{1,0:T(1,128)} %bitcast.22, ...), custom_call_target="tpu_custom_call" | custom-call | tf_op jit(solution)/shard_map/weights/pallas_call | solution.py:86
  45.3 0.0 collective-permute-done.next_level_ref
  45.3 0.0 collective-permute-done.1.next_frames_ref
  45.3 0.0 copy-start.2
  45.3 0.0 collective-permute-done.2.next_ring_ref
  45.3 0.0 copy-start.7
  45.3 0.0 collective-permute-done.3.far_ref
  45.3 0.0 copy-start.4
  45.3 0.5 copy-done.10
  45.8 0.1 copy-done.2
  46.0 0.0 copy-done.7
  46.0 0.0 copy-done.4
  46.0 13.0 %step.2.queue_ref = f32[4,69,256]{2,1,0:T(8,128)} custom-call(s32[3]{0:T(128)} %pad_add_fusion.place_ref, s32[16,4]{1,0:T(8,128)} %copy.32.near_ref, f32[17]{0:T(128)} %plan_ref.3, s32[4]{0:T(128)} %level_ref.3, s32[4]{0:T(128)} %copy-done.10, f32[4,69,256]{2,1,0:T(8,128)} %bitcast.15, f32[1,69,256]{2,1,0:T(8,128)} %bitcast.18, ...), custom_call_target="tpu_custom_call" | custom-call | tf_op jit(solution)/shard_map/step/pallas_call | solution.py:379
  59.0 2.1 %border.3 = (bf16[4,72,256]{2,1,0:T(8,128)(2,1)}, bf16[16,72,128]{2,1,0:T(8,128)(2,1)}) custom-call(s32[3]{0:T(128)} %pad_add_fusion.place_ref, s32[16,4]{1,0:T(8,128)} %copy.32.near_ref, f32[4,69,256]{2,1,0:T(8,128)} %step.2.queue_ref, f32[1,69,256]{2,1,0:T(8,128)} %bitcast.19), custom_call_target="tpu_custom_call" | custom-call | tf_op jit(solution)/shard_map/border/pallas_call | solution.py:147
  61.1 3.5 %all-to-all-start.1 = ((bf16[16,72,128]{2,1,0:T(8,128)(2,1)}), bf16[16,72,128]{2,1,0:T(8,128)(2,1)S(1)}, u32[]{:S(2)}, u32[]{:S(2)}) async-start(bf16[16,72,128]{2,1,0:T(8,128)(2,1)} %get-tuple-element.30), calls=%async_computation.1 | async-start | bytes 589824 | tf_op jit(solution)/shard_map/all_to_all | solution.py:375
  64.6 3.1 %collective-permute-start.4 = (bf16[4,72,256]{2,1,0:T(8,128)(2,1)}, bf16[4,72,256]{2,1,0:T(8,128)(2,1)S(1)}, u32[]{:S(2)}, u32[]{:S(2)}) collective-permute-start(bf16[4,72,256]{2,1,0:T(8,128)(2,1)} %get-tuple-element.31.frames_ref), channel_id=1, source_target_pairs={{16,0},{32,16},{48,32},{64,48},{80,64},{96,80},{112,96},{128,112},... | collective-permute-start | bytes 442376 | tf_op jit(solution)/shard_map/ppermute | solution.py:374
  67.7 6.5 %all-to-all-done.1.slots_ref = bf16[16,72,128]{2,1,0:T(8,128)(2,1)S(1)} async-done(((bf16[16,72,128]{2,1,0:T(8,128)(2,1)}), bf16[16,72,128]{2,1,0:T(8,128)(2,1)S(1)}, u32[]{:S(2)}, u32[]{:S(2)}) %all-to-all-start.1) | async-done | bytes 294944 | tf_op jit(solution)/shard_map/all_to_all | solution.py:375
  74.3 0.7 copy-done.1
  75.0 2.0 %ring.3 = (bf16[5,72,128]{2,1,0:T(8,128)(2,1)}, bf16[2,72,128]{2,1,0:T(8,128)(2,1)}, bf16[72,384]{1,0:T(8,128)(2,1)}) custom-call(s32[3]{0:T(128)} %pad_add_fusion.place_ref, s32[16,4]{1,0:T(8,128)} %copy.32.near_ref, bf16[16,72,128]{2,1,0:T(8,128)(2,1)} %copy-done.1, bf16[4,72,256]{2,1,0:T(8,128)(2,1)} %get-tuple-element.31.frames_ref), custom_call_target="tpu_custom_call" | custom-call | tf_op jit(solution)/shard_map/ring/pallas_call | solution.py:197
  77.0 1.9 %collective-permute-start.6 = (bf16[72,384]{1,0:T(8,128)(2,1)}, bf16[72,384]{1,0:T(8,128)(2,1)S(1)}, u32[]{:S(2)}, u32[]{:S(2)}) collective-permute-start(bf16[72,384]{1,0:T(8,128)(2,1)} %get-tuple-element.34), channel_id=1, source_target_pairs={{32,0},{48,16},{64,32},{80,48},{96,64},{112,80},{128,96},{144,112}... | collective-permute-start | bytes 165896 | tf_op jit(solution)/shard_map/ppermute | solution.py:378
  78.9 3.1 %collective-permute-start.5 = (bf16[2,72,128]{2,1,0:T(8,128)(2,1)}, bf16[2,72,128]{2,1,0:T(8,128)(2,1)S(1)}, u32[]{:S(2)}, u32[]{:S(2)}) collective-permute-start(bf16[2,72,128]{2,1,0:T(8,128)(2,1)} %get-tuple-element.33), channel_id=1, source_target_pairs={{16,0},{32,16},{48,32},{64,48},{80,64},{96,80},{112,96},{128,112},... | collective-permute-start | bytes 110600 | tf_op jit(solution)/shard_map/ppermute | solution.py:377
  82.0 0.0 collective-permute-done.4.next_frames_ref
  82.0 0.0 copy-start.3
  82.0 3.6 %collective-permute-done.5.next_ring_ref = bf16[2,72,128]{2,1,0:T(8,128)(2,1)S(1)} collective-permute-done((bf16[2,72,128]{2,1,0:T(8,128)(2,1)}, bf16[2,72,128]{2,1,0:T(8,128)(2,1)S(1)}, u32[]{:S(2)}, u32[]{:S(2)}) %collective-permute-start.5) | collective-permute-done | bytes 36896 | tf_op jit(solution)/shard_map/ppermute | solution.py:377
  85.6 0.0 collective-permute-done.6.far_ref
  85.6 0.0 copy-done.3
  85.6 0.6 copy-done.8
  86.2 0.0 copy-done.5
  86.2 13.0 %step.3 = f32[4,69,256]{2,1,0:T(8,128)} custom-call(s32[3]{0:T(128)} %pad_add_fusion.place_ref, s32[16,4]{1,0:T(8,128)} %copy.32.near_ref, f32[17]{0:T(128)} %plan_ref.3, s32[4]{0:T(128)} %level_ref.3, s32[4]{0:T(128)} %copy-done.10, f32[4,69,256]{2,1,0:T(8,128)} %step.2.queue_ref, f32[1,69,256]{2,1,0:T(8,128)} %bitcast.20, ...), custom_call_target="tpu_custom_call" | custom-call | tf_op jit(solution)/shard_map/step/pallas_call | solution.py:379
  99.2 2.0 %copy.33 = f32[4,69,1,256]{3,2,1,0:T(1,128)} copy(f32[4,69,1,256]{3,1,0,2:T(8,128)} %bitcast.16) | data formatting | bytes 565248 | tf_op jit(solution)/shard_map/reshape | solution.py:418
  (7 shorter events, 0.0 us)
Async XLA Ops:
  1.4 36.5 %copy-start.9 = (s32[4]{0:T(128)S(1)}, s32[4]{0:T(128)}, u32[]{:S(2)}) copy-start(s32[4]{0:T(128)} %level_ref.3) | copy-start | bytes 52
  1.4 39.5 %copy-start.6 = (bf16[256,69]{0,1:T(8,128)(2,1)S(1)}, bf16[256,69]{0,1:T(8,128)(2,1)}, u32[]{:S(2)}) copy-start(bf16[256,69]{0,1:T(8,128)(2,1)} %param.18) | copy-start | bytes 105988
  7.4 15.8 %all-to-all-start = ((bf16[16,72,128]{2,1,0:T(8,128)(2,1)}), bf16[16,72,128]{2,1,0:T(8,128)(2,1)S(1)}, u32[]{:S(2)}, u32[]{:S(2)}) async-start(bf16[16,72,128]{2,1,0:T(8,128)(2,1)} %get-tuple-element.20), calls=%async_computation | async-start | bytes 589824 | tf_op jit(solution)/shard_map/all_to_all | solution.py:375
  13.6 31.7 %collective-permute-start.1 = (bf16[4,72,256]{2,1,0:T(8,128)(2,1)}, bf16[4,72,256]{2,1,0:T(8,128)(2,1)S(1)}, u32[]{:S(2)}, u32[]{:S(2)}) collective-permute-start(bf16[4,72,256]{2,1,0:T(8,128)(2,1)} %get-tuple-element.21.frames_ref), channel_id=1, source_target_pairs={{16,0},{32,16},{48,32},{64,48},{80,64},{96,80},{112,96},{128,112},... | collective-permute-start | bytes 442376 | tf_op jit(solution)/shard_map/ppermute | solution.py:374
  23.3 0.7 copy-start
  26.0 19.4 %collective-permute-start.3 = (bf16[72,384]{1,0:T(8,128)(2,1)}, bf16[72,384]{1,0:T(8,128)(2,1)S(1)}, u32[]{:S(2)}, u32[]{:S(2)}) collective-permute-start(bf16[72,384]{1,0:T(8,128)(2,1)} %get-tuple-element.24), channel_id=1, source_target_pairs={{32,0},{48,16},{64,32},{80,48},{96,64},{112,80},{128,96},{144,112}... | collective-permute-start | bytes 165896 | tf_op jit(solution)/shard_map/ppermute | solution.py:378
  35.0 10.3 %collective-permute-start.2 = (bf16[2,72,128]{2,1,0:T(8,128)(2,1)}, bf16[2,72,128]{2,1,0:T(8,128)(2,1)S(1)}, u32[]{:S(2)}, u32[]{:S(2)}) collective-permute-start(bf16[2,72,128]{2,1,0:T(8,128)(2,1)} %get-tuple-element.23), channel_id=1, source_target_pairs={{16,0},{32,16},{48,32},{64,48},{80,64},{96,80},{112,96},{128,112},... | collective-permute-start | bytes 110600 | tf_op jit(solution)/shard_map/ppermute | solution.py:377
  37.9 7.4 %collective-permute-start = (s32[4]{0:T(128)S(1)}, s32[4]{0:T(128)S(1)}, u32[]{:S(2)}, u32[]{:S(2)}) collective-permute-start(s32[4]{0:T(128)S(1)} %copy-done.9), channel_id=1, source_target_pairs={{16,0},{32,16},{48,32},{64,48},{80,64},{96,80},{112,96},{128,112},... | collective-permute-start | bytes 56 | tf_op jit(solution)/shard_map/ppermute | solution.py:407
  45.3 0.6 copy-start.10
  45.3 0.7 copy-start.2
  45.3 0.6 copy-start.7
  45.3 0.6 copy-start.4
  61.1 13.2 %all-to-all-start.1 = ((bf16[16,72,128]{2,1,0:T(8,128)(2,1)}), bf16[16,72,128]{2,1,0:T(8,128)(2,1)S(1)}, u32[]{:S(2)}, u32[]{:S(2)}) async-start(bf16[16,72,128]{2,1,0:T(8,128)(2,1)} %get-tuple-element.30), calls=%async_computation.1 | async-start | bytes 589824 | tf_op jit(solution)/shard_map/all_to_all | solution.py:375
  64.6 17.4 %collective-permute-start.4 = (bf16[4,72,256]{2,1,0:T(8,128)(2,1)}, bf16[4,72,256]{2,1,0:T(8,128)(2,1)S(1)}, u32[]{:S(2)}, u32[]{:S(2)}) collective-permute-start(bf16[4,72,256]{2,1,0:T(8,128)(2,1)} %get-tuple-element.31.frames_ref), channel_id=1, source_target_pairs={{16,0},{32,16},{48,32},{64,48},{80,64},{96,80},{112,96},{128,112},... | collective-permute-start | bytes 442376 | tf_op jit(solution)/shard_map/ppermute | solution.py:374
  74.3 0.7 copy-start.1
  77.0 8.6 %collective-permute-start.6 = (bf16[72,384]{1,0:T(8,128)(2,1)}, bf16[72,384]{1,0:T(8,128)(2,1)S(1)}, u32[]{:S(2)}, u32[]{:S(2)}) collective-permute-start(bf16[72,384]{1,0:T(8,128)(2,1)} %get-tuple-element.34), channel_id=1, source_target_pairs={{32,0},{48,16},{64,32},{80,48},{96,64},{112,80},{128,96},{144,112}... | collective-permute-start | bytes 165896 | tf_op jit(solution)/shard_map/ppermute | solution.py:378
  78.9 6.7 %collective-permute-start.5 = (bf16[2,72,128]{2,1,0:T(8,128)(2,1)}, bf16[2,72,128]{2,1,0:T(8,128)(2,1)S(1)}, u32[]{:S(2)}, u32[]{:S(2)}) collective-permute-start(bf16[2,72,128]{2,1,0:T(8,128)(2,1)} %get-tuple-element.33), channel_id=1, source_target_pairs={{16,0},{32,16},{48,32},{64,48},{80,64},{96,80},{112,96},{128,112},... | collective-permute-start | bytes 110600 | tf_op jit(solution)/shard_map/ppermute | solution.py:377
  82.0 3.6 %copy-start.3 = (bf16[4,72,256]{2,1,0:T(8,128)(2,1)}, bf16[4,72,256]{2,1,0:T(8,128)(2,1)S(1)}, u32[]{:S(2)}) copy-start(bf16[4,72,256]{2,1,0:T(8,128)(2,1)S(1)} %collective-permute-done.4.next_frames_ref) | copy-start | bytes 442372
  85.6 0.6 copy-start.8
  85.6 0.6 copy-start.5

commit v2 on v1

--- a/solution.py
+++ b/solution.py
@@ -1,3 +1,5 @@
+import functools
+
 import jax
 import jax.numpy as jnp
 from jax import lax
@@ -14,6 +16,7 @@
 TILE = 16
 CELLS = TILE * TILE
 TAPS = 9
+UNROLL = 4
 FR_DEV = 4
 STEPS = 2
 NTILES = 16
@@ -43,13 +46,12 @@
 
 
 def weights_kernel(
-    in_ref, embed_ref, conv_ref, gain_ref, query_ref, memory_ref, out_ref, decode_ref,
+    in_ref, embed_ref, conv_ref, gain_ref, query_ref, memory_ref, out_ref, decode_ref, after_ref,
     taps_out, lift_out, qkv_out, attend_out, decode_out, folded,
 ):
     rows = iota((ROWS, WIDTH), 0)
-    weight = in_ref[...].astype(F32)
     unit = (iota((ROWS, FIELDS), 0) == iota((ROWS, FIELDS), 1)).astype(BF)
-    lift_t = mm_nt(unit, weight.astype(BF))
+    lift_t = mm(unit, in_ref[...])
     embed = jnp.broadcast_to(embed_ref[...], (ROWS, WIDTH))
     embed_hi, embed_lo = split_hi_lo(embed)
     stacked = jnp.where(
@@ -78,11 +80,10 @@
             mm(order, memory_ref[pl.ds(part * WIDTH, WIDTH), :]) * gain
         ).astype(BF)
     attend_out[...] = mm_nt(out_ref[...], order).astype(BF)
-    unit = (iota((ROWS, FIELDS), 0) == iota((ROWS, FIELDS), 1)).astype(BF)
     decode_out[...] = mm(unit, decode_ref[...]).astype(BF)
 
 
-def prepare_weights(in_weight, embed, conv, gain, query, memory, attend, decode):
+def prepare_weights(in_weight, embed, conv, gain, query, memory, attend, decode, after):
     return pl.pallas_call(
         weights_kernel,
         out_shape=(
@@ -92,19 +93,40 @@
             jax.ShapeDtypeStruct((WIDTH, WIDTH), BF),
             jax.ShapeDtypeStruct((ROWS, WIDTH), BF),
         ),
-        in_specs=[VMEM] * 8,
+        in_specs=[VMEM] * 8 + [SMEM],
         out_specs=(VMEM,) * 5,
         scratch_shapes=[pltpu.VMEM((TAPS * ROWS, WIDTH), F32)],
         name="weights",
-    )(in_weight, embed.reshape(1, WIDTH), conv, gain.reshape(1, WIDTH), query, memory, attend, decode)
-
-
-def border_kernel(place_ref, near_ref, queue_ref, fresh_ref, frames_out, slots_out, full, lines):
-    me = place_ref[0]
-    full[...] = jnp.zeros_like(full)
+    )(
+        in_weight.T, embed.reshape(1, WIDTH), conv, gain.reshape(1, WIDTH), query, memory, attend,
+        decode, after,
+    )
+
+
+def frame_rows(queue_ref, frame):
+    halves = [
+        queue_ref[pl.ds(frame * 2 * FIELDS + half, FIELDS, stride=2), :] for half in range(2)
+    ]
+    return jnp.concatenate(halves, axis=1)
+
+
+def border_kernel(
+    step, near_ref, plan_ref, level_ref, queue_ref, fresh_ref,
+    frames_out, slots_out, after_out, full, lines,
+):
+    me = lax.axis_index(TILE_AXES)
+    after_out[0] = 0
+    low_row = iota((8, CELLS), 0)
     for f in range(FR_DEV):
-        full[pl.ds(f * ROWS, FIELDS), :] = queue_ref[f]
-    full[pl.ds(FR_DEV * ROWS, FIELDS), :] = fresh_ref[0]
+        sigma = jnp.full((8, CELLS), plan_ref[level_ref[f]], F32)
+        first, rest = split_hi_lo(sigma)
+        second, third = split_hi_lo(rest)
+        full[pl.ds(f * ROWS + 64, 8), :] = jnp.where(
+            low_row == 5, first, jnp.where(low_row == 6, second, third)
+        )
+        full[pl.ds(f * ROWS, FIELDS), :] = frame_rows(queue_ref, f)
+    full[pl.ds(FR_DEV * ROWS + 64, 8), :] = jnp.zeros((8, CELLS), F32)
+    full[pl.ds(FR_DEV * ROWS, FIELDS), :] = fresh_ref[step, :, 0, :]
     frames = full[...].astype(BF)
     for f in range(FR_DEV):
         frames_out[f] = full[pl.ds(f * ROWS, ROWS), :].astype(BF)
@@ -134,41 +156,42 @@
             packed = jnp.where(lane_block == f, one, packed)
         lines[r] = packed.astype(BF)
     for j in range(NTILES):
-        north = near_ref[j, 2]
-        beside = jnp.maximum(north, near_ref[j, 3])
-        from_west = jnp.logical_or(near_ref[j, 0] == me, near_ref[beside, 0] == me)
-        from_east = jnp.logical_or(near_ref[j, 1] == me, near_ref[beside, 1] == me)
+        north = near_ref[2, j]
+        beside = jnp.maximum(north, near_ref[3, j])
+        from_west = jnp.logical_or(near_ref[0, j] == me, near_ref[0, beside] == me)
+        from_east = jnp.logical_or(near_ref[1, j] == me, near_ref[1, beside] == me)
         vertical = jnp.where(north >= 0, 2, 3)
         code = jnp.where(from_west, 0, jnp.where(from_east, 1, vertical))
         slots_out[j] = lines[code]
 
 
-def border_lines(place, near, queue, fresh):
+def border_lines(step, near, plan, levels, queue, fresh):
     return pl.pallas_call(
-        border_kernel,
+        functools.partial(border_kernel, step),
         out_shape=(
             jax.ShapeDtypeStruct((FR_DEV, ROWS, CELLS), BF),
             jax.ShapeDtypeStruct((NTILES, ROWS, 128), BF),
+            jax.ShapeDtypeStruct((1,), jnp.int32),
         ),
-        in_specs=[SMEM, SMEM, VMEM, VMEM],
-        out_specs=(VMEM, VMEM),
+        in_specs=[SMEM, SMEM, SMEM, VMEM, VMEM],
+        out_specs=(VMEM, VMEM, SMEM),
         scratch_shapes=[
             pltpu.VMEM(((FR_DEV + 1) * ROWS, CELLS), F32),
             pltpu.VMEM((4, ROWS, 128), BF),
         ],
         name="border",
-    )(place, near, queue, fresh)
-
-
-def ring_kernel(place_ref, near_ref, slots_ref, frames_ref, ring_out, near_out, far_out):
-    me = place_ref[0]
-    north = near_ref[me, 2]
-    beside = jnp.maximum(north, near_ref[me, 3])
-    west = slots_ref[near_ref[me, 0]].astype(F32)
-    east = slots_ref[near_ref[me, 1]].astype(F32)
+    )(near, plan, levels, queue, fresh)
+
+
+def ring_kernel(near_ref, slots_ref, frames_ref, wait_ref, ring_out, near_out, far_out):
+    me = lax.axis_index(TILE_AXES)
+    north = near_ref[2, me]
+    beside = jnp.maximum(north, near_ref[3, me])
+    west = slots_ref[near_ref[0, me]].astype(F32)
+    east = slots_ref[near_ref[1, me]].astype(F32)
     line = slots_ref[beside].astype(F32)
-    corner_west = slots_ref[near_ref[beside, 0]].astype(F32)
-    corner_east = slots_ref[near_ref[beside, 1]].astype(F32)
+    corner_west = slots_ref[near_ref[0, beside]].astype(F32)
+    corner_east = slots_ref[near_ref[1, beside]].astype(F32)
     lane = iota((ROWS, 128), 1)
     below = north >= 0
     west_end = jnp.where(below, pltpu.roll(corner_west, 128 - (TILE - 1), 1), corner_west)
@@ -193,7 +216,7 @@
     far_out[:, CELLS : CELLS + 128] = rings[0].astype(BF)
 
 
-def ring_cells(place, near, slots, frames):
+def ring_cells(near, slots, frames, wait):
     return pl.pallas_call(
         ring_kernel,
         out_shape=(
@@ -201,10 +224,10 @@
             jax.ShapeDtypeStruct((2, ROWS, 128), BF),
             jax.ShapeDtypeStruct((ROWS, CELLS + 128), BF),
         ),
-        in_specs=[SMEM, SMEM, VMEM, VMEM],
+        in_specs=[SMEM, VMEM, VMEM, pl.BlockSpec(memory_space=pl.ANY)],
         out_specs=(VMEM,) * 3,
         name="ring",
-    )(place, near, slots, frames)
+    )(near, slots, frames, wait)
 
 
 def with_log_rows(scaled, log_hi, log_lo, lanes):
@@ -215,39 +238,39 @@
 
 
 def step_kernel(
-    place_ref, near_ref, plan_ref, level_ref, next_level_ref,
+    step, near_ref, plan_ref, level_ref,
     queue_ref, fresh_ref, ring_ref, next_frames_ref, next_ring_ref, far_ref,
     taps_ref, lift_ref, qkv_ref, attend_ref, decode_ref,
-    out_ref, states, rings, spread_ref, hidden_all, qkv_all, context_all,
+    out_ref, states, rings, sigmas, images, hidden_all, qkv_all, context_all,
 ):
-    me = place_ref[0]
-    group = place_ref[1]
-    is_last = group == place_ref[2] - 1
-    is_second_last = group == place_ref[2] - 2
-    north_here = (near_ref[me, 2] >= 0).astype(F32)
-    south_here = (near_ref[me, 3] >= 0).astype(F32)
-
-    def sigma_at(p, lanes=128):
-        level = jnp.where(p < FR_DEV, level_ref[p % FR_DEV], next_level_ref[p % FR_DEV])
-        return jnp.full((1, lanes), plan_ref[level], F32)
+    me = lax.axis_index(TILE_AXES)
+    group = lax.axis_index("noise")
+    groups = lax.axis_size("noise")
+    is_last = group == groups - 1
+    is_second_last = group == groups - 2
+    north_here = (near_ref[2, me] >= 0).astype(F32)
+    south_here = (near_ref[3, me] >= 0).astype(F32)
 
     for p in range(FR_DEV - 1):
         states[p, 64:ROWS, :] = jnp.zeros((ROWS - 64, CELLS), F32)
-        states[p, 0:FIELDS, :] = queue_ref[p + 1]
+        states[p, 0:FIELDS, :] = frame_rows(queue_ref, p + 1)
         rings[p] = ring_ref[p + 1].astype(F32)
-    lane = iota((ROWS, 128), 1)
     for f in range(FR_DEV):
-        states[FR_DEV - 1 + f] = next_frames_ref[f].astype(F32)
+        came = next_frames_ref[f].astype(F32)
+        states[FR_DEV - 1 + f] = came
+        parts = came[FIELDS : FIELDS + 1] + came[FIELDS + 1 : FIELDS + 2]
+        parts = parts + came[FIELDS + 2 : FIELDS + 3]
+        sigmas[FR_DEV + f] = jnp.where(is_last, 1.0, parts)
+        sigmas[f] = jnp.full((1, CELLS), plan_ref[level_ref[f]], F32)
         pair = next_ring_ref[f // 2].astype(F32)
         rings[FR_DEV - 1 + f] = pair if f % 2 == 0 else pltpu.roll(pair, 64, 1)
     states[2 * FR_DEV - 1] = far_ref[:, 0:CELLS].astype(F32)
     rings[2 * FR_DEV - 1] = far_ref[:, CELLS : CELLS + 128].astype(F32)
 
     def enter(p):
-        amount = sigma_at(p)
         states[p, 64:ROWS, :] = jnp.zeros((ROWS - 64, CELLS), F32)
-        states[p, 0:FIELDS, :] = fresh_ref[0] * sigma_at(p, CELLS)
-        rings[p] = ring_ref[FR_DEV].astype(F32) * amount
+        states[p, 0:FIELDS, :] = fresh_ref[step, :, 0, :] * sigmas[p]
+        rings[p] = ring_ref[FR_DEV].astype(F32) * sigmas[p][:, 0:128]
 
     @pl.when(is_last)
     def _():
@@ -256,6 +279,11 @@
     @pl.when(is_second_last)
     def _():
         enter(2 * FR_DEV - 1)
+
+    def scales(p, lanes):
+        sigma = sigmas[p][:, 0:lanes]
+        log_hi, log_lo = split_hi_lo(jnp.log(sigma))
+        return 1.0 / jnp.sqrt(sigma * sigma + 1.0), log_hi, log_lo
 
     across = iota((ROWS, CELLS), 1) % TILE
     down = iota((ROWS, CELLS), 1) // TILE
@@ -269,21 +297,21 @@
         line_x < 0, 3 * TILE, jnp.where(line_x >= TILE, 3 * TILE + 1, 2 * TILE + line_x)
     )
     from_side = jnp.where(cell_x == 0, cell_y, TILE + cell_y)
-    spread_ref[...] = (ring_row == jnp.where(column < CELLS, from_side, from_line)).astype(BF)
+    spread = (ring_row == jnp.where(column < CELLS, from_side, from_line)).astype(BF)
+    ring_low = []
+    for p in range(2 * FR_DEV):
+        scale, log_hi, log_lo = scales(p, 128)
+        ring_low.append(with_log_rows(rings[p] * scale, log_hi, log_lo, 128))
+    images[...] = mm(jnp.concatenate(ring_low, axis=0).astype(BF), spread).reshape(
+        2 * FR_DEV, ROWS, 4 * CELLS
+    )
 
     def features(p):
-        sigma = sigma_at(p)
-        scale = 1.0 / jnp.sqrt(sigma * sigma + 1.0)
-        log_hi, log_lo = split_hi_lo(jnp.log(sigma))
-        scale2 = jnp.concatenate([scale, scale], axis=1)
-        log_hi2 = jnp.concatenate([log_hi, log_hi], axis=1)
-        log_lo2 = jnp.concatenate([log_lo, log_lo], axis=1)
-        inner = with_log_rows(states[p] * scale2, log_hi2, log_lo2, CELLS)
-        ring = with_log_rows(rings[p] * scale, log_hi, log_lo, 128)
+        scale, log_hi, log_lo = scales(p, CELLS)
+        inner = with_log_rows(states[p] * scale, log_hi, log_lo, CELLS)
         inner_low = inner.astype(BF)
         inner = inner_low.astype(F32)
-        image = mm(ring.astype(BF), spread_ref[...])
-        sides = image[:, 0:CELLS]
+        sides = images[p, :, 0:CELLS]
         shifted = (
             jnp.where(across == 0, sides, pltpu.roll(inner, 1, 1)),
             inner,
@@ -292,7 +320,7 @@
         up = []
         low = []
         for b in range(3):
-            line = image[:, (b + 1) * CELLS : (b + 2) * CELLS]
+            line = images[p, :, (b + 1) * CELLS : (b + 2) * CELLS]
             up.append(jnp.where(down == 0, line * north_here, pltpu.roll(shifted[b], TILE, 1)))
             low.append(
                 jnp.where(
@@ -319,8 +347,8 @@
         )
         return carry
 
-    lax.fori_loop(0, FR_DEV, own, 0)
-    lax.fori_loop(FR_DEV, 2 * FR_DEV, following, 0)
+    lax.fori_loop(0, FR_DEV, own, 0, unroll=UNROLL)
+    lax.fori_loop(FR_DEV, 2 * FR_DEV, following, 0, unroll=UNROLL)
 
     hide = jnp.where(is_last, -jnp.inf, 0.0)
     for half in range(2):
@@ -354,66 +382,66 @@
         context = context_all[p].reshape(WIDTH, CELLS).astype(BF)
         refined = (hidden_all[p] + mm(attend_ref[...], context)).astype(BF)
         projected = mm(decode_ref[...], refined)
-        sigma = sigma_at(p, CELLS)
+        sigma = sigmas[p]
         sigma_next = jnp.full((1, CELLS), plan_ref[level_ref[p] + 1], F32)
         spread = sigma * sigma + 1.0
         slope = (sigma_next - sigma) / sigma
         state = states[p]
         denoised = state / spread + sigma / jnp.sqrt(spread) * projected
-        out_ref[p] = (state + slope * (state - denoised))[0:FIELDS]
+        moved = (state + slope * (state - denoised))[0:FIELDS]
+        for half in range(2):
+            out_ref[pl.ds(p * 2 * FIELDS + half, FIELDS, stride=2), :] = moved[
+                :, half * 128 : half * 128 + 128
+            ]
         return carry
 
-    lax.fori_loop(0, FR_DEV, finish, 0)
-
-
-def rolling_step(place, near, plan, levels, next_levels, queue, fresh, weights):
+    lax.fori_loop(0, FR_DEV, finish, 0, unroll=UNROLL)
+
+
+def rolling_step(step, near, plan, levels, queue, fresh, raw_weights, weights):
     groups = lax.axis_size("noise")
     from_next = [(i + 1, i) for i in range(groups - 1)]
     from_second = [(i + 2, i) for i in range(groups - 2)]
-    frames, slots = border_lines(place, near, queue, fresh)
+    frames, slots, after = border_lines(step, near, plan, levels, queue, fresh)
     next_frames = lax.ppermute(frames, "noise", from_next)
     slots = lax.all_to_all(slots, TILE_AXES, split_axis=0, concat_axis=0, tiled=True)
-    rings, pair_rings, far = ring_cells(place, near, slots, frames)
+    if weights is None:
+        weights = prepare_weights(*raw_weights, after)
+    rings, pair_rings, far = ring_cells(near, slots, frames, weights[1])
     next_rings = lax.ppermute(pair_rings, "noise", from_next)
     far = lax.ppermute(far, "noise", from_second)
-    return pl.pallas_call(
-        step_kernel,
-        out_shape=jax.ShapeDtypeStruct((FR_DEV, FIELDS, CELLS), F32),
-        in_specs=[SMEM] * 5 + [VMEM] * 11,
+    moved = pl.pallas_call(
+        functools.partial(step_kernel, step),
+        out_shape=jax.ShapeDtypeStruct((FR_DEV * FIELDS * 2, 128), F32),
+        in_specs=[SMEM] * 3 + [VMEM] * 11,
         out_specs=VMEM,
         scratch_shapes=[
             pltpu.VMEM((2 * FR_DEV, ROWS, CELLS), F32),
             pltpu.VMEM((2 * FR_DEV, ROWS, 128), F32),
-            pltpu.VMEM((128, 4 * CELLS), BF),
+            pltpu.VMEM((2 * FR_DEV, 1, CELLS), F32),
+            pltpu.VMEM((2 * FR_DEV, ROWS, 4 * CELLS), F32),
             pltpu.VMEM((FR_DEV, WIDTH, CELLS), F32),
             pltpu.VMEM((2 * FR_DEV, 3 * HEAD, HEADS, CELLS), F32),
             pltpu.VMEM((FR_DEV, HEAD, HEADS, CELLS), F32),
         ],
         name="step",
-    )(
-        place, near, plan, levels, next_levels,
-        queue, fresh, rings, next_frames, next_rings, far, *weights,
-    )
+    )(near, plan, levels, queue, fresh, rings, next_frames, next_rings, far, *weights)
+    return moved, weights
 
 
 def shards(
     queue_state, fresh_noise, plan, levels, neighbours, in_weight, level_embed, conv_weight,
     norm_gain, query_weight, memory_weight, attend_out, decode_weight,
 ):
-    groups = lax.axis_size("noise")
-    place = jnp.stack(
-        [lax.axis_index(TILE_AXES), lax.axis_index("noise"), jnp.int32(groups)]
-    ).astype(jnp.int32)
-    next_levels = lax.ppermute(levels, "noise", [(i + 1, i) for i in range(groups - 1)])
-    weights = prepare_weights(
+    raw_weights = (
         in_weight, level_embed, conv_weight, norm_gain, query_weight, memory_weight,
         attend_out, decode_weight,
     )
-    queue = queue_state.reshape(FR_DEV, FIELDS, CELLS)
-    noise = fresh_noise.reshape(STEPS, FIELDS, CELLS)
+    queue = queue_state.reshape(FR_DEV * FIELDS * 2, 128)
+    weights = None
     for step in range(STEPS):
-        queue = rolling_step(
-            place, neighbours, plan, levels, next_levels, queue, noise[step : step + 1], weights
+        queue, weights = rolling_step(
+            step, neighbours.T, plan, levels, queue, fresh_noise, raw_weights, weights
         )
     return queue.reshape(queue_state.shape)
 

time: 102 us -> 84.7 us (0.83)
  local copies, waits for them, and re-layouts: 10.7 us -> 2.73 us
  Pallas kernels: 37.3 us -> 29.6 us
    pallas_call x4, Pallas kernels: 30.2 us -> 22 us  [the longest x2 17.8 us: rolling_step(): pl.pallas_call(functools.partial(step_kernel, step), out_shape=jax.ShapeD...]
    unnamed x27 -> x16, local copies, waits for them, and re-layouts: 7.75 us -> 2.73 us
    all_to_all x2, waiting for transfers between devices: 7.65 us -> 4.1 us  [rolling_step(): lax.all_to_all(slots, TILE_AXES, split_axis=0, concat_axis=0, tiled=True)]
    ppermute x2, waiting for transfers between devices: 3.56 us -> 6.68 us  [rolling_step(): next_rings = lax.ppermute(pair_rings, 'noise', from_next)]
    ppermute x1 -> x0, starting transfers between devices: 2.92 us -> none  [shards(): lax.ppermute(levels, 'noise', [(i + 1, i) for i in range(groups - 1)])]
    ppermute x2, starting transfers between devices: 11.7 us -> 14.1 us  [rolling_step(): next_frames = lax.ppermute(frames, 'noise', from_next)]
    reshape x1 -> x0, local copies, waits for them, and re-layouts: 1.96 us -> none  [shards(): return queue.reshape(queue_state.shape)]
    slice x1 -> x0, local copies, waits for them, and re-layouts: 1.03 us -> none  [shards(): noise[step:step + 1]]
  transfers between devices with their start and end apart: 9 -> 8, of which waited for: 3 -> 3; matrix products, arithmetic and copies ran while one was open for 1% -> 0% of each run, Pallas kernels for 7% -> 9%
where the time goes in v2:
time: 84.7 us; the launch traced here: 84 us
  starting transfers between devices  40.7 us (48%)
  Pallas kernels  29.6 us (35%)
  waiting for transfers between devices  10.8 us (13%)
  local copies, waits for them, and re-layouts  2.73 us (3%)
    pallas_call x2, Pallas kernels, rolling_step(): pl.pallas_call(functools.partial(step_kernel, step), out_shape=jax.ShapeD...  17.8 us
    ppermute x2, starting transfers between devices, rolling_step(): next_frames = lax.ppermute(frames, 'noise', from_next)  14.1 us
    ppermute x2, starting transfers between devices, rolling_step(): far = lax.ppermute(far, 'noise', from_second)  10.7 us
    all_to_all x2, starting transfers between devices, rolling_step(): lax.all_to_all(slots, TILE_AXES, split_axis=0, concat_axis=0, tiled=True)  9.7 us
    ppermute x2, waiting for transfers between devices, rolling_step(): next_rings = lax.ppermute(pair_rings, 'noise', from_next)  6.68 us
    ppermute x2, starting transfers between devices, rolling_step(): next_rings = lax.ppermute(pair_rings, 'noise', from_next)  6.21 us
    pallas_call x2, Pallas kernels, border_lines(): pl.pallas_call(functools.partial(border_kernel, step), out_shape=(jax.Sha...  4.25 us
    all_to_all x2, waiting for transfers between devices, rolling_step(): lax.all_to_all(slots, TILE_AXES, split_axis=0, concat_axis=0, tiled=True)  4.1 us
  transfers between devices with their start and end apart: 8, of which 3 were waited for; matrix products, arithmetic and copies ran while one was open for 0% of the time, Pallas kernels for 9%

profile of v2, /device:TPU:8, one launch (start us, length us, event | category | flops | bytes accessed | tf_op | source)
XLA Modules:
  0.0 84.0 jit_solution(4677295679719889411)
XLA Ops:
  0.0 2.1 %border.2 = (bf16[4,72,256]{2,1,0:T(8,128)(2,1)}, bf16[16,72,128]{2,1,0:T(8,128)(2,1)}, s32[1]{0:T(128)}) custom-call(s32[4,16]{1,0:T(4,128)} %bitcast.8, f32[17]{0:T(128)} %plan_ref.7, s32[4]{0:T(128)} %level_ref.7, f32[552,128]{1,0:T(8,128)} %bitcast.6, f32[2,69,1,256]{3,2,1,0:T(1,128)} %fresh_ref.7), custom_call_target="tpu_custom_call" | custom-call | tf_op jit(solution)/shard_map/border/pallas_call | solution.py:169
  2.1 6.1 %all-to-all-start = ((bf16[16,72,128]{2,1,0:T(8,128)(2,1)}), bf16[16,72,128]{2,1,0:T(8,128)(2,1)S(1)}, u32[]{:S(2)}, u32[]{:S(2)}) async-start(bf16[16,72,128]{2,1,0:T(8,128)(2,1)} %get-tuple-element.21), calls=%async_computation | async-start | bytes 589824 | tf_op jit(solution)/shard_map/all_to_all | solution.py:407
  8.3 8.5 %collective-permute-start = (bf16[4,72,256]{2,1,0:T(8,128)(2,1)}, bf16[4,72,256]{2,1,0:T(8,128)(2,1)S(1)}, u32[]{:S(2)}, u32[]{:S(2)}) collective-permute-start(bf16[4,72,256]{2,1,0:T(8,128)(2,1)} %get-tuple-element.22.frames_ref), channel_id=1, source_target_pairs={{16,0},{32,16},{48,32},{64,48},{80,64},{96,80},{112,96},{128,112},... | collective-permute-start | bytes 442376 | tf_op jit(solution)/shard_map/ppermute | solution.py:406
  16.8 3.6 %weights.1 = (bf16[256,648]{1,0:T(8,128)(2,1)}, bf16[256,72]{1,0:T(8,128)(2,1)}, bf16[768,256]{1,0:T(8,128)(2,1)}, bf16[256,256]{1,0:T(8,128)(2,1)}, bf16[72,256]{1,0:T(8,128)(2,1)}) custom-call(bf16[69,256]{1,0:T(8,128)(2,1)} %bitcast.14, f32[1,256]{1,0:T(1,128)} %bitcast.15, bf16[9,256,256]{2,1,0:T(8,128)(2,1)} %conv_ref.1, f32[1,256]{1,0:T(1,128)} %bitcast.16, ...), custom_call_target="tpu_custom_call" | custom-call | tf_op jit(solution)/shard_map/weights/pallas_call | solution.py:87
  20.4 0.0 all-to-all-done.slots_ref
  20.4 0.0 copy-start
  20.5 0.7 copy-done
  21.2 2.0 %ring.2 = (bf16[5,72,128]{2,1,0:T(8,128)(2,1)}, bf16[2,72,128]{2,1,0:T(8,128)(2,1)}, bf16[72,384]{1,0:T(8,128)(2,1)}) custom-call(s32[4,16]{1,0:T(4,128)} %bitcast.9, bf16[16,72,128]{2,1,0:T(8,128)(2,1)} %copy-done, bf16[4,72,256]{2,1,0:T(8,128)(2,1)} %get-tuple-element.22.frames_ref, bf16[256,72]{1,0:T(8,128)(2,1)} %get-tuple-element.24.wait_ref.lift_ref), custom_call_target="tpu_custom_call" | custom-call | tf_op jit(solution)/shard_map/ring/pallas_call | solution.py:220
  23.2 6.5 %collective-permute-start.2 = (bf16[72,384]{1,0:T(8,128)(2,1)}, bf16[72,384]{1,0:T(8,128)(2,1)S(1)}, u32[]{:S(2)}, u32[]{:S(2)}) collective-permute-start(bf16[72,384]{1,0:T(8,128)(2,1)} %get-tuple-element.27), channel_id=1, source_target_pairs={{32,0},{48,16},{64,32},{80,48},{96,64},{112,80},{128,96},{144,112}... | collective-permute-start | bytes 165896 | tf_op jit(solution)/shard_map/ppermute | solution.py:412
  29.7 2.9 %collective-permute-start.1 = (bf16[2,72,128]{2,1,0:T(8,128)(2,1)}, bf16[2,72,128]{2,1,0:T(8,128)(2,1)S(1)}, u32[]{:S(2)}, u32[]{:S(2)}) collective-permute-start(bf16[2,72,128]{2,1,0:T(8,128)(2,1)} %get-tuple-element.26), channel_id=1, source_target_pairs={{16,0},{32,16},{48,32},{64,48},{80,64},{96,80},{112,96},{128,112},... | collective-permute-start | bytes 110600 | tf_op jit(solution)/shard_map/ppermute | solution.py:411
  32.6 0.0 collective-permute-done.next_frames_ref
  32.6 0.0 copy-start.2
  32.6 3.1 %collective-permute-done.1.next_ring_ref = bf16[2,72,128]{2,1,0:T(8,128)(2,1)S(1)} collective-permute-done((bf16[2,72,128]{2,1,0:T(8,128)(2,1)}, bf16[2,72,128]{2,1,0:T(8,128)(2,1)S(1)}, u32[]{:S(2)}, u32[]{:S(2)}) %collective-permute-start.1) | collective-permute-done | bytes 36896 | tf_op jit(solution)/shard_map/ppermute | solution.py:411
  35.8 0.0 copy-start.7
  35.8 0.0 collective-permute-done.2.far_ref
  35.8 0.0 copy-start.5
  35.8 0.0 copy-done.2
  35.8 0.6 copy-done.7
  36.4 0.0 copy-done.5
  36.4 8.9 %step.2.queue_ref = f32[552,128]{1,0:T(8,128)} custom-call(s32[4,16]{1,0:T(4,128)} %bitcast.10, f32[17]{0:T(128)} %plan_ref.7, s32[4]{0:T(128)} %level_ref.7, f32[552,128]{1,0:T(8,128)} %bitcast.7, f32[2,69,1,256]{3,2,1,0:T(1,128)} %fresh_ref.7, bf16[5,72,128]{2,1,0:T(8,128)(2,1)} %get-tuple-element.25.ring_ref, bf16[4,72,256]{2,1,0:T(8,128)(2,1)} %copy-done.2, ...), custom_call_target="tpu_custom_call" | custom-call | tf_op jit(solution)/shard_map/step/pallas_call | solution.py:413
  45.3 2.1 %border.3 = (bf16[4,72,256]{2,1,0:T(8,128)(2,1)}, bf16[16,72,128]{2,1,0:T(8,128)(2,1)}, s32[1]{0:T(128)}) custom-call(s32[4,16]{1,0:T(4,128)} %bitcast.11, f32[17]{0:T(128)} %plan_ref.7, s32[4]{0:T(128)} %level_ref.7, f32[552,128]{1,0:T(8,128)} %step.2.queue_ref, f32[2,69,1,256]{3,2,1,0:T(1,128)} %fresh_ref.7), custom_call_target="tpu_custom_call" | custom-call | tf_op jit(solution)/shard_map/border/pallas_call | solution.py:169
  47.4 3.5 %all-to-all-start.1 = ((bf16[16,72,128]{2,1,0:T(8,128)(2,1)}), bf16[16,72,128]{2,1,0:T(8,128)(2,1)S(1)}, u32[]{:S(2)}, u32[]{:S(2)}) async-start(bf16[16,72,128]{2,1,0:T(8,128)(2,1)} %get-tuple-element.32), calls=%async_computation.1 | async-start | bytes 589824 | tf_op jit(solution)/shard_map/all_to_all | solution.py:407
  51.0 5.5 %collective-permute-start.3 = (bf16[4,72,256]{2,1,0:T(8,128)(2,1)}, bf16[4,72,256]{2,1,0:T(8,128)(2,1)S(1)}, u32[]{:S(2)}, u32[]{:S(2)}) collective-permute-start(bf16[4,72,256]{2,1,0:T(8,128)(2,1)} %get-tuple-element.33.frames_ref), channel_id=1, source_target_pairs={{16,0},{32,16},{48,32},{64,48},{80,64},{96,80},{112,96},{128,112},... | collective-permute-start | bytes 442376 | tf_op jit(solution)/shard_map/ppermute | solution.py:406
  56.5 4.1 %all-to-all-done.1.slots_ref = bf16[16,72,128]{2,1,0:T(8,128)(2,1)S(1)} async-done(((bf16[16,72,128]{2,1,0:T(8,128)(2,1)}), bf16[16,72,128]{2,1,0:T(8,128)(2,1)S(1)}, u32[]{:S(2)}, u32[]{:S(2)}) %all-to-all-start.1) | async-done | bytes 294944 | tf_op jit(solution)/shard_map/all_to_all | solution.py:407
  60.6 0.0 copy-start.1
  60.6 0.7 copy-done.1
  61.4 2.0 %ring.3 = (bf16[5,72,128]{2,1,0:T(8,128)(2,1)}, bf16[2,72,128]{2,1,0:T(8,128)(2,1)}, bf16[72,384]{1,0:T(8,128)(2,1)}) custom-call(s32[4,16]{1,0:T(4,128)} %bitcast.12, bf16[16,72,128]{2,1,0:T(8,128)(2,1)} %copy-done.1, bf16[4,72,256]{2,1,0:T(8,128)(2,1)} %get-tuple-element.33.frames_ref, bf16[256,72]{1,0:T(8,128)(2,1)} %get-tuple-element.24.wait_ref.lift_ref), custom_call_target="tpu_custom_call" | custom-call | tf_op jit(solution)/shard_map/ring/pallas_call | solution.py:220
  63.4 4.2 %collective-permute-start.5 = (bf16[72,384]{1,0:T(8,128)(2,1)}, bf16[72,384]{1,0:T(8,128)(2,1)S(1)}, u32[]{:S(2)}, u32[]{:S(2)}) collective-permute-start(bf16[72,384]{1,0:T(8,128)(2,1)} %get-tuple-element.36), channel_id=1, source_target_pairs={{32,0},{48,16},{64,32},{80,48},{96,64},{112,80},{128,96},{144,112}... | collective-permute-start | bytes 165896 | tf_op jit(solution)/shard_map/ppermute | solution.py:412
  67.6 3.3 %collective-permute-start.4 = (bf16[2,72,128]{2,1,0:T(8,128)(2,1)}, bf16[2,72,128]{2,1,0:T(8,128)(2,1)S(1)}, u32[]{:S(2)}, u32[]{:S(2)}) collective-permute-start(bf16[2,72,128]{2,1,0:T(8,128)(2,1)} %get-tuple-element.35), channel_id=1, source_target_pairs={{16,0},{32,16},{48,32},{64,48},{80,64},{96,80},{112,96},{128,112},... | collective-permute-start | bytes 110600 | tf_op jit(solution)/shard_map/ppermute | solution.py:411
  70.9 0.0 collective-permute-done.3.next_frames_ref
  70.9 0.0 copy-start.3
  70.9 3.6 %collective-permute-done.4.next_ring_ref = bf16[2,72,128]{2,1,0:T(8,128)(2,1)S(1)} collective-permute-done((bf16[2,72,128]{2,1,0:T(8,128)(2,1)}, bf16[2,72,128]{2,1,0:T(8,128)(2,1)S(1)}, u32[]{:S(2)}, u32[]{:S(2)}) %collective-permute-start.4) | collective-permute-done | bytes 36896 | tf_op jit(solution)/shard_map/ppermute | solution.py:411
  74.5 0.0 copy-start.6
  74.5 0.0 collective-permute-done.5.far_ref
  74.5 0.0 copy-start.4
  74.5 0.0 copy-done.3
  74.5 0.6 copy-done.6
  75.1 0.0 copy-done.4
  75.1 8.9 %step.3 = f32[552,128]{1,0:T(8,128)} custom-call(s32[4,16]{1,0:T(4,128)} %bitcast.13, f32[17]{0:T(128)} %plan_ref.7, s32[4]{0:T(128)} %level_ref.7, f32[552,128]{1,0:T(8,128)} %step.2.queue_ref, f32[2,69,1,256]{3,2,1,0:T(1,128)} %fresh_ref.7, bf16[5,72,128]{2,1,0:T(8,128)(2,1)} %get-tuple-element.34.ring_ref, bf16[4,72,256]{2,1,0:T(8,128)(2,1)} %copy-done.3, ...), custom_call_target="tpu_custom_call" | custom-call | tf_op jit(solution)/shard_map/step/pallas_call | solution.py:413
Async XLA Ops:
  2.1 18.3 %all-to-all-start = ((bf16[16,72,128]{2,1,0:T(8,128)(2,1)}), bf16[16,72,128]{2,1,0:T(8,128)(2,1)S(1)}, u32[]{:S(2)}, u32[]{:S(2)}) async-start(bf16[16,72,128]{2,1,0:T(8,128)(2,1)} %get-tuple-element.21), calls=%async_computation | async-start | bytes 589824 | tf_op jit(solution)/shard_map/all_to_all | solution.py:407
  8.3 24.3 %collective-permute-start = (bf16[4,72,256]{2,1,0:T(8,128)(2,1)}, bf16[4,72,256]{2,1,0:T(8,128)(2,1)S(1)}, u32[]{:S(2)}, u32[]{:S(2)}) collective-permute-start(bf16[4,72,256]{2,1,0:T(8,128)(2,1)} %get-tuple-element.22.frames_ref), channel_id=1, source_target_pairs={{16,0},{32,16},{48,32},{64,48},{80,64},{96,80},{112,96},{128,112},... | collective-permute-start | bytes 442376 | tf_op jit(solution)/shard_map/ppermute | solution.py:406
  20.4 0.7 copy-start
  23.2 12.6 %collective-permute-start.2 = (bf16[72,384]{1,0:T(8,128)(2,1)}, bf16[72,384]{1,0:T(8,128)(2,1)S(1)}, u32[]{:S(2)}, u32[]{:S(2)}) collective-permute-start(bf16[72,384]{1,0:T(8,128)(2,1)} %get-tuple-element.27), channel_id=1, source_target_pairs={{32,0},{48,16},{64,32},{80,48},{96,64},{112,80},{128,96},{144,112}... | collective-permute-start | bytes 165896 | tf_op jit(solution)/shard_map/ppermute | solution.py:412
  29.7 6.1 %collective-permute-start.1 = (bf16[2,72,128]{2,1,0:T(8,128)(2,1)}, bf16[2,72,128]{2,1,0:T(8,128)(2,1)S(1)}, u32[]{:S(2)}, u32[]{:S(2)}) collective-permute-start(bf16[2,72,128]{2,1,0:T(8,128)(2,1)} %get-tuple-element.26), channel_id=1, source_target_pairs={{16,0},{32,16},{48,32},{64,48},{80,64},{96,80},{112,96},{128,112},... | collective-permute-start | bytes 110600 | tf_op jit(solution)/shard_map/ppermute | solution.py:411
  32.6 3.1 %copy-start.2 = (bf16[4,72,256]{2,1,0:T(8,128)(2,1)}, bf16[4,72,256]{2,1,0:T(8,128)(2,1)S(1)}, u32[]{:S(2)}) copy-start(bf16[4,72,256]{2,1,0:T(8,128)(2,1)S(1)} %collective-permute-done.next_frames_ref) | copy-start | bytes 442372
  35.8 0.6 copy-start.7
  35.8 0.7 copy-start.5
  47.4 13.2 %all-to-all-start.1 = ((bf16[16,72,128]{2,1,0:T(8,128)(2,1)}), bf16[16,72,128]{2,1,0:T(8,128)(2,1)S(1)}, u32[]{:S(2)}, u32[]{:S(2)}) async-start(bf16[16,72,128]{2,1,0:T(8,128)(2,1)} %get-tuple-element.32), calls=%async_computation.1 | async-start | bytes 589824 | tf_op jit(solution)/shard_map/all_to_all | solution.py:407
  51.0 19.9 %collective-permute-start.3 = (bf16[4,72,256]{2,1,0:T(8,128)(2,1)}, bf16[4,72,256]{2,1,0:T(8,128)(2,1)S(1)}, u32[]{:S(2)}, u32[]{:S(2)}) collective-permute-start(bf16[4,72,256]{2,1,0:T(8,128)(2,1)} %get-tuple-element.33.frames_ref), channel_id=1, source_target_pairs={{16,0},{32,16},{48,32},{64,48},{80,64},{96,80},{112,96},{128,112},... | collective-permute-start | bytes 442376 | tf_op jit(solution)/shard_map/ppermute | solution.py:406
  60.6 0.7 copy-start.1
  63.4 11.1 %collective-permute-start.5 = (bf16[72,384]{1,0:T(8,128)(2,1)}, bf16[72,384]{1,0:T(8,128)(2,1)S(1)}, u32[]{:S(2)}, u32[]{:S(2)}) collective-permute-start(bf16[72,384]{1,0:T(8,128)(2,1)} %get-tuple-element.36), channel_id=1, source_target_pairs={{32,0},{48,16},{64,32},{80,48},{96,64},{112,80},{128,96},{144,112}... | collective-permute-start | bytes 165896 | tf_op jit(solution)/shard_map/ppermute | solution.py:412
  67.6 6.9 %collective-permute-start.4 = (bf16[2,72,128]{2,1,0:T(8,128)(2,1)}, bf16[2,72,128]{2,1,0:T(8,128)(2,1)S(1)}, u32[]{:S(2)}, u32[]{:S(2)}) collective-permute-start(bf16[2,72,128]{2,1,0:T(8,128)(2,1)} %get-tuple-element.35), channel_id=1, source_target_pairs={{16,0},{32,16},{48,32},{64,48},{80,64},{96,80},{112,96},{128,112},... | collective-permute-start | bytes 110600 | tf_op jit(solution)/shard_map/ppermute | solution.py:411
  70.9 3.6 %copy-start.3 = (bf16[4,72,256]{2,1,0:T(8,128)(2,1)}, bf16[4,72,256]{2,1,0:T(8,128)(2,1)S(1)}, u32[]{:S(2)}) copy-start(bf16[4,72,256]{2,1,0:T(8,128)(2,1)S(1)} %collective-permute-done.3.next_frames_ref) | copy-start | bytes 442372
  74.5 0.6 copy-start.6
  74.5 0.6 copy-start.4

commit v3 on v2

v3 whole, which is shorter than its diff:
```python
import functools

import jax
import jax.numpy as jnp
from jax import lax
from jax.experimental import pallas as pl
from jax.experimental.pallas import tpu as pltpu
from jax.sharding import Mesh
from jax.sharding import PartitionSpec as P

FIELDS = 69
ROWS = 72
WIDTH = 256
HEADS = 8
HEAD = WIDTH // HEADS
TILE = 16
CELLS = TILE * TILE
TAPS = 9
SLOT = 80
UNROLL = 4
FR_DEV = 4
STEPS = 2
NTILES = 16
TILE_AXES = ("tile_0", "tile_1", "tile_2")
BF = jnp.bfloat16
F32 = jnp.float32

VMEM = pl.BlockSpec(memory_space=pltpu.VMEM)
SMEM = pl.BlockSpec(memory_space=pltpu.SMEM)


def iota(shape, dim):
    return lax.broadcasted_iota(jnp.int32, shape, dim)


def mm(a, b):
    return jnp.dot(a, b, preferred_element_type=F32)


def mm_nt(a, b):
    return lax.dot_general(a, b, (((1,), (1,)), ((), ())), preferred_element_type=F32)


def split_hi_lo(v):
    hi = v.astype(BF).astype(F32)
    return hi, v - hi


def weights_kernel(
    in_ref, embed_ref, conv_ref, gain_ref, query_ref, memory_ref, out_ref, decode_ref, after_ref,
    taps_out, lift_out, qkv_out, attend_out, decode_out, folded,
):
    rows = iota((ROWS, WIDTH), 0)
    unit = (iota((ROWS, FIELDS), 0) == iota((ROWS, FIELDS), 1)).astype(BF)
    lift_t = mm(unit, in_ref[...])
    embed = jnp.broadcast_to(embed_ref[...], (ROWS, WIDTH))
    embed_hi, embed_lo = split_hi_lo(embed)
    stacked = jnp.where(
        rows == FIELDS, embed_hi, jnp.where(rows == FIELDS + 1, embed_lo, lift_t)
    ).astype(BF)
    lift_rows = jnp.where(
        rows >= FIELDS, jnp.where(rows == FIELDS + 2, embed_lo, embed_hi), lift_t
    )
    lift_out[...] = jnp.transpose(lift_rows).astype(BF)
    for tap in range(TAPS):
        both = mm_nt(stacked, conv_ref[tap])
        whole = jnp.broadcast_to(
            both[FIELDS : FIELDS + 1] + both[FIELDS + 1 : FIELDS + 2], (ROWS, WIDTH)
        )
        hi, lo = split_hi_lo(whole)
        folded[pl.ds(tap * ROWS, ROWS), :] = jnp.where(
            rows >= FIELDS, jnp.where(rows == FIELDS + 2, lo, hi), both
        )
    taps_out[...] = jnp.transpose(folded[...]).astype(BF)
    place = iota((WIDTH, WIDTH), 0)
    order = ((place % HEADS) * HEAD + place // HEADS == iota((WIDTH, WIDTH), 1)).astype(BF)
    gain = gain_ref[...]
    qkv_out[0:WIDTH, :] = (mm(order, query_ref[...]) * gain).astype(BF)
    for part in range(2):
        qkv_out[pl.ds((part + 1) * WIDTH, WIDTH), :] = (
            mm(order, memory_ref[pl.ds(part * WIDTH, WIDTH), :]) * gain
        ).astype(BF)
    attend_out[...] = mm_nt(out_ref[...], order).astype(BF)
    decode_out[...] = mm(unit, decode_ref[...]).astype(BF)


def prepare_weights(in_weight, embed, conv, gain, query, memory, attend, decode, after):
    return pl.pallas_call(
        weights_kernel,
        out_shape=(
            jax.ShapeDtypeStruct((WIDTH, TAPS * ROWS), BF),
            jax.ShapeDtypeStruct((WIDTH, ROWS), BF),
            jax.ShapeDtypeStruct((3 * WIDTH, WIDTH), BF),
            jax.ShapeDtypeStruct((WIDTH, WIDTH), BF),
            jax.ShapeDtypeStruct((ROWS, WIDTH), BF),
        ),
        in_specs=[VMEM] * 8 + [SMEM],
        out_specs=(VMEM,) * 5,
        scratch_shapes=[pltpu.VMEM((TAPS * ROWS, WIDTH), F32)],
        name="weights",
    )(
        in_weight.T, embed.reshape(1, WIDTH), conv, gain.reshape(1, WIDTH), query, memory, attend,
        decode, after,
    )


def frame_rows(queue_ref, frame):
    halves = [
        queue_ref[pl.ds(frame * 2 * FIELDS + half, FIELDS, stride=2), :] for half in range(2)
    ]
    return jnp.concatenate(halves, axis=1)


def sigma_rows(sigma, lanes):
    rows = iota((8, lanes), 0)
    first, rest = split_hi_lo(jnp.broadcast_to(sigma, (8, lanes)))
    second, third = split_hi_lo(rest)
    return jnp.where(rows == 5, first, jnp.where(rows == 6, second, third))


def border_kernel(
    near_ref, plan_ref, level_ref, queue_ref, fresh_ref,
    frames_out, slots_out, after_out, full, folded, later, lines,
):
    me = lax.axis_index(TILE_AXES)
    after_out[0] = 0
    for f in range(FR_DEV):
        sigma = jnp.full((8, CELLS), plan_ref[level_ref[f]], F32)
        full[pl.ds(f * ROWS + 64, 8), :] = sigma_rows(sigma, CELLS)
        full[pl.ds(f * ROWS, FIELDS), :] = frame_rows(queue_ref, f)
    full[pl.ds(FR_DEV * ROWS + 64, 8), :] = jnp.zeros((8, CELLS), F32)
    full[pl.ds(FR_DEV * ROWS, FIELDS), :] = fresh_ref[1, :, 0, :]

    @pl.when(lax.axis_index("noise") == 0)
    def _():
        full[0:FIELDS, :] = fresh_ref[0, :, 0, :]

    frames = full[...].astype(BF)
    for f in range(FR_DEV):
        frames_out[f] = full[pl.ds(f * ROWS, ROWS), :].astype(BF)
    cell = iota((CELLS, 128), 0)
    want = iota((CELLS, 128), 1)
    line = want // (2 * TILE)
    depth = want % (2 * TILE) // TILE
    along = want % TILE
    source = jnp.where(
        line == 0,
        along * TILE + TILE - 1 - depth,
        jnp.where(
            line == 1,
            along * TILE + depth,
            jnp.where(line == 2, (TILE - 1 - depth) * TILE + along, depth * TILE + along),
        ),
    )
    found = mm(frames, (cell == source).astype(BF))
    later[...] = found[FR_DEV * ROWS :]
    lane = iota((ROWS, 128), 1)
    lane9 = iota((9, 128), 1)
    folded[ROWS:SLOT, :] = jnp.zeros((SLOT - ROWS, 128), F32)
    for r in range(4):
        packed = jnp.zeros((ROWS, 128), F32)
        for f in range(FR_DEV):
            one = found[f * ROWS : (f + 1) * ROWS]
            turn = (2 * TILE * (f - r)) % 128
            if turn:
                one = pltpu.roll(one, turn, 1)
            packed = jnp.where(lane // (2 * TILE) == f, one, packed)
        folded[0:ROWS, :] = packed
        packed = jnp.zeros((9, 128), F32)
        for k in range(8):
            one = later[pl.ds(9 * k, 9), :]
            turn = (TILE * k - 2 * TILE * r) % 128
            if turn:
                one = pltpu.roll(one, turn, 1)
            packed = jnp.where(lane9 // TILE == k, one, packed)
        folded[FIELDS : FIELDS + 9, :] = packed
        lines[r] = folded[...].astype(BF)
    for j in range(NTILES):
        north = near_ref[2, j]
        beside = jnp.maximum(north, near_ref[3, j])
        from_west = jnp.logical_or(near_ref[0, j] == me, near_ref[0, beside] == me)
        from_east = jnp.logical_or(near_ref[1, j] == me, near_ref[1, beside] == me)
        vertical = jnp.where(north >= 0, 2, 3)
        code = jnp.where(from_west, 0, jnp.where(from_east, 1, vertical))
        slots_out[j] = lines[code]


def border_lines(near, plan, levels, queue, fresh):
    return pl.pallas_call(
        border_kernel,
        out_shape=(
            jax.ShapeDtypeStruct((FR_DEV, ROWS, CELLS), BF),
            jax.ShapeDtypeStruct((NTILES, SLOT, 128), BF),
            jax.ShapeDtypeStruct((1,), jnp.int32),
        ),
        in_specs=[SMEM, SMEM, SMEM, VMEM, VMEM],
        out_specs=(VMEM, VMEM, SMEM),
        scratch_shapes=[
            pltpu.VMEM(((FR_DEV + 1) * ROWS, CELLS), F32),
            pltpu.VMEM((SLOT, 128), F32),
            pltpu.VMEM((ROWS, 128), F32),
            pltpu.VMEM((4, SLOT, 128), BF),
        ],
        name="border",
    )(near, plan, levels, queue, fresh)


def halo_lane(row, column, near_row, far_row):
    west = jnp.where(column == -1, row, 64 + row)
    east = jnp.where(column == TILE, TILE + row, 80 + row)
    sides = jnp.where(column < 0, west, east)
    near_line = jnp.where(
        column == -1,
        48,
        jnp.where(column == TILE, 49, jnp.where(column < 0, 112, jnp.where(column > TILE, 115, 32 + column))),
    )
    far_line = jnp.where(
        column == -1,
        113,
        jnp.where(column == TILE, 116, jnp.where(column < 0, 114, jnp.where(column > TILE, 117, 96 + column))),
    )
    inside = jnp.logical_and(row >= 0, row < TILE)
    return jnp.where(
        inside,
        sides,
        jnp.where(row == near_row, near_line, jnp.where(row == far_row, far_line, -1)),
    )


def ring_kernel(near_ref, slots_ref, frames_ref, wait_ref, halo_out, later_out, far_out, picked, spare):
    me = lax.axis_index(TILE_AXES)
    north = near_ref[2, me]
    beside = jnp.maximum(north, near_ref[3, me])
    picked[:, 0:128] = slots_ref[near_ref[0, me]].astype(F32)
    picked[:, 128:256] = slots_ref[near_ref[1, me]].astype(F32)
    picked[:, 256:384] = slots_ref[beside].astype(F32)
    picked[:, 384:512] = slots_ref[near_ref[0, beside]].astype(F32)
    picked[:, 512:640] = slots_ref[near_ref[1, beside]].astype(F32)
    low = picked[...].astype(BF)
    is_north = (north >= 0).astype(jnp.int32)
    near_place = is_north * (TILE - 1)
    far_place = is_north * (TILE - 2) + (1 - is_north)

    def source(lane):
        block = lane // TILE
        along = lane % TILE
        side = jnp.where(block < 3, block, block - 4)
        deep = (lane >= 64).astype(jnp.int32)
        corner = jnp.logical_or(block == 3, block == 7)
        east_corner = jnp.where(block == 3, along, (along >= 3).astype(jnp.int32))
        which = jnp.where(block == 3, 0, 1 + along % 3)
        corner_deep = jnp.logical_or(which == 1, which == 3).astype(jnp.int32)
        corner_place = jnp.where(which >= 2, far_place, near_place)
        known = along < jnp.where(block == 3, 2, 6)
        plain = side * 128 + deep * TILE + along
        ends = (3 + east_corner) * 128 + corner_deep * TILE + corner_place
        lost = jnp.logical_and(corner, jnp.logical_not(known))
        later = jnp.where(corner, (3 + east_corner) * 128 + corner_place, side * 128 + along)
        return (
            jnp.where(lost, -10000, jnp.where(corner, ends, plain)),
            jnp.where(lost, -10000, later),
        )

    column = iota((8, FR_DEV * 128), 1)
    spot = source(column % 128)[0] + 2 * TILE * (column // 128)
    pick = (iota((5 * 128, FR_DEV * 128), 0) == spot[0:1]).astype(BF)
    halos = mm(low[0:ROWS], pick)
    for f in range(FR_DEV):
        halo_out[f] = halos[:, f * 128 : (f + 1) * 128].astype(BF)
    far_out[:, 0:CELLS] = frames_ref[0]
    far_out[:, CELLS : CELLS + 128] = halos[:, 0:128].astype(BF)
    column = iota((8, 8 * 64), 1)
    spot = source(column % 64)[1] + TILE * (column // 64)
    pick = (iota((5 * 128, 8 * 64), 0) == spot[0:1]).astype(BF)
    spare[...] = jnp.zeros_like(spare)
    blocks = mm(picked[64:SLOT].astype(BF), pick)
    for k in range(8):
        one = blocks[5:14, (k // 2) * 128 : (k // 2 + 1) * 128]
        spare[pl.ds(9 * k, 9), :] = pltpu.roll(one, 64, 1) if k % 2 else one
    later_out[...] = spare[...].astype(BF)


def halo_cells(near, slots, frames, wait):
    return pl.pallas_call(
        ring_kernel,
        out_shape=(
            jax.ShapeDtypeStruct((FR_DEV, ROWS, 128), BF),
            jax.ShapeDtypeStruct((ROWS, 128), BF),
            jax.ShapeDtypeStruct((ROWS, CELLS + 128), BF),
        ),
        in_specs=[SMEM, VMEM, VMEM, pl.BlockSpec(memory_space=pl.ANY)],
        out_specs=(VMEM,) * 3,
        scratch_shapes=[pltpu.VMEM((SLOT, 5 * 128), F32), pltpu.VMEM((ROWS, 128), F32)],
        name="ring",
    )(near, slots, frames, wait)


def with_log_rows(scaled, log_hi, log_lo, lanes):
    rows = iota((ROWS, lanes), 0)
    return jnp.where(
        rows >= FIELDS, jnp.where(rows == FIELDS + 1, log_lo, log_hi), scaled
    )


def wide(row, lanes):
    return jnp.concatenate([row] * (lanes // 128), axis=1)


def denoise(
    lanes, near_ref, plan_ref, level_ref, weights, states, sigmas, scaled, images, ring_windows,
    hidden_all, qkv_all, context_all, finished,
):
    taps_ref, lift_ref, qkv_ref, attend_ref, decode_ref = weights
    me = lax.axis_index(TILE_AXES)
    is_last = lax.axis_index("noise") == lax.axis_size("noise") - 1
    at_north = near_ref[2, me] >= 0
    north_here = at_north.astype(F32)
    south_here = 1.0 - north_here
    extended = lanes > CELLS

    for p in range(2 * FR_DEV):
        sigma = sigmas[p]
        log_hi, log_lo = split_hi_lo(jnp.log(sigma))
        scale = 1.0 / jnp.sqrt(sigma * sigma + 1.0)
        total = CELLS + 128
        scaled[p] = with_log_rows(
            states[p] * wide(scale, total), wide(log_hi, total), wide(log_lo, total), total
        )
    ring_row = iota((128, 4 * CELLS), 0)
    column = iota((8, 4 * CELLS), 1)
    shift = column // CELLS - 2
    cell_x = column % TILE
    cell_y = (column % CELLS) // TILE
    line_x = cell_x + shift
    from_line = jnp.where(
        line_x < 0, 3 * TILE, jnp.where(line_x >= TILE, 3 * TILE + 1, 2 * TILE + line_x)
    )
    from_side = jnp.where(cell_x == 0, cell_y, TILE + cell_y)
    spot = jnp.where(column < CELLS, from_side, from_line)
    spread = (ring_row == spot[0:1]).astype(BF)
    low = scaled[...].reshape(2 * FR_DEV * ROWS, CELLS + 128).astype(BF)
    images[...] = mm(low[:, CELLS:], spread).reshape(2 * FR_DEV, ROWS, 4 * CELLS)
    if extended:
        near_row = jnp.where(at_north, -1, TILE)
        far_row = jnp.where(at_north, -2, TILE + 1)
        column = iota((8, 5 * 128), 1)
        tap = column // 64
        cell = column % 64
        block = cell // TILE
        along = cell % TILE
        row = jnp.where(block < 2, along, near_row) + tap // 3 - 1
        col = jnp.where(
            block == 0,
            -1,
            jnp.where(block == 1, TILE, jnp.where(block == 2, along, jnp.where(along == 0, -1, TILE))),
        )
        col = col + tap % 3 - 1
        in_tile = jnp.logical_and(
            jnp.logical_and(row >= 0, row < TILE), jnp.logical_and(col >= 0, col < TILE)
        )
        halo = halo_lane(row, col, near_row, far_row)
        spot = jnp.where(
            in_tile, row * TILE + col, jnp.where(halo >= 0, CELLS + halo, -1)
        )
        spot = jnp.where(cell < 50, spot, -1)
        pick = (iota((CELLS + 128, 5 * 128), 0) == spot[0:1]).astype(BF)
        ring_windows[...] = mm(low, pick).reshape(2 * FR_DEV, ROWS, 5 * 128)

    across = iota((ROWS, CELLS), 1) % TILE
    down = iota((ROWS, CELLS), 1) // TILE

    def features(p):
        inner = scaled[p, :, 0:CELLS].astype(BF).astype(F32)
        sides = images[p, :, 0:CELLS]
        shifted = (
            jnp.where(across == 0, sides, pltpu.roll(inner, 1, 1)),
            inner,
            jnp.where(across == TILE - 1, sides, pltpu.roll(inner, CELLS - 1, 1)),
        )
        up = []
        low = []
        for b in range(3):
            line = images[p, :, (b + 1) * CELLS : (b + 2) * CELLS]
            up.append(jnp.where(down == 0, line * north_here, pltpu.roll(shifted[b], TILE, 1)))
            low.append(
                jnp.where(
                    down == TILE - 1, line * south_here, pltpu.roll(shifted[b], CELLS - TILE, 1)
                )
            )
        windows = jnp.concatenate([*up, *shifted, *low], axis=0)
        if extended:
            beyond = []
            for tap in range(TAPS):
                one = ring_windows[p, :, (tap // 2) * 128 : (tap // 2 + 1) * 128]
                beyond.append(pltpu.roll(one, 64, 1) if tap % 2 else one)
            windows = jnp.concatenate([windows, jnp.concatenate(beyond, axis=0)], axis=1)
        convolved = mm(taps_ref[...], windows.astype(BF))
        lifted = mm(lift_ref[...], scaled[p, :, 0:lanes].astype(BF))
        hidden = lifted + convolved / (1.0 + jnp.exp(-convolved))
        power = jnp.mean(hidden * hidden, axis=0, keepdims=True)
        return hidden, (hidden * lax.rsqrt(power + 1e-06)).astype(BF)

    def own(p, carry):
        hidden, normed = features(p)
        hidden_all[p] = hidden
        qkv_all[p] = mm(qkv_ref[...], normed).reshape(3 * HEAD, HEADS, lanes)
        return carry

    def following(p, carry):
        _, normed = features(p)
        qkv_all[p, HEAD : 3 * HEAD] = mm(qkv_ref[WIDTH : 3 * WIDTH, :], normed).reshape(
            2 * HEAD, HEADS, lanes
        )
        return carry

    lax.fori_loop(0, FR_DEV, own, 0, unroll=UNROLL)
    lax.fori_loop(FR_DEV, 2 * FR_DEV, following, 0, unroll=UNROLL)

    hide = jnp.where(is_last, -jnp.inf, 0.0)
    for part in range(lanes // 128):
        at = slice(part * 128, part * 128 + 128)

        def score(d, sums):
            keys = qkv_all[:, HEAD + d, :, at]
            return tuple(sums[i] + qkv_all[i, d, :, at][None] * keys for i in range(FR_DEV))

        zero = jnp.zeros((2 * FR_DEV, HEADS, 128), F32)
        sums = lax.fori_loop(0, HEAD, score, (zero,) * FR_DEV, unroll=4)
        second_half = iota((2 * FR_DEV, HEADS, 128), 0) >= FR_DEV
        weights = []
        for i in range(FR_DEV):
            scores = sums[i] * HEAD ** (-0.5) + jnp.where(second_half, hide, 0.0)
            top = jnp.max(scores, axis=0, keepdims=True)
            raised = jnp.exp(scores - top)
            weights.append(raised / jnp.sum(raised, axis=0, keepdims=True))

        def combine(d, carry):
            values = qkv_all[:, 2 * HEAD + d, :, at]
            for i in range(FR_DEV):
                context_all[i, d, :, at] = jnp.sum(weights[i] * values, axis=0)
            return carry

        lax.fori_loop(0, HEAD, combine, 0, unroll=4)

    for p in range(FR_DEV):
        context = context_all[p].reshape(WIDTH, lanes).astype(BF)
        refined = (hidden_all[p] + mm(attend_ref[...], context)).astype(BF)
        projected = mm(decode_ref[...], refined)
        sigma = wide(sigmas[p], lanes)
        sigma_next = jnp.full((1, lanes), plan_ref[level_ref[p] + 1], F32)
        spread_of = sigma * sigma + 1.0
        slope = (sigma_next - sigma) / sigma
        state = states[p, :, 0:lanes]
        denoised = state / spread_of + sigma / jnp.sqrt(spread_of) * projected
        finished(p, state + slope * (state - denoised))


def fill_sigmas(plan_ref, level_ref, next_frames_ref, sigmas):
    for f in range(FR_DEV):
        came = next_frames_ref[f, 64:ROWS, 0:128].astype(F32)
        sigmas[f] = jnp.full((1, 128), plan_ref[level_ref[f]], F32)
        sigmas[FR_DEV + f] = came[5:6] + came[6:7] + came[7:8]


def scale_entering(states, sigmas):
    group = lax.axis_index("noise")
    groups = lax.axis_size("noise")
    for p, holder in ((FR_DEV - 1, groups - 1), (2 * FR_DEV - 1, groups - 2)):

        @pl.when(group == holder)
        def _(p=p):
            states[p] = states[p] * wide(sigmas[p], CELLS + 128)


def first_kernel(
    near_ref, plan_ref, level_ref, queue_ref, fresh_ref, halo_ref, later_ref, next_frames_ref,
    next_halo_ref, far_ref, taps_ref, lift_ref, qkv_ref, attend_ref, decode_ref,
    own_out, near_out, far_out,
    states, sigmas, scaled, images, ring_windows, hidden_all, qkv_all, context_all, message,
):
    fill_sigmas(plan_ref, level_ref, next_frames_ref, sigmas)
    for p in range(FR_DEV - 1):
        states[p, 64:ROWS, 0:CELLS] = jnp.zeros((ROWS - 64, CELLS), F32)
        states[p, 0:FIELDS, 0:CELLS] = frame_rows(queue_ref, p + 1)
        states[p, :, CELLS:] = halo_ref[p + 1].astype(F32)
    for f in range(FR_DEV):
        states[FR_DEV - 1 + f, :, 0:CELLS] = next_frames_ref[f].astype(F32)
        states[FR_DEV - 1 + f, :, CELLS:] = next_halo_ref[f].astype(F32)
    states[2 * FR_DEV - 1] = far_ref[...].astype(F32)
    scale_entering(states, sigmas)

    def finished(p, moved):
        own_out[p] = moved
        message[p, 0:64] = moved[0:64]
        rows = iota((8, CELLS + 128), 0)
        message[p, 64:ROWS] = jnp.where(
            rows >= FIELDS - 64, sigma_rows(wide(sigmas[p], CELLS + 128), CELLS + 128), moved[64:ROWS]
        )

    denoise(
        CELLS + 128, near_ref, plan_ref, level_ref,
        (taps_ref, lift_ref, qkv_ref, attend_ref, decode_ref),
        states, sigmas, scaled, images, ring_windows, hidden_all, qkv_all, context_all, finished,
    )

    @pl.when(lax.axis_index("noise") == 0)
    def _():
        message[0, 0:FIELDS, 0:CELLS] = fresh_ref[1, :, 0, :]
        message[0, 0:FIELDS, CELLS:] = later_ref[...].astype(F32)[0:FIELDS]

    lane = iota((ROWS, 128), 1)
    for f in range(FR_DEV):
        near_out[f] = message[f, :, 0:CELLS].astype(BF)
    for pair in range(2):
        near_out[FR_DEV, :, pair * 128 : pair * 128 + 128] = jnp.where(
            lane < 64,
            message[2 * pair, :, CELLS:],
            pltpu.roll(message[2 * pair + 1, :, CELLS:], 64, 1),
        ).astype(BF)
    far_out[...] = message[0].astype(BF)


def second_kernel(
    near_ref, plan_ref, level_ref, own_ref, came_ref, far_ref,
    taps_ref, lift_ref, qkv_ref, attend_ref, decode_ref,
    out_ref, states, sigmas, scaled, images, hidden_all, qkv_all, context_all,
):
    fill_sigmas(plan_ref, level_ref, came_ref, sigmas)
    for p in range(FR_DEV - 1):
        states[p] = own_ref[p + 1]
    for f in range(FR_DEV):
        states[FR_DEV - 1 + f, :, 0:CELLS] = came_ref[f].astype(F32)
        pair = came_ref[FR_DEV, :, (f // 2) * 128 : (f // 2 + 1) * 128].astype(F32)
        states[FR_DEV - 1 + f, :, CELLS:] = pltpu.roll(pair, 64, 1) if f % 2 else pair
    states[2 * FR_DEV - 1] = far_ref[...].astype(F32)
    scale_entering(states, sigmas)

    def finished(p, moved):
        for half in range(2):
            out_ref[pl.ds(p * 2 * FIELDS + half, FIELDS, stride=2), :] = moved[
                0:FIELDS, half * 128 : half * 128 + 128
            ]

    denoise(
        CELLS, near_ref, plan_ref, level_ref,
        (taps_ref, lift_ref, qkv_ref, attend_ref, decode_ref),
        states, sigmas, scaled, images, None, hidden_all, qkv_all, context_all, finished,
    )


def common_scratch(lanes):
    frames = 2 * FR_DEV
    return [
        pltpu.VMEM((frames, ROWS, CELLS + 128), F32),
        pltpu.VMEM((frames, 1, 128), F32),
        pltpu.VMEM((frames, ROWS, CELLS + 128), F32),
        pltpu.VMEM((frames, ROWS, 4 * CELLS), F32),
    ], [
        pltpu.VMEM((FR_DEV, WIDTH, lanes), F32),
        pltpu.VMEM((frames, 3 * HEAD, HEADS, lanes), F32),
        pltpu.VMEM((FR_DEV, HEAD, HEADS, lanes), F32),
    ]


def shards(
    queue_state, fresh_noise, plan, levels, neighbours, in_weight, level_embed, conv_weight,
    norm_gain, query_weight, memory_weight, attend_out, decode_weight,
):
    groups = lax.axis_size("noise")
    from_next = [((i + 1) % groups, i) for i in range(groups)]
    from_second = [((i + 2) % groups, i) for i in range(groups)]
    near = neighbours.T
    queue = queue_state.reshape(FR_DEV * FIELDS * 2, 128)
    frames, slots, after = border_lines(near, plan, levels, queue, fresh_noise)
    next_frames = lax.ppermute(frames, "noise", from_next)
    slots = lax.all_to_all(slots, TILE_AXES, split_axis=0, concat_axis=0, tiled=True)
    weights = prepare_weights(
        in_weight, level_embed, conv_weight, norm_gain, query_weight, memory_weight,
        attend_out, decode_weight, after,
    )
    halos, later, far = halo_cells(near, slots, frames, weights[1])
    next_halos = lax.ppermute(halos, "noise", from_next)
    far = lax.ppermute(far, "noise", from_second)
    before, after_features = common_scratch(CELLS + 128)
    own, near_message, far_message = pl.pallas_call(
        first_kernel,
        out_shape=(
            jax.ShapeDtypeStruct((FR_DEV, ROWS, CELLS + 128), F32),
            jax.ShapeDtypeStruct((FR_DEV + 1, ROWS, CELLS), BF),
            jax.ShapeDtypeStruct((ROWS, CELLS + 128), BF),
        ),
        in_specs=[SMEM] * 3 + [VMEM] * 12,
        out_specs=(VMEM,) * 3,
        scratch_shapes=[
            *before,
            pltpu.VMEM((2 * FR_DEV, ROWS, 5 * 128), F32),
            *after_features,
            pltpu.VMEM((FR_DEV, ROWS, CELLS + 128), F32),
        ],
        name="first",
    )(
        near, plan, levels, queue, fresh_noise, halos, later, next_frames, next_halos, far, *weights
    )
    came = lax.ppermute(near_message, "noise", from_next)
    far = lax.ppermute(far_message, "noise", from_second)
    before, after_features = common_scratch(CELLS)
    moved = pl.pallas_call(
        second_kernel,
        out_shape=jax.ShapeDtypeStruct((FR_DEV * FIELDS * 2, 128), F32),
        in_specs=[SMEM] * 3 + [VMEM] * 8,
        out_specs=VMEM,
        scratch_shapes=[*before, *after_features],
        name="second",
    )(near, plan, levels, own, came, far, *weights)
    return moved.reshape(queue_state.shape)


def solution(mesh):
    split = Mesh(
        mesh.devices.reshape(mesh.shape["noise"], 2, 4, 2), ("noise", "tile_0", "tile_1", "tile_2")
    )
    placed = (
        P("noise", None, TILE_AXES, None),
        P(None, None, TILE_AXES, None),
        P(),
        P("noise"),
        P(),
        P(),
        P(),
        P(),
        P(),
        P(),
        P(),
        P(),
        P(),
    )
    return jax.shard_map(
        shards,
        mesh=split,
        in_specs=placed,
        out_specs=P("noise", None, TILE_AXES, None),
        check_vma=False,
    )
```

time: 84.7 us -> 64.4 us (0.76)
  starting transfers between devices: 40.7 us -> 24.8 us
  waiting for transfers between devices: 10.8 us -> 8.75 us
  Pallas kernels: 29.6 us -> 28.4 us
    ppermute x6 -> x5, starting transfers between devices: 31 us -> 18.7 us  [the longest x1 7.81 us: shards(): next_halos = lax.ppermute(halos, 'noise', from_next)]
    all_to_all x2 -> x1, waiting for transfers between devices: 4.1 us -> 0.01 us  [shards(): lax.all_to_all(slots, TILE_AXES, split_axis=0, concat_axis=0, tiled=True)]
    all_to_all x2 -> x1, starting transfers between devices: 9.7 us -> 6.15 us  [shards(): lax.all_to_all(slots, TILE_AXES, split_axis=0, concat_axis=0, tiled=True)]
    ppermute x6 -> x5, waiting for transfers between devices: 6.69 us -> 8.75 us  [the longest x1 5.25 us: shards(): far = lax.ppermute(far, 'noise', from_second)]
    pallas_call x6 -> x4, Pallas kernels: 26 us -> 24.8 us  [the longest x1 11.7 us: shards(): pl.pallas_call(first_kernel, out_shape=(jax.ShapeDtypeStruct((FR_DEV, ROW...]
    unnamed x16 -> x12, local copies, waits for them, and re-layouts: 2.73 us -> 2.06 us
  transfers between devices with their start and end apart: 8 -> 6, of which waited for: 3 -> 2; matrix products, arithmetic and copies ran while one was open for 0% -> 0% of each run, Pallas kernels for 9% -> 9%
where the time goes in v3:
time: 64.4 us; the launch traced here: 64.1 us
  Pallas kernels  28.4 us (44%)
  starting transfers between devices  24.8 us (39%)
  waiting for transfers between devices  8.75 us (14%)
  local copies, waits for them, and re-layouts  2.06 us (3%)
    pallas_call x1, Pallas kernels, shards(): pl.pallas_call(first_kernel, out_shape=(jax.ShapeDtypeStruct((FR_DEV, ROW...  11.7 us
    pallas_call x1, Pallas kernels, shards(): pl.pallas_call(second_kernel, out_shape=jax.ShapeDtypeStruct((FR_DEV * FI...  8.75 us
    ppermute x1, starting transfers between devices, shards(): next_halos = lax.ppermute(halos, 'noise', from_next)  7.81 us
    ppermute x1, starting transfers between devices, shards(): next_frames = lax.ppermute(frames, 'noise', from_next)  6.71 us
    all_to_all x1, starting transfers between devices, shards(): lax.all_to_all(slots, TILE_AXES, split_axis=0, concat_axis=0, tiled=True)  6.15 us
    ppermute x1, waiting for transfers between devices, shards(): far = lax.ppermute(far, 'noise', from_second)  5.25 us
    pallas_call x1, Pallas kernels, prepare_weights(): pl.pallas_call(weights_kernel, out_shape=(jax.ShapeDtypeStruct((WIDTH, TA...  3.58 us
    ppermute x1, waiting for transfers between devices, shards(): far = lax.ppermute(far_message, 'noise', from_second)  3.49 us
  transfers between devices with their start and end apart: 6, of which 2 were waited for; matrix products, arithmetic and copies ran while one was open for 0% of the time, Pallas kernels for 9%

profile of v3, /device:TPU:8, one launch (start us, length us, event | category | flops | bytes accessed | tf_op | source)
XLA Modules:
  0.0 64.1 jit_solution(15230497506196083809)
XLA Ops:
  0.0 2.3 %border.1 = (bf16[4,72,256]{2,1,0:T(8,128)(2,1)}, bf16[16,80,128]{2,1,0:T(8,128)(2,1)}, s32[1]{0:T(128)}) custom-call(s32[4,16]{1,0:T(4,128)} %bitcast.9, f32[17]{0:T(128)} %plan_ref.5, s32[4]{0:T(128)} %level_ref.5, f32[552,128]{1,0:T(8,128)} %bitcast.6, f32[2,69,1,256]{3,2,1,0:T(1,128)} %fresh_ref.3), custom_call_target="tpu_custom_call" | custom-call | tf_op jit(solution)/shard_map/border/pallas_call | solution.py:189
  2.3 6.1 %all-to-all-start = ((bf16[16,80,128]{2,1,0:T(8,128)(2,1)}), bf16[16,80,128]{2,1,0:T(8,128)(2,1)S(1)}, u32[]{:S(2)}, u32[]{:S(2)}) async-start(bf16[16,80,128]{2,1,0:T(8,128)(2,1)} %get-tuple-element.19), calls=%async_computation | async-start | bytes 655360 | tf_op jit(solution)/shard_map/all_to_all | solution.py:576
  8.4 6.7 %collective-permute-start = (bf16[4,72,256]{2,1,0:T(8,128)(2,1)}, bf16[4,72,256]{2,1,0:T(8,128)(2,1)S(1)}, u32[]{:S(2)}, u32[]{:S(2)}) collective-permute-start(bf16[4,72,256]{2,1,0:T(8,128)(2,1)} %get-tuple-element.20.frames_ref), channel_id=1, source_target_pairs={{16,0},{32,16},{48,32},{64,48},{80,64},{96,80},{112,96},{128,112},... | collective-permute-start | bytes 442376 | tf_op jit(solution)/shard_map/ppermute | solution.py:575
  15.2 3.6 %weights.1 = (bf16[256,648]{1,0:T(8,128)(2,1)}, bf16[256,72]{1,0:T(8,128)(2,1)}, bf16[768,256]{1,0:T(8,128)(2,1)}, bf16[256,256]{1,0:T(8,128)(2,1)}, bf16[72,256]{1,0:T(8,128)(2,1)}) custom-call(bf16[69,256]{1,0:T(8,128)(2,1)} %bitcast.8, f32[1,256]{1,0:T(1,128)} %bitcast.13, bf16[9,256,256]{2,1,0:T(8,128)(2,1)} %conv_ref.1, f32[1,256]{1,0:T(1,128)} %bitcast.14, ...), custom_call_target="tpu_custom_call" | custom-call | tf_op jit(solution)/shard_map/weights/pallas_call | solution.py:88
  18.7 0.0 all-to-all-done.slots_ref
  18.7 0.0 copy-start
  18.7 0.7 %copy-done = bf16[16,80,128]{2,1,0:T(8,128)(2,1)} copy-done((bf16[16,80,128]{2,1,0:T(8,128)(2,1)}, bf16[16,80,128]{2,1,0:T(8,128)(2,1)S(1)}, u32[]{:S(2)}) %copy-start) | copy-done | bytes 327704
  19.5 2.1 %ring.1 = (bf16[4,72,128]{2,1,0:T(8,128)(2,1)}, bf16[72,128]{1,0:T(8,128)(2,1)}, bf16[72,384]{1,0:T(8,128)(2,1)}) custom-call(s32[4,16]{1,0:T(4,128)} %bitcast.10, bf16[16,80,128]{2,1,0:T(8,128)(2,1)} %copy-done, bf16[4,72,256]{2,1,0:T(8,128)(2,1)} %get-tuple-element.20.frames_ref, bf16[256,72]{1,0:T(8,128)(2,1)} %get-tuple-element.22.wait_ref.lift_ref), custom_call_target="tpu_custom_call" | custom-call | tf_op jit(solution)/shard_map/ring/pallas_call | solution.py:284
  21.6 7.8 %collective-permute-start.1 = (bf16[4,72,128]{2,1,0:T(8,128)(2,1)}, bf16[4,72,128]{2,1,0:T(8,128)(2,1)S(1)}, u32[]{:S(2)}, u32[]{:S(2)}) collective-permute-start(bf16[4,72,128]{2,1,0:T(8,128)(2,1)} %get-tuple-element.23.halo_ref), channel_id=1, source_target_pairs={{16,0},{32,16},{48,32},{64,48},{80,64},{96,80},{112,96},{128,112},... | collective-permute-start | bytes 221192 | tf_op jit(solution)/shard_map/ppermute | solution.py:582
  29.4 0.0 collective-permute-start.2
  29.4 0.0 collective-permute-done.next_frames_ref
  29.4 0.0 copy-start.2
  29.4 5.3 %collective-permute-done.2.far_ref = bf16[72,384]{1,0:T(8,128)(2,1)S(1)} collective-permute-done((bf16[72,384]{1,0:T(8,128)(2,1)}, bf16[72,384]{1,0:T(8,128)(2,1)S(1)}, u32[]{:S(2)}, u32[]{:S(2)}) %collective-permute-start.2) | collective-permute-done | bytes 55328 | tf_op jit(solution)/shard_map/ppermute | solution.py:583
  34.7 0.0 copy-start.4
  34.7 0.0 collective-permute-done.1.next_halo_ref
  34.7 0.0 copy-start.3
  34.7 0.0 copy-done.2
  34.7 0.6 copy-done.4
  35.3 0.0 copy-done.3
  35.3 11.7 %first.1 = (f32[4,72,384]{2,1,0:T(8,128)}, bf16[5,72,256]{2,1,0:T(8,128)(2,1)}, bf16[72,384]{1,0:T(8,128)(2,1)}) custom-call(s32[4,16]{1,0:T(4,128)} %bitcast.11, f32[17]{0:T(128)} %plan_ref.5, s32[4]{0:T(128)} %level_ref.5, f32[552,128]{1,0:T(8,128)} %bitcast.7, f32[2,69,1,256]{3,2,1,0:T(1,128)} %fresh_ref.3, ...), custom_call_target="tpu_custom_call" | custom-call | tf_op jit(solution)/shard_map/first/pallas_call | solution.py:585
  47.0 2.4 %collective-permute-start.3 = (bf16[5,72,256]{2,1,0:T(8,128)(2,1)}, bf16[5,72,256]{2,1,0:T(8,128)(2,1)S(1)}, u32[]{:S(2)}, u32[]{:S(2)}) collective-permute-start(bf16[5,72,256]{2,1,0:T(8,128)(2,1)} %get-tuple-element.31), channel_id=1, source_target_pairs={{16,0},{32,16},{48,32},{64,48},{80,64},{96,80},{112,96},{128,112},... | collective-permute-start | bytes 552968 | tf_op jit(solution)/shard_map/ppermute | solution.py:604
  49.4 1.8 %collective-permute-start.4 = (bf16[72,384]{1,0:T(8,128)(2,1)}, bf16[72,384]{1,0:T(8,128)(2,1)S(1)}, u32[]{:S(2)}, u32[]{:S(2)}) collective-permute-start(bf16[72,384]{1,0:T(8,128)(2,1)} %get-tuple-element.32), channel_id=1, source_target_pairs={{32,0},{48,16},{64,32},{80,48},{96,64},{112,80},{128,96},{144,112}... | collective-permute-start | bytes 165896 | tf_op jit(solution)/shard_map/ppermute | solution.py:605
  51.1 3.5 %collective-permute-done.4.far_ref = bf16[72,384]{1,0:T(8,128)(2,1)S(1)} collective-permute-done((bf16[72,384]{1,0:T(8,128)(2,1)}, bf16[72,384]{1,0:T(8,128)(2,1)S(1)}, u32[]{:S(2)}, u32[]{:S(2)}) %collective-permute-start.4) | collective-permute-done | bytes 55328 | tf_op jit(solution)/shard_map/ppermute | solution.py:605
  54.6 0.0 copy-start.5
  54.6 0.0 collective-permute-done.3.came_ref
  54.6 0.0 copy-start.1
  54.6 0.6 copy-done.5
  55.3 0.1 copy-done.1
  55.3 8.7 %second.1 = f32[552,128]{1,0:T(8,128)} custom-call(s32[4,16]{1,0:T(4,128)} %bitcast.12, f32[17]{0:T(128)} %plan_ref.5, s32[4]{0:T(128)} %level_ref.5, f32[4,72,384]{2,1,0:T(8,128)} %get-tuple-element.30.own_ref, bf16[5,72,256]{2,1,0:T(8,128)(2,1)} %copy-done.1, bf16[72,384]{1,0:T(8,128)(2,1)} %copy-done.5, bf16[256,648]{1,0:T(8,128)(2,1)} %get-tuple-element.26.taps_ref, ...), custom_call_target="tpu_custom_call" | custom-call | tf_op jit(solution)/shard_map/second/pallas_call | solution.py:607
Async XLA Ops:
  2.3 16.4 %all-to-all-start = ((bf16[16,80,128]{2,1,0:T(8,128)(2,1)}), bf16[16,80,128]{2,1,0:T(8,128)(2,1)S(1)}, u32[]{:S(2)}, u32[]{:S(2)}) async-start(bf16[16,80,128]{2,1,0:T(8,128)(2,1)} %get-tuple-element.19), calls=%async_computation | async-start | bytes 655360 | tf_op jit(solution)/shard_map/all_to_all | solution.py:576
  8.4 21.0 %collective-permute-start = (bf16[4,72,256]{2,1,0:T(8,128)(2,1)}, bf16[4,72,256]{2,1,0:T(8,128)(2,1)S(1)}, u32[]{:S(2)}, u32[]{:S(2)}) collective-permute-start(bf16[4,72,256]{2,1,0:T(8,128)(2,1)} %get-tuple-element.20.frames_ref), channel_id=1, source_target_pairs={{16,0},{32,16},{48,32},{64,48},{80,64},{96,80},{112,96},{128,112},... | collective-permute-start | bytes 442376 | tf_op jit(solution)/shard_map/ppermute | solution.py:575
  18.7 0.7 %copy-start = (bf16[16,80,128]{2,1,0:T(8,128)(2,1)}, bf16[16,80,128]{2,1,0:T(8,128)(2,1)S(1)}, u32[]{:S(2)}) copy-start(bf16[16,80,128]{2,1,0:T(8,128)(2,1)S(1)} %all-to-all-done.slots_ref) | copy-start | bytes 983044
  21.6 13.1 %collective-permute-start.1 = (bf16[4,72,128]{2,1,0:T(8,128)(2,1)}, bf16[4,72,128]{2,1,0:T(8,128)(2,1)S(1)}, u32[]{:S(2)}, u32[]{:S(2)}) collective-permute-start(bf16[4,72,128]{2,1,0:T(8,128)(2,1)} %get-tuple-element.23.halo_ref), channel_id=1, source_target_pairs={{16,0},{32,16},{48,32},{64,48},{80,64},{96,80},{112,96},{128,112},... | collective-permute-start | bytes 221192 | tf_op jit(solution)/shard_map/ppermute | solution.py:582
  29.4 5.3 %collective-permute-start.2 = (bf16[72,384]{1,0:T(8,128)(2,1)}, bf16[72,384]{1,0:T(8,128)(2,1)S(1)}, u32[]{:S(2)}, u32[]{:S(2)}) collective-permute-start(bf16[72,384]{1,0:T(8,128)(2,1)} %get-tuple-element.25), channel_id=1, source_target_pairs={{32,0},{48,16},{64,32},{80,48},{96,64},{112,80},{128,96},{144,112}... | collective-permute-start | bytes 165896 | tf_op jit(solution)/shard_map/ppermute | solution.py:583
  29.4 5.3 %copy-start.2 = (bf16[4,72,256]{2,1,0:T(8,128)(2,1)}, bf16[4,72,256]{2,1,0:T(8,128)(2,1)S(1)}, u32[]{:S(2)}) copy-start(bf16[4,72,256]{2,1,0:T(8,128)(2,1)S(1)} %collective-permute-done.next_frames_ref) | copy-start | bytes 442372
  34.7 0.6 copy-start.4
  34.7 0.7 %copy-start.3 = (bf16[4,72,128]{2,1,0:T(8,128)(2,1)}, bf16[4,72,128]{2,1,0:T(8,128)(2,1)S(1)}, u32[]{:S(2)}) copy-start(bf16[4,72,128]{2,1,0:T(8,128)(2,1)S(1)} %collective-permute-done.1.next_halo_ref) | copy-start | bytes 221188
  47.0 7.6 %collective-permute-start.3 = (bf16[5,72,256]{2,1,0:T(8,128)(2,1)}, bf16[5,72,256]{2,1,0:T(8,128)(2,1)S(1)}, u32[]{:S(2)}, u32[]{:S(2)}) collective-permute-start(bf16[5,72,256]{2,1,0:T(8,128)(2,1)} %get-tuple-element.31), channel_id=1, source_target_pairs={{16,0},{32,16},{48,32},{64,48},{80,64},{96,80},{112,96},{128,112},... | collective-permute-start | bytes 552968 | tf_op jit(solution)/shard_map/ppermute | solution.py:604
  49.4 5.3 %collective-permute-start.4 = (bf16[72,384]{1,0:T(8,128)(2,1)}, bf16[72,384]{1,0:T(8,128)(2,1)S(1)}, u32[]{:S(2)}, u32[]{:S(2)}) collective-permute-start(bf16[72,384]{1,0:T(8,128)(2,1)} %get-tuple-element.32), channel_id=1, source_target_pairs={{32,0},{48,16},{64,32},{80,48},{96,64},{112,80},{128,96},{144,112}... | collective-permute-start | bytes 165896 | tf_op jit(solution)/shard_map/ppermute | solution.py:605
  54.6 0.6 copy-start.5
  54.6 0.7 %copy-start.1 = (bf16[5,72,256]{2,1,0:T(8,128)(2,1)}, bf16[5,72,256]{2,1,0:T(8,128)(2,1)S(1)}, u32[]{:S(2)}) copy-start(bf16[5,72,256]{2,1,0:T(8,128)(2,1)S(1)} %collective-permute-done.3.came_ref) | copy-start | bytes 552964

commit v4 on v3

--- a/solution.py
+++ b/solution.py
@@ -1,5 +1,3 @@
-import functools
-
 import jax
 import jax.numpy as jnp
 from jax import lax
@@ -17,9 +15,7 @@
 CELLS = TILE * TILE
 TAPS = 9
 SLOT = 80
-UNROLL = 4
 FR_DEV = 4
-STEPS = 2
 NTILES = 16
 TILE_AXES = ("tile_0", "tile_1", "tile_2")
 BF = jnp.bfloat16
@@ -27,6 +23,14 @@
 
 VMEM = pl.BlockSpec(memory_space=pltpu.VMEM)
 SMEM = pl.BlockSpec(memory_space=pltpu.SMEM)
+
+
+def near_core(array):
+    return pltpu.with_memory_space_constraint(array, pltpu.VMEM)
+
+
+def far_from_core(array):
+    return pltpu.with_memory_space_constraint(array, pltpu.HBM)
 
 
 def iota(shape, dim):
@@ -88,19 +92,26 @@
     return pl.pallas_call(
         weights_kernel,
         out_shape=(
-            jax.ShapeDtypeStruct((WIDTH, TAPS * ROWS), BF),
-            jax.ShapeDtypeStruct((WIDTH, ROWS), BF),
-            jax.ShapeDtypeStruct((3 * WIDTH, WIDTH), BF),
-            jax.ShapeDtypeStruct((WIDTH, WIDTH), BF),
-            jax.ShapeDtypeStruct((ROWS, WIDTH), BF),
+            pltpu.VMEM((WIDTH, TAPS * ROWS), BF),
+            pltpu.VMEM((WIDTH, ROWS), BF),
+            pltpu.VMEM((3 * WIDTH, WIDTH), BF),
+            pltpu.VMEM((WIDTH, WIDTH), BF),
+            pltpu.VMEM((ROWS, WIDTH), BF),
         ),
         in_specs=[VMEM] * 8 + [SMEM],
         out_specs=(VMEM,) * 5,
         scratch_shapes=[pltpu.VMEM((TAPS * ROWS, WIDTH), F32)],
+        compiler_params=pltpu.CompilerParams(vmem_limit_bytes=40 << 20),
         name="weights",
     )(
-        in_weight.T, embed.reshape(1, WIDTH), conv, gain.reshape(1, WIDTH), query, memory, attend,
-        decode, after,
+        *map(
+            far_from_core,
+            (
+                in_weight.T, embed.reshape(1, WIDTH), conv, gain.reshape(1, WIDTH), query, memory,
+                attend, decode,
+            ),
+        ),
+        after,
     )
 
 
@@ -120,7 +131,7 @@
 
 def border_kernel(
     near_ref, plan_ref, level_ref, queue_ref, fresh_ref,
-    frames_out, slots_out, after_out, full, folded, later, lines,
+    frames_out, front_out, slots_out, after_out, full, folded, later, lines,
 ):
     me = lax.axis_index(TILE_AXES)
     after_out[0] = 0
@@ -138,6 +149,7 @@
     frames = full[...].astype(BF)
     for f in range(FR_DEV):
         frames_out[f] = full[pl.ds(f * ROWS, ROWS), :].astype(BF)
+    front_out[...] = full[0:ROWS, :].astype(BF)
     cell = iota((CELLS, 128), 0)
     want = iota((CELLS, 128), 1)
     line = want // (2 * TILE)
@@ -190,17 +202,19 @@
         border_kernel,
         out_shape=(
             jax.ShapeDtypeStruct((FR_DEV, ROWS, CELLS), BF),
+            jax.ShapeDtypeStruct((ROWS, CELLS), BF),
             jax.ShapeDtypeStruct((NTILES, SLOT, 128), BF),
             jax.ShapeDtypeStruct((1,), jnp.int32),
         ),
         in_specs=[SMEM, SMEM, SMEM, VMEM, VMEM],
-        out_specs=(VMEM, VMEM, SMEM),
+        out_specs=(VMEM, VMEM, VMEM, SMEM),
         scratch_shapes=[
             pltpu.VMEM(((FR_DEV + 1) * ROWS, CELLS), F32),
             pltpu.VMEM((SLOT, 128), F32),
             pltpu.VMEM((ROWS, 128), F32),
             pltpu.VMEM((4, SLOT, 128), BF),
         ],
+        compiler_params=pltpu.CompilerParams(vmem_limit_bytes=40 << 20),
         name="border",
     )(near, plan, levels, queue, fresh)
 
@@ -227,7 +241,7 @@
     )
 
 
-def ring_kernel(near_ref, slots_ref, frames_ref, wait_ref, halo_out, later_out, far_out, picked, spare):
+def ring_kernel(near_ref, slots_ref, wait_ref, halo_out, front_out, later_out, picked, spare):
     me = lax.axis_index(TILE_AXES)
     north = near_ref[2, me]
     beside = jnp.maximum(north, near_ref[3, me])
@@ -267,8 +281,7 @@
     halos = mm(low[0:ROWS], pick)
     for f in range(FR_DEV):
         halo_out[f] = halos[:, f * 128 : (f + 1) * 128].astype(BF)
-    far_out[:, 0:CELLS] = frames_ref[0]
-    far_out[:, CELLS : CELLS + 128] = halos[:, 0:128].astype(BF)
+    front_out[...] = halos[:, 0:128].astype(BF)
     column = iota((8, 8 * 64), 1)
     spot = source(column % 64)[1] + TILE * (column // 64)
     pick = (iota((5 * 128, 8 * 64), 0) == spot[0:1]).astype(BF)
@@ -280,19 +293,20 @@
     later_out[...] = spare[...].astype(BF)
 
 
-def halo_cells(near, slots, frames, wait):
+def halo_cells(near, slots, wait):
     return pl.pallas_call(
         ring_kernel,
         out_shape=(
             jax.ShapeDtypeStruct((FR_DEV, ROWS, 128), BF),
             jax.ShapeDtypeStruct((ROWS, 128), BF),
-            jax.ShapeDtypeStruct((ROWS, CELLS + 128), BF),
+            jax.ShapeDtypeStruct((ROWS, 128), BF),
         ),
-        in_specs=[SMEM, VMEM, VMEM, pl.BlockSpec(memory_space=pl.ANY)],
+        in_specs=[SMEM, VMEM, pl.BlockSpec(memory_space=pl.ANY)],
         out_specs=(VMEM,) * 3,
         scratch_shapes=[pltpu.VMEM((SLOT, 5 * 128), F32), pltpu.VMEM((ROWS, 128), F32)],
+        compiler_params=pltpu.CompilerParams(vmem_limit_bytes=40 << 20),
         name="ring",
-    )(near, slots, frames, wait)
+    )(near, slots, wait)
 
 
 def with_log_rows(scaled, log_hi, log_lo, lanes):
@@ -306,23 +320,22 @@
     return jnp.concatenate([row] * (lanes // 128), axis=1)
 
 
-def denoise(
-    lanes, near_ref, plan_ref, level_ref, weights, states, sigmas, scaled, images, ring_windows,
-    hidden_all, qkv_all, context_all, finished,
-):
-    taps_ref, lift_ref, qkv_ref, attend_ref, decode_ref = weights
+def features_of(
+    frames, lanes, near_ref, taps_ref, lift_ref, states, sigmas, scaled, images, ring_windows
+):
     me = lax.axis_index(TILE_AXES)
-    is_last = lax.axis_index("noise") == lax.axis_size("noise") - 1
     at_north = near_ref[2, me] >= 0
     north_here = at_north.astype(F32)
     south_here = 1.0 - north_here
     extended = lanes > CELLS
-
-    for p in range(2 * FR_DEV):
+    count = len(frames)
+    begin = frames[0]
+    total = CELLS + 128
+
+    for p in frames:
         sigma = sigmas[p]
         log_hi, log_lo = split_hi_lo(jnp.log(sigma))
         scale = 1.0 / jnp.sqrt(sigma * sigma + 1.0)
-        total = CELLS + 128
         scaled[p] = with_log_rows(
             states[p] * wide(scale, total), wide(log_hi, total), wide(log_lo, total), total
         )
@@ -338,8 +351,8 @@
     from_side = jnp.where(cell_x == 0, cell_y, TILE + cell_y)
     spot = jnp.where(column < CELLS, from_side, from_line)
     spread = (ring_row == spot[0:1]).astype(BF)
-    low = scaled[...].reshape(2 * FR_DEV * ROWS, CELLS + 128).astype(BF)
-    images[...] = mm(low[:, CELLS:], spread).reshape(2 * FR_DEV, ROWS, 4 * CELLS)
+    low = scaled[begin : begin + count].reshape(count * ROWS, total).astype(BF)
+    images[begin : begin + count] = mm(low[:, CELLS:], spread).reshape(count, ROWS, 4 * CELLS)
     if extended:
         near_row = jnp.where(at_north, -1, TILE)
         far_row = jnp.where(at_north, -2, TILE + 1)
@@ -364,7 +377,7 @@
         )
         spot = jnp.where(cell < 50, spot, -1)
         pick = (iota((CELLS + 128, 5 * 128), 0) == spot[0:1]).astype(BF)
-        ring_windows[...] = mm(low, pick).reshape(2 * FR_DEV, ROWS, 5 * 128)
+        ring_windows[begin : begin + count] = mm(low, pick).reshape(count, ROWS, 5 * 128)
 
     across = iota((ROWS, CELLS), 1) % TILE
     down = iota((ROWS, CELLS), 1) // TILE
@@ -400,21 +413,47 @@
         power = jnp.mean(hidden * hidden, axis=0, keepdims=True)
         return hidden, (hidden * lax.rsqrt(power + 1e-06)).astype(BF)
 
-    def own(p, carry):
+    return features
+
+
+OWN = range(FR_DEV - 1)
+REST = range(FR_DEV - 1, 2 * FR_DEV)
+
+
+def own_frames(lanes, near_ref, weights, states, sigmas, scratch, hidden_out, qkv_out):
+    taps_ref, lift_ref, qkv_ref = weights
+    features = features_of(OWN, lanes, near_ref, taps_ref, lift_ref, states, sigmas, *scratch)
+    for p in OWN:
         hidden, normed = features(p)
-        hidden_all[p] = hidden
-        qkv_all[p] = mm(qkv_ref[...], normed).reshape(3 * HEAD, HEADS, lanes)
-        return carry
-
-    def following(p, carry):
-        _, normed = features(p)
-        qkv_all[p, HEAD : 3 * HEAD] = mm(qkv_ref[WIDTH : 3 * WIDTH, :], normed).reshape(
-            2 * HEAD, HEADS, lanes
-        )
-        return carry
-
-    lax.fori_loop(0, FR_DEV, own, 0, unroll=UNROLL)
-    lax.fori_loop(FR_DEV, 2 * FR_DEV, following, 0, unroll=UNROLL)
+        hidden_out[p] = hidden
+        qkv_out[p] = mm(qkv_ref[...], normed).reshape(3 * HEAD, HEADS, lanes)
+
+
+def denoise(
+    lanes, near_ref, plan_ref, level_ref, weights, states, sigmas, scratch,
+    hidden_own, qkv_own, hidden_all, qkv_all, context_all, arrived, finished,
+):
+    taps_ref, lift_ref, qkv_ref, attend_ref, decode_ref = weights
+    is_last = lax.axis_index("noise") == lax.axis_size("noise") - 1
+    held = len(OWN)
+    copies = (
+        pltpu.make_async_copy(qkv_own, qkv_all.at[pl.ds(0, held)], arrived.at[0]),
+        pltpu.make_async_copy(hidden_own, hidden_all.at[pl.ds(0, held)], arrived.at[1]),
+    )
+    for copy in copies:
+        copy.start()
+    features = features_of(REST, lanes, near_ref, taps_ref, lift_ref, states, sigmas, *scratch)
+    for p in REST:
+        hidden, normed = features(p)
+        if p < FR_DEV:
+            hidden_all[p] = hidden
+            qkv_all[p] = mm(qkv_ref[...], normed).reshape(3 * HEAD, HEADS, lanes)
+        else:
+            qkv_all[p, HEAD : 3 * HEAD] = mm(qkv_ref[WIDTH : 3 * WIDTH, :], normed).reshape(
+                2 * HEAD, HEADS, lanes
+            )
+    for copy in copies:
+        copy.wait()
 
     hide = jnp.where(is_last, -jnp.inf, 0.0)
     for part in range(lanes // 128):
@@ -455,10 +494,14 @@
         finished(p, state + slope * (state - denoised))
 
 
-def fill_sigmas(plan_ref, level_ref, next_frames_ref, sigmas):
+def own_sigmas(plan_ref, level_ref, sigmas):
+    for f in range(FR_DEV):
+        sigmas[f] = jnp.full((1, 128), plan_ref[level_ref[f]], F32)
+
+
+def next_sigmas(next_frames_ref, sigmas):
     for f in range(FR_DEV):
         came = next_frames_ref[f, 64:ROWS, 0:128].astype(F32)
-        sigmas[f] = jnp.full((1, 128), plan_ref[level_ref[f]], F32)
         sigmas[FR_DEV + f] = came[5:6] + came[6:7] + came[7:8]
 
 
@@ -472,21 +515,40 @@
             states[p] = states[p] * wide(sigmas[p], CELLS + 128)
 
 
-def first_kernel(
-    near_ref, plan_ref, level_ref, queue_ref, fresh_ref, halo_ref, later_ref, next_frames_ref,
-    next_halo_ref, far_ref, taps_ref, lift_ref, qkv_ref, attend_ref, decode_ref,
-    own_out, near_out, far_out,
-    states, sigmas, scaled, images, ring_windows, hidden_all, qkv_all, context_all, message,
-):
-    fill_sigmas(plan_ref, level_ref, next_frames_ref, sigmas)
-    for p in range(FR_DEV - 1):
+def first_own_states(queue_ref, halo_ref, states):
+    for p in OWN:
         states[p, 64:ROWS, 0:CELLS] = jnp.zeros((ROWS - 64, CELLS), F32)
         states[p, 0:FIELDS, 0:CELLS] = frame_rows(queue_ref, p + 1)
         states[p, :, CELLS:] = halo_ref[p + 1].astype(F32)
+
+
+def first_own_kernel(
+    near_ref, plan_ref, level_ref, queue_ref, halo_ref, taps_ref, lift_ref, qkv_ref,
+    hidden_out, qkv_out, states, sigmas, *scratch,
+):
+    own_sigmas(plan_ref, level_ref, sigmas)
+    first_own_states(queue_ref, halo_ref, states)
+    own_frames(
+        CELLS + 128, near_ref, (taps_ref, lift_ref, qkv_ref), states, sigmas, scratch,
+        hidden_out, qkv_out,
+    )
+
+
+def first_kernel(
+    near_ref, plan_ref, level_ref, queue_ref, fresh_ref, halo_ref, later_ref, next_frames_ref,
+    next_halo_ref, far_ref, far_halo_ref, hidden_own, qkv_own,
+    taps_ref, lift_ref, qkv_ref, attend_ref, decode_ref,
+    own_out, near_out, far_out,
+    states, sigmas, scaled, images, ring_windows, hidden_all, qkv_all, context_all, arrived, message,
+):
+    own_sigmas(plan_ref, level_ref, sigmas)
+    next_sigmas(next_frames_ref, sigmas)
+    first_own_states(queue_ref, halo_ref, states)
     for f in range(FR_DEV):
         states[FR_DEV - 1 + f, :, 0:CELLS] = next_frames_ref[f].astype(F32)
         states[FR_DEV - 1 + f, :, CELLS:] = next_halo_ref[f].astype(F32)
-    states[2 * FR_DEV - 1] = far_ref[...].astype(F32)
+    states[2 * FR_DEV - 1, :, 0:CELLS] = far_ref[...].astype(F32)
+    states[2 * FR_DEV - 1, :, CELLS:] = far_halo_ref[...].astype(F32)
     scale_entering(states, sigmas)
 
     def finished(p, moved):
@@ -500,7 +562,8 @@
     denoise(
         CELLS + 128, near_ref, plan_ref, level_ref,
         (taps_ref, lift_ref, qkv_ref, attend_ref, decode_ref),
-        states, sigmas, scaled, images, ring_windows, hidden_all, qkv_all, context_all, finished,
+        states, sigmas, (scaled, images, ring_windows), hidden_own, qkv_own,
+        hidden_all, qkv_all, context_all, arrived, finished,
     )
 
     @pl.when(lax.axis_index("noise") == 0)
@@ -520,14 +583,31 @@
     far_out[...] = message[0].astype(BF)
 
 
+def second_own_states(own_ref, states):
+    for p in OWN:
+        states[p] = own_ref[p + 1]
+
+
+def second_own_kernel(
+    near_ref, plan_ref, level_ref, own_ref, taps_ref, lift_ref, qkv_ref,
+    hidden_out, qkv_out, states, sigmas, *scratch,
+):
+    own_sigmas(plan_ref, level_ref, sigmas)
+    second_own_states(own_ref, states)
+    own_frames(
+        CELLS, near_ref, (taps_ref, lift_ref, qkv_ref), states, sigmas, (*scratch, None),
+        hidden_out, qkv_out,
+    )
+
+
 def second_kernel(
-    near_ref, plan_ref, level_ref, own_ref, came_ref, far_ref,
+    near_ref, plan_ref, level_ref, own_ref, came_ref, far_ref, hidden_own, qkv_own,
     taps_ref, lift_ref, qkv_ref, attend_ref, decode_ref,
-    out_ref, states, sigmas, scaled, images, hidden_all, qkv_all, context_all,
-):
-    fill_sigmas(plan_ref, level_ref, came_ref, sigmas)
-    for p in range(FR_DEV - 1):
-        states[p] = own_ref[p + 1]
+    out_ref, states, sigmas, scaled, images, hidden_all, qkv_all, context_all, arrived,
+):
+    own_sigmas(plan_ref, level_ref, sigmas)
+    next_sigmas(came_ref, sigmas)
+    second_own_states(own_ref, states)
     for f in range(FR_DEV):
         states[FR_DEV - 1 + f, :, 0:CELLS] = came_ref[f].astype(F32)
         pair = came_ref[FR_DEV, :, (f // 2) * 128 : (f // 2 + 1) * 128].astype(F32)
@@ -544,22 +624,44 @@
     denoise(
         CELLS, near_ref, plan_ref, level_ref,
         (taps_ref, lift_ref, qkv_ref, attend_ref, decode_ref),
-        states, sigmas, scaled, images, None, hidden_all, qkv_all, context_all, finished,
-    )
-
-
-def common_scratch(lanes):
-    frames = 2 * FR_DEV
-    return [
+        states, sigmas, (scaled, images, None), hidden_own, qkv_own,
+        hidden_all, qkv_all, context_all, arrived, finished,
+    )
+
+
+def window_scratch(lanes, frames):
+    found = [
         pltpu.VMEM((frames, ROWS, CELLS + 128), F32),
         pltpu.VMEM((frames, 1, 128), F32),
         pltpu.VMEM((frames, ROWS, CELLS + 128), F32),
         pltpu.VMEM((frames, ROWS, 4 * CELLS), F32),
-    ], [
+    ]
+    if lanes > CELLS:
+        found.append(pltpu.VMEM((frames, ROWS, 5 * 128), F32))
+    return found
+
+
+def attention_scratch(lanes):
+    return [
         pltpu.VMEM((FR_DEV, WIDTH, lanes), F32),
-        pltpu.VMEM((frames, 3 * HEAD, HEADS, lanes), F32),
+        pltpu.VMEM((2 * FR_DEV, 3 * HEAD, HEADS, lanes), F32),
         pltpu.VMEM((FR_DEV, HEAD, HEADS, lanes), F32),
+        pltpu.SemaphoreType.DMA((2,)),
     ]
+
+
+def own_call(kernel, lanes, *operands):
+    return pl.pallas_call(
+        kernel,
+        out_shape=(
+            pltpu.VMEM((len(OWN), WIDTH, lanes), F32),
+            pltpu.VMEM((len(OWN), 3 * HEAD, HEADS, lanes), F32),
+        ),
+        in_specs=[SMEM] * 3 + [VMEM] * (len(operands) - 3),
+        out_specs=(VMEM, VMEM),
+        scratch_shapes=window_scratch(lanes, FR_DEV),
+        compiler_params=pltpu.CompilerParams(vmem_limit_bytes=40 << 20),
+    )(*operands)
 
 
 def shards(
@@ -569,49 +671,58 @@
     groups = lax.axis_size("noise")
     from_next = [((i + 1) % groups, i) for i in range(groups)]
     from_second = [((i + 2) % groups, i) for i in range(groups)]
-    near = neighbours.T
-    queue = queue_state.reshape(FR_DEV * FIELDS * 2, 128)
-    frames, slots, after = border_lines(near, plan, levels, queue, fresh_noise)
-    next_frames = lax.ppermute(frames, "noise", from_next)
-    slots = lax.all_to_all(slots, TILE_AXES, split_axis=0, concat_axis=0, tiled=True)
+    near = far_from_core(neighbours.T)
+    plan = far_from_core(plan)
+    levels = far_from_core(levels)
+    fresh_noise = far_from_core(fresh_noise)
+    queue = far_from_core(queue_state.reshape(FR_DEV * FIELDS * 2, 128))
+    frames, front, slots, after = border_lines(near, plan, levels, queue, fresh_noise)
+    next_frames = near_core(lax.ppermute(frames, "noise", from_next))
+    slots = near_core(lax.all_to_all(slots, TILE_AXES, split_axis=0, concat_axis=0, tiled=True))
+    far = lax.ppermute(front, "noise", from_second)
     weights = prepare_weights(
         in_weight, level_embed, conv_weight, norm_gain, query_weight, memory_weight,
         attend_out, decode_weight, after,
     )
-    halos, later, far = halo_cells(near, slots, frames, weights[1])
-    next_halos = lax.ppermute(halos, "noise", from_next)
-    far = lax.ppermute(far, "noise", from_second)
-    before, after_features = common_scratch(CELLS + 128)
+    far = near_core(far)
+    halos, front_halo, later = halo_cells(near, slots, weights[1])
+    next_halos = near_core(lax.ppermute(halos, "noise", from_next))
+    far_halo = near_core(lax.ppermute(front_halo, "noise", from_second))
+    both = (pl.BlockSpec(memory_space=pl.ANY),) * 2
+    lanes = CELLS + 128
+    own_part = own_call(first_own_kernel, lanes, near, plan, levels, queue, halos, *weights[:3])
     own, near_message, far_message = pl.pallas_call(
         first_kernel,
         out_shape=(
-            jax.ShapeDtypeStruct((FR_DEV, ROWS, CELLS + 128), F32),
+            jax.ShapeDtypeStruct((FR_DEV, ROWS, lanes), F32),
             jax.ShapeDtypeStruct((FR_DEV + 1, ROWS, CELLS), BF),
-            jax.ShapeDtypeStruct((ROWS, CELLS + 128), BF),
+            jax.ShapeDtypeStruct((ROWS, lanes), BF),
         ),
-        in_specs=[SMEM] * 3 + [VMEM] * 12,
+        in_specs=[*([SMEM] * 3 + [VMEM] * 8), *both, *([VMEM] * 5)],
         out_specs=(VMEM,) * 3,
         scratch_shapes=[
-            *before,
-            pltpu.VMEM((2 * FR_DEV, ROWS, 5 * 128), F32),
-            *after_features,
-            pltpu.VMEM((FR_DEV, ROWS, CELLS + 128), F32),
+            *window_scratch(lanes, 2 * FR_DEV),
+            *attention_scratch(lanes),
+            pltpu.VMEM((FR_DEV, ROWS, lanes), F32),
         ],
+        compiler_params=pltpu.CompilerParams(vmem_limit_bytes=40 << 20),
         name="first",
     )(
-        near, plan, levels, queue, fresh_noise, halos, later, next_frames, next_halos, far, *weights
-    )
-    came = lax.ppermute(near_message, "noise", from_next)
-    far = lax.ppermute(far_message, "noise", from_second)
-    before, after_features = common_scratch(CELLS)
+        near, plan, levels, queue, fresh_noise, halos, later, next_frames, next_halos, far,
+        far_halo, *own_part, *weights,
+    )
+    came = near_core(lax.ppermute(near_message, "noise", from_next))
+    far = near_core(lax.ppermute(far_message, "noise", from_second))
+    own_part = own_call(second_own_kernel, CELLS, near, plan, levels, own, *weights[:3])
     moved = pl.pallas_call(
         second_kernel,
         out_shape=jax.ShapeDtypeStruct((FR_DEV * FIELDS * 2, 128), F32),
-        in_specs=[SMEM] * 3 + [VMEM] * 8,
+        in_specs=[*([SMEM] * 3 + [VMEM] * 3), *both, *([VMEM] * 5)],
         out_specs=VMEM,
-        scratch_shapes=[*before, *after_features],
+        scratch_shapes=[*window_scratch(CELLS, 2 * FR_DEV), *attention_scratch(CELLS)],
+        compiler_params=pltpu.CompilerParams(vmem_limit_bytes=40 << 20),
         name="second",
-    )(near, plan, levels, own, came, far, *weights)
+    )(near, plan, levels, own, came, far, *own_part, *weights)
     return moved.reshape(queue_state.shape)
 
 

time: 64.4 us -> 58 us (0.901)
  waiting for transfers between devices: 8.75 us -> 3.45 us
  local copies, waits for them, and re-layouts: 2.06 us -> 0 us
  starting transfers between devices: 24.8 us -> 25.7 us
    ppermute x5 -> x6, waiting for transfers between devices: 8.75 us -> 2.97 us  [the longest x1 1.97 us: shards(): far = near_core(lax.ppermute(far_message, 'noise', from_second))]
    pallas_call x1 -> x3, Pallas kernels: 3.58 us -> 8.91 us  [the longest x2 6.12 us: own_call(): pl.pallas_call(kernel, out_shape=(pltpu.VMEM((len(OWN), WIDTH, lanes), F3...]
    pallas_call x1, Pallas kernels: 11.7 us -> 9.06 us  [shards(): pl.pallas_call(first_kernel, out_shape=(jax.ShapeDtypeStruct((FR_DEV, ROW...]
    pallas_call x1, Pallas kernels: 8.75 us -> 6.65 us  [shards(): pl.pallas_call(second_kernel, out_shape=jax.ShapeDtypeStruct((FR_DEV * FI...]
    unnamed x12 -> x0, local copies, waits for them, and re-layouts: 2.06 us -> none
    pallas_call x1, Pallas kernels: 2.11 us -> 1.16 us  [halo_cells(): pl.pallas_call(ring_kernel, out_shape=(jax.ShapeDtypeStruct((FR_DEV, ROWS...]
    ppermute x5 -> x6, starting transfers between devices: 18.7 us -> 19.5 us  [the longest x1 8.24 us: shards(): next_halos = near_core(lax.ppermute(halos, 'noise', from_next))]
  transfers between devices with their start and end apart: 6 -> 7, of which waited for: 2 -> 4; matrix products, arithmetic and copies ran while one was open for 0% -> 0% of each run, Pallas kernels for 9% -> 18%
where the time goes in v4:
time: 58 us; the launch traced here: 57.4 us
  Pallas kernels  28 us (48%)
  starting transfers between devices  25.7 us (44%)
  waiting for transfers between devices  3.45 us (6%)
    pallas_call x1, Pallas kernels, shards(): pl.pallas_call(first_kernel, out_shape=(jax.ShapeDtypeStruct((FR_DEV, ROW...  9.06 us
    ppermute x1, starting transfers between devices, shards(): next_halos = near_core(lax.ppermute(halos, 'noise', from_next))  8.24 us
    ppermute x1, starting transfers between devices, shards(): next_frames = near_core(lax.ppermute(frames, 'noise', from_next))  6.72 us
    pallas_call x1, Pallas kernels, shards(): pl.pallas_call(second_kernel, out_shape=jax.ShapeDtypeStruct((FR_DEV * FI...  6.65 us
    all_to_all x1, starting transfers between devices, shards(): lax.all_to_all(slots, TILE_AXES, split_axis=0, concat_axis=0, tiled=True)  6.14 us
    pallas_call x2, Pallas kernels, own_call(): pl.pallas_call(kernel, out_shape=(pltpu.VMEM((len(OWN), WIDTH, lanes), F3...  6.12 us
    pallas_call x1, Pallas kernels, prepare_weights(): pl.pallas_call(weights_kernel, out_shape=(pltpu.VMEM((WIDTH, TAPS * ROWS)...  2.8 us
    ppermute x1, starting transfers between devices, shards(): came = near_core(lax.ppermute(near_message, 'noise', from_next))  2.73 us
  transfers between devices with their start and end apart: 7, of which 4 were waited for; matrix products, arithmetic and copies ran while one was open for 0% of the time, Pallas kernels for 18%

profile of v4, /device:TPU:8, one launch (start us, length us, event | category | flops | bytes accessed | tf_op | source)
XLA Modules:
  0.0 57.4 jit_solution(9495628632581181287)
XLA Ops:
  0.0 2.3 %border.1 = (bf16[4,72,256]{2,1,0:T(8,128)(2,1)S(1)}, bf16[72,256]{1,0:T(8,128)(2,1)S(1)}, bf16[16,80,128]{2,1,0:T(8,128)(2,1)}, s32[1]{0:T(128)}) custom-call(s32[4,16]{1,0:T(4,128)} %bitcast.9, f32[17]{0:T(128)} %plan_ref.9, s32[4]{0:T(128)} %level_ref.9, f32[552,128]{1,0:T(8,128)} %bitcast.6, f32[2,69,1,256]{3,2,1,0:T(1,128)} %fresh_ref.3), custom_call_target="tpu_custom_call" | custom-call | tf_op jit(solution)/shard_map/border/pallas_call | solution.py:201
  2.3 6.1 %all-to-all-start = ((bf16[16,80,128]{2,1,0:T(8,128)(2,1)}), bf16[16,80,128]{2,1,0:T(8,128)(2,1)S(1)}, u32[]{:S(2)}, u32[]{:S(2)}) async-start(bf16[16,80,128]{2,1,0:T(8,128)(2,1)} %get-tuple-element.24), calls=%async_computation | async-start | bytes 655360 | tf_op jit(solution)/shard_map/all_to_all | solution.py:681
  8.4 6.7 %collective-permute-start = (bf16[4,72,256]{2,1,0:T(8,128)(2,1)S(1)}, bf16[4,72,256]{2,1,0:T(8,128)(2,1)S(1)}, u32[]{:S(2)}, u32[]{:S(2)}) collective-permute-start(bf16[4,72,256]{2,1,0:T(8,128)(2,1)S(1)} %get-tuple-element.29), channel_id=1, source_target_pairs={{16,0},{32,16},{48,32},{64,48},{80,64},{96,80},{112,96},{128,112},... | collective-permute-start | bytes 442376 | tf_op jit(solution)/shard_map/ppermute | solution.py:680
  15.1 2.8 %weights.1 = (bf16[256,648]{1,0:T(8,128)(2,1)S(1)}, bf16[256,72]{1,0:T(8,128)(2,1)S(1)}, bf16[768,256]{1,0:T(8,128)(2,1)S(1)}, bf16[256,256]{1,0:T(8,128)(2,1)S(1)}, bf16[72,256]{1,0:T(8,128)(2,1)S(1)}) custom-call(bf16[69,256]{1,0:T(8,128)(2,1)} %bitcast.15, f32[1,256]{1,0:T(1,128)} %bitcast.16, bf16[9,256,256]{2,1,0:T(8,128)(2,1)} %conv_ref.1, ...), custom_call_target="tpu_custom_call" | custom-call | tf_op jit(solution)/shard_map/weights/pallas_call | solution.py:92
  17.9 0.5 all-to-all-done.slots_ref
  18.4 1.2 %ring.1 = (bf16[4,72,128]{2,1,0:T(8,128)(2,1)S(1)}, bf16[72,128]{1,0:T(8,128)(2,1)S(1)}, bf16[72,128]{1,0:T(8,128)(2,1)S(1)}) custom-call(s32[4,16]{1,0:T(4,128)} %bitcast.10, bf16[16,80,128]{2,1,0:T(8,128)(2,1)S(1)} %all-to-all-done.slots_ref, bf16[256,72]{1,0:T(8,128)(2,1)S(1)} %get-tuple-element.26.wait_ref.lift_ref), custom_call_target="tpu_custom_call" | custom-call | tf_op jit(solution)/shard_map/ring/pallas_call | solution.py:297
  19.6 8.2 %collective-permute-start.1 = (bf16[4,72,128]{2,1,0:T(8,128)(2,1)S(1)}, bf16[4,72,128]{2,1,0:T(8,128)(2,1)S(1)}, u32[]{:S(2)}, u32[]{:S(2)}) collective-permute-start(bf16[4,72,128]{2,1,0:T(8,128)(2,1)S(1)} %get-tuple-element.27.halo_ref), channel_id=1, source_target_pairs={{16,0},{32,16},{48,32},{64,48},{80,64},{96,80},{112,96},{128,112},... | collective-permute-start | bytes 221192 | tf_op jit(solution)/shard_map/ppermute | solution.py:689
  27.8 0.0 collective-permute-start.2
  27.8 0.5 collective-permute-start.3
  28.3 3.6 %shard_map.127 = (f32[3,256,384]{2,1,0:T(8,128)S(1)}, f32[3,96,8,384]{3,2,1,0:T(8,128)S(1)}) custom-call(s32[4,16]{1,0:T(4,128)} %bitcast.11, f32[17]{0:T(128)} %plan_ref.9, s32[4]{0:T(128)} %level_ref.9, f32[552,128]{1,0:T(8,128)} %bitcast.7, bf16[4,72,128]{2,1,0:T(8,128)(2,1)S(1)} %get-tuple-element.27.halo_ref, ...), custom_call_target="tpu_custom_call" | custom-call | tf_op jit(solution)/shard_map/pallas_call | solution.py:654
  31.9 0.8 %collective-permute-done.2.far_ref = bf16[72,256]{1,0:T(8,128)(2,1)S(1)} collective-permute-done((bf16[72,256]{1,0:T(8,128)(2,1)S(1)}, bf16[72,256]{1,0:T(8,128)(2,1)S(1)}, u32[]{:S(2)}, u32[]{:S(2)}) %collective-permute-start.2) | collective-permute-done | bytes 36896 | tf_op jit(solution)/shard_map/ppermute | solution.py:682
  32.7 0.0 collective-permute-done.next_frames_ref
  32.7 0.2 collective-permute-done.3.far_halo_ref
  32.9 0.0 collective-permute-done.1.next_halo_ref
  32.9 9.1 %first.1 = (f32[4,72,384]{2,1,0:T(8,128)S(1)}, bf16[5,72,256]{2,1,0:T(8,128)(2,1)S(1)}, bf16[72,384]{1,0:T(8,128)(2,1)S(1)}) custom-call(s32[4,16]{1,0:T(4,128)} %bitcast.12, f32[17]{0:T(128)} %plan_ref.9, s32[4]{0:T(128)} %level_ref.9, f32[552,128]{1,0:T(8,128)} %bitcast.8, f32[2,69,1,256]{3,2,1,0:T(1,128)} %fresh_ref.3, ...), custom_call_target="tpu_custom_call" | custom-call | tf_op jit(solution)/shard_map/first/pallas_call | solution.py:694
  41.9 2.7 %collective-permute-start.4 = (bf16[5,72,256]{2,1,0:T(8,128)(2,1)S(1)}, bf16[5,72,256]{2,1,0:T(8,128)(2,1)S(1)}, u32[]{:S(2)}, u32[]{:S(2)}) collective-permute-start(bf16[5,72,256]{2,1,0:T(8,128)(2,1)S(1)} %get-tuple-element.39), channel_id=1, source_target_pairs={{16,0},{32,16},{48,32},{64,48},{80,64},{96,80},{112,96},{128,112},... | collective-permute-start | bytes 552968 | tf_op jit(solution)/shard_map/ppermute | solution.py:714
  44.7 1.4 %collective-permute-start.5 = (bf16[72,384]{1,0:T(8,128)(2,1)S(1)}, bf16[72,384]{1,0:T(8,128)(2,1)S(1)}, u32[]{:S(2)}, u32[]{:S(2)}) collective-permute-start(bf16[72,384]{1,0:T(8,128)(2,1)S(1)} %get-tuple-element.40), channel_id=1, source_target_pairs={{32,0},{48,16},{64,32},{80,48},{96,64},{112,80},{128,96},{144,112}... | collective-permute-start | bytes 165896 | tf_op jit(solution)/shard_map/ppermute | solution.py:715
  46.0 2.5 %shard_map.128 = (f32[3,256,256]{2,1,0:T(8,128)S(1)}, f32[3,96,8,256]{3,2,1,0:T(8,128)S(1)}) custom-call(s32[4,16]{1,0:T(4,128)} %bitcast.13, f32[17]{0:T(128)} %plan_ref.9, s32[4]{0:T(128)} %level_ref.9, f32[4,72,384]{2,1,0:T(8,128)S(1)} %get-tuple-element.38.own_ref, bf16[256,648]{1,0:T(8,128)(2,1)S(1)} %get-tuple-element.32.taps_ref, ...), custom_call_target="tpu_custom_call" | custom-call | tf_op jit(solution)/shard_map/pallas_call | solution.py:654
  48.6 2.0 %collective-permute-done.5.far_ref = bf16[72,384]{1,0:T(8,128)(2,1)S(1)} collective-permute-done((bf16[72,384]{1,0:T(8,128)(2,1)S(1)}, bf16[72,384]{1,0:T(8,128)(2,1)S(1)}, u32[]{:S(2)}, u32[]{:S(2)}) %collective-permute-start.5) | collective-permute-done | bytes 55328 | tf_op jit(solution)/shard_map/ppermute | solution.py:715
  50.6 0.0 collective-permute-done.4.came_ref
  50.6 6.7 %second.1 = f32[552,128]{1,0:T(8,128)} custom-call(s32[4,16]{1,0:T(4,128)} %bitcast.14, f32[17]{0:T(128)} %plan_ref.9, s32[4]{0:T(128)} %level_ref.9, f32[4,72,384]{2,1,0:T(8,128)S(1)} %get-tuple-element.38.own_ref, bf16[5,72,256]{2,1,0:T(8,128)(2,1)S(1)} %collective-permute-done.4.came_ref, bf16[72,384]{1,0:T(8,128)(2,1)S(1)} %collective-permute-done.5.far_ref, ...), custom_call_target="tpu_custom_call" | custom-call | tf_op jit(solution)/shard_map/second/pallas_call | solution.py:717
Async XLA Ops:
  2.3 16.2 %all-to-all-start = ((bf16[16,80,128]{2,1,0:T(8,128)(2,1)}), bf16[16,80,128]{2,1,0:T(8,128)(2,1)S(1)}, u32[]{:S(2)}, u32[]{:S(2)}) async-start(bf16[16,80,128]{2,1,0:T(8,128)(2,1)} %get-tuple-element.24), calls=%async_computation | async-start | bytes 655360 | tf_op jit(solution)/shard_map/all_to_all | solution.py:681
  8.4 24.3 %collective-permute-start = (bf16[4,72,256]{2,1,0:T(8,128)(2,1)S(1)}, bf16[4,72,256]{2,1,0:T(8,128)(2,1)S(1)}, u32[]{:S(2)}, u32[]{:S(2)}) collective-permute-start(bf16[4,72,256]{2,1,0:T(8,128)(2,1)S(1)} %get-tuple-element.29), channel_id=1, source_target_pairs={{16,0},{32,16},{48,32},{64,48},{80,64},{96,80},{112,96},{128,112},... | collective-permute-start | bytes 442376 | tf_op jit(solution)/shard_map/ppermute | solution.py:680
  19.6 13.3 %collective-permute-start.1 = (bf16[4,72,128]{2,1,0:T(8,128)(2,1)S(1)}, bf16[4,72,128]{2,1,0:T(8,128)(2,1)S(1)}, u32[]{:S(2)}, u32[]{:S(2)}) collective-permute-start(bf16[4,72,128]{2,1,0:T(8,128)(2,1)S(1)} %get-tuple-element.27.halo_ref), channel_id=1, source_target_pairs={{16,0},{32,16},{48,32},{64,48},{80,64},{96,80},{112,96},{128,112},... | collective-permute-start | bytes 221192 | tf_op jit(solution)/shard_map/ppermute | solution.py:689
  27.8 4.9 %collective-permute-start.2 = (bf16[72,256]{1,0:T(8,128)(2,1)S(1)}, bf16[72,256]{1,0:T(8,128)(2,1)S(1)}, u32[]{:S(2)}, u32[]{:S(2)}) collective-permute-start(bf16[72,256]{1,0:T(8,128)(2,1)S(1)} %get-tuple-element.30), channel_id=1, source_target_pairs={{32,0},{48,16},{64,32},{80,48},{96,64},{112,80},{128,96},{144,112}... | collective-permute-start | bytes 110600 | tf_op jit(solution)/shard_map/ppermute | solution.py:682
  27.8 5.1 %collective-permute-start.3 = (bf16[72,128]{1,0:T(8,128)(2,1)S(1)}, bf16[72,128]{1,0:T(8,128)(2,1)S(1)}, u32[]{:S(2)}, u32[]{:S(2)}) collective-permute-start(bf16[72,128]{1,0:T(8,128)(2,1)S(1)} %get-tuple-element.31), channel_id=1, source_target_pairs={{32,0},{48,16},{64,32},{80,48},{96,64},{112,80},{128,96},{144,112}... | collective-permute-start | bytes 55304 | tf_op jit(solution)/shard_map/ppermute | solution.py:690
  41.9 8.6 %collective-permute-start.4 = (bf16[5,72,256]{2,1,0:T(8,128)(2,1)S(1)}, bf16[5,72,256]{2,1,0:T(8,128)(2,1)S(1)}, u32[]{:S(2)}, u32[]{:S(2)}) collective-permute-start(bf16[5,72,256]{2,1,0:T(8,128)(2,1)S(1)} %get-tuple-element.39), channel_id=1, source_target_pairs={{16,0},{32,16},{48,32},{64,48},{80,64},{96,80},{112,96},{128,112},... | collective-permute-start | bytes 552968 | tf_op jit(solution)/shard_map/ppermute | solution.py:714
  44.7 5.9 %collective-permute-start.5 = (bf16[72,384]{1,0:T(8,128)(2,1)S(1)}, bf16[72,384]{1,0:T(8,128)(2,1)S(1)}, u32[]{:S(2)}, u32[]{:S(2)}) collective-permute-start(bf16[72,384]{1,0:T(8,128)(2,1)S(1)} %get-tuple-element.40), channel_id=1, source_target_pairs={{32,0},{48,16},{64,32},{80,48},{96,64},{112,80},{128,96},{144,112}... | collective-permute-start | bytes 165896 | tf_op jit(solution)/shard_map/ppermute | solution.py:715

commit v5 on v4

--- a/solution.py
+++ b/solution.py
@@ -459,12 +459,17 @@
     for part in range(lanes // 128):
         at = slice(part * 128, part * 128 + 128)
 
-        def score(d, sums):
-            keys = qkv_all[:, HEAD + d, :, at]
-            return tuple(sums[i] + qkv_all[i, d, :, at][None] * keys for i in range(FR_DEV))
-
         zero = jnp.zeros((2 * FR_DEV, HEADS, 128), F32)
-        sums = lax.fori_loop(0, HEAD, score, (zero,) * FR_DEV, unroll=4)
+        sums = []
+        for pair in range(0, FR_DEV, 2):
+
+            def score(d, so_far, pair=pair):
+                keys = qkv_all[:, HEAD + d, :, at]
+                return tuple(
+                    so_far[i] + qkv_all[pair + i, d, :, at][None] * keys for i in range(2)
+                )
+
+            sums.extend(lax.fori_loop(0, HEAD, score, (zero,) * 2, unroll=HEAD))
         second_half = iota((2 * FR_DEV, HEADS, 128), 0) >= FR_DEV
         weights = []
         for i in range(FR_DEV):
@@ -479,7 +484,7 @@
                 context_all[i, d, :, at] = jnp.sum(weights[i] * values, axis=0)
             return carry
 
-        lax.fori_loop(0, HEAD, combine, 0, unroll=4)
+        lax.fori_loop(0, HEAD, combine, 0, unroll=HEAD)
 
     for p in range(FR_DEV):
         context = context_all[p].reshape(WIDTH, lanes).astype(BF)

time: 58 us -> 56.7 us (0.978)
  Pallas kernels: 28 us -> 26.7 us
    pallas_call x1, Pallas kernels: 9.06 us -> 8.21 us  [shards(): pl.pallas_call(first_kernel, out_shape=(jax.ShapeDtypeStruct((FR_DEV, ROW...]
where the time goes in v5:
time: 56.7 us; the launch traced here: 56.1 us
  Pallas kernels  26.7 us (47%)
  starting transfers between devices  25.7 us (45%)
  waiting for transfers between devices  3.45 us (6%)
    ppermute x1, starting transfers between devices, shards(): next_halos = near_core(lax.ppermute(halos, 'noise', from_next))  8.24 us
    pallas_call x1, Pallas kernels, shards(): pl.pallas_call(first_kernel, out_shape=(jax.ShapeDtypeStruct((FR_DEV, ROW...  8.21 us
    ppermute x1, starting transfers between devices, shards(): next_frames = near_core(lax.ppermute(frames, 'noise', from_next))  6.72 us
    pallas_call x1, Pallas kernels, shards(): pl.pallas_call(second_kernel, out_shape=jax.ShapeDtypeStruct((FR_DEV * FI...  6.19 us
    all_to_all x1, starting transfers between devices, shards(): lax.all_to_all(slots, TILE_AXES, split_axis=0, concat_axis=0, tiled=True)  6.14 us
    pallas_call x2, Pallas kernels, own_call(): pl.pallas_call(kernel, out_shape=(pltpu.VMEM((len(OWN), WIDTH, lanes), F3...  6.11 us
    pallas_call x1, Pallas kernels, prepare_weights(): pl.pallas_call(weights_kernel, out_shape=(pltpu.VMEM((WIDTH, TAPS * ROWS)...  2.8 us
    ppermute x1, starting transfers between devices, shards(): came = near_core(lax.ppermute(near_message, 'noise', from_next))  2.74 us
  transfers between devices with their start and end apart: 7, of which 4 were waited for; matrix products, arithmetic and copies ran while one was open for 0% of the time, Pallas kernels for 18%

profile of v5, /device:TPU:8, one launch (start us, length us, event | category | flops | bytes accessed | tf_op | source)
XLA Modules:
  0.0 56.1 jit_solution(8465994264045651004)
XLA Ops:
  0.0 2.3 %border.1 = (bf16[4,72,256]{2,1,0:T(8,128)(2,1)S(1)}, bf16[72,256]{1,0:T(8,128)(2,1)S(1)}, bf16[16,80,128]{2,1,0:T(8,128)(2,1)}, s32[1]{0:T(128)}) custom-call(s32[4,16]{1,0:T(4,128)} %bitcast.9, f32[17]{0:T(128)} %plan_ref.9, s32[4]{0:T(128)} %level_ref.9, f32[552,128]{1,0:T(8,128)} %bitcast.6, f32[2,69,1,256]{3,2,1,0:T(1,128)} %fresh_ref.3), custom_call_target="tpu_custom_call" | custom-call | tf_op jit(solution)/shard_map/border/pallas_call | solution.py:201
  2.3 6.1 %all-to-all-start = ((bf16[16,80,128]{2,1,0:T(8,128)(2,1)}), bf16[16,80,128]{2,1,0:T(8,128)(2,1)S(1)}, u32[]{:S(2)}, u32[]{:S(2)}) async-start(bf16[16,80,128]{2,1,0:T(8,128)(2,1)} %get-tuple-element.24), calls=%async_computation | async-start | bytes 655360 | tf_op jit(solution)/shard_map/all_to_all | solution.py:686
  8.4 6.7 %collective-permute-start = (bf16[4,72,256]{2,1,0:T(8,128)(2,1)S(1)}, bf16[4,72,256]{2,1,0:T(8,128)(2,1)S(1)}, u32[]{:S(2)}, u32[]{:S(2)}) collective-permute-start(bf16[4,72,256]{2,1,0:T(8,128)(2,1)S(1)} %get-tuple-element.29), channel_id=1, source_target_pairs={{16,0},{32,16},{48,32},{64,48},{80,64},{96,80},{112,96},{128,112},... | collective-permute-start | bytes 442376 | tf_op jit(solution)/shard_map/ppermute | solution.py:685
  15.1 2.8 %weights.1 = (bf16[256,648]{1,0:T(8,128)(2,1)S(1)}, bf16[256,72]{1,0:T(8,128)(2,1)S(1)}, bf16[768,256]{1,0:T(8,128)(2,1)S(1)}, bf16[256,256]{1,0:T(8,128)(2,1)S(1)}, bf16[72,256]{1,0:T(8,128)(2,1)S(1)}) custom-call(bf16[69,256]{1,0:T(8,128)(2,1)} %bitcast.15, f32[1,256]{1,0:T(1,128)} %bitcast.16, bf16[9,256,256]{2,1,0:T(8,128)(2,1)} %conv_ref.1, ...), custom_call_target="tpu_custom_call" | custom-call | tf_op jit(solution)/shard_map/weights/pallas_call | solution.py:92
  17.9 0.5 all-to-all-done.slots_ref
  18.4 1.2 %ring.1 = (bf16[4,72,128]{2,1,0:T(8,128)(2,1)S(1)}, bf16[72,128]{1,0:T(8,128)(2,1)S(1)}, bf16[72,128]{1,0:T(8,128)(2,1)S(1)}) custom-call(s32[4,16]{1,0:T(4,128)} %bitcast.10, bf16[16,80,128]{2,1,0:T(8,128)(2,1)S(1)} %all-to-all-done.slots_ref, bf16[256,72]{1,0:T(8,128)(2,1)S(1)} %get-tuple-element.26.wait_ref.lift_ref), custom_call_target="tpu_custom_call" | custom-call | tf_op jit(solution)/shard_map/ring/pallas_call | solution.py:297
  19.6 8.2 %collective-permute-start.1 = (bf16[4,72,128]{2,1,0:T(8,128)(2,1)S(1)}, bf16[4,72,128]{2,1,0:T(8,128)(2,1)S(1)}, u32[]{:S(2)}, u32[]{:S(2)}) collective-permute-start(bf16[4,72,128]{2,1,0:T(8,128)(2,1)S(1)} %get-tuple-element.27.halo_ref), channel_id=1, source_target_pairs={{16,0},{32,16},{48,32},{64,48},{80,64},{96,80},{112,96},{128,112},... | collective-permute-start | bytes 221192 | tf_op jit(solution)/shard_map/ppermute | solution.py:694
  27.8 0.0 collective-permute-start.2
  27.8 0.5 collective-permute-start.3
  28.3 3.6 %shard_map.127 = (f32[3,256,384]{2,1,0:T(8,128)S(1)}, f32[3,96,8,384]{3,2,1,0:T(8,128)S(1)}) custom-call(s32[4,16]{1,0:T(4,128)} %bitcast.11, f32[17]{0:T(128)} %plan_ref.9, s32[4]{0:T(128)} %level_ref.9, f32[552,128]{1,0:T(8,128)} %bitcast.7, bf16[4,72,128]{2,1,0:T(8,128)(2,1)S(1)} %get-tuple-element.27.halo_ref, ...), custom_call_target="tpu_custom_call" | custom-call | tf_op jit(solution)/shard_map/pallas_call | solution.py:659
  31.9 0.8 %collective-permute-done.2.far_ref = bf16[72,256]{1,0:T(8,128)(2,1)S(1)} collective-permute-done((bf16[72,256]{1,0:T(8,128)(2,1)S(1)}, bf16[72,256]{1,0:T(8,128)(2,1)S(1)}, u32[]{:S(2)}, u32[]{:S(2)}) %collective-permute-start.2) | collective-permute-done | bytes 36896 | tf_op jit(solution)/shard_map/ppermute | solution.py:687
  32.7 0.0 collective-permute-done.next_frames_ref
  32.7 0.2 collective-permute-done.3.far_halo_ref
  32.9 0.0 collective-permute-done.1.next_halo_ref
  32.9 8.2 %first.1 = (f32[4,72,384]{2,1,0:T(8,128)S(1)}, bf16[5,72,256]{2,1,0:T(8,128)(2,1)S(1)}, bf16[72,384]{1,0:T(8,128)(2,1)S(1)}) custom-call(s32[4,16]{1,0:T(4,128)} %bitcast.12, f32[17]{0:T(128)} %plan_ref.9, s32[4]{0:T(128)} %level_ref.9, f32[552,128]{1,0:T(8,128)} %bitcast.8, f32[2,69,1,256]{3,2,1,0:T(1,128)} %fresh_ref.3, ...), custom_call_target="tpu_custom_call" | custom-call | tf_op jit(solution)/shard_map/first/pallas_call | solution.py:699
  41.1 2.7 %collective-permute-start.4 = (bf16[5,72,256]{2,1,0:T(8,128)(2,1)S(1)}, bf16[5,72,256]{2,1,0:T(8,128)(2,1)S(1)}, u32[]{:S(2)}, u32[]{:S(2)}) collective-permute-start(bf16[5,72,256]{2,1,0:T(8,128)(2,1)S(1)} %get-tuple-element.39), channel_id=1, source_target_pairs={{16,0},{32,16},{48,32},{64,48},{80,64},{96,80},{112,96},{128,112},... | collective-permute-start | bytes 552968 | tf_op jit(solution)/shard_map/ppermute | solution.py:719
  43.8 1.4 %collective-permute-start.5 = (bf16[72,384]{1,0:T(8,128)(2,1)S(1)}, bf16[72,384]{1,0:T(8,128)(2,1)S(1)}, u32[]{:S(2)}, u32[]{:S(2)}) collective-permute-start(bf16[72,384]{1,0:T(8,128)(2,1)S(1)} %get-tuple-element.40), channel_id=1, source_target_pairs={{32,0},{48,16},{64,32},{80,48},{96,64},{112,80},{128,96},{144,112}... | collective-permute-start | bytes 165896 | tf_op jit(solution)/shard_map/ppermute | solution.py:720
  45.2 2.5 %shard_map.128 = (f32[3,256,256]{2,1,0:T(8,128)S(1)}, f32[3,96,8,256]{3,2,1,0:T(8,128)S(1)}) custom-call(s32[4,16]{1,0:T(4,128)} %bitcast.13, f32[17]{0:T(128)} %plan_ref.9, s32[4]{0:T(128)} %level_ref.9, f32[4,72,384]{2,1,0:T(8,128)S(1)} %get-tuple-element.38.own_ref, bf16[256,648]{1,0:T(8,128)(2,1)S(1)} %get-tuple-element.32.taps_ref, ...), custom_call_target="tpu_custom_call" | custom-call | tf_op jit(solution)/shard_map/pallas_call | solution.py:659
  47.7 2.0 %collective-permute-done.5.far_ref = bf16[72,384]{1,0:T(8,128)(2,1)S(1)} collective-permute-done((bf16[72,384]{1,0:T(8,128)(2,1)S(1)}, bf16[72,384]{1,0:T(8,128)(2,1)S(1)}, u32[]{:S(2)}, u32[]{:S(2)}) %collective-permute-start.5) | collective-permute-done | bytes 55328 | tf_op jit(solution)/shard_map/ppermute | solution.py:720
  49.7 0.0 collective-permute-done.4.came_ref
  49.7 6.2 %second.1 = f32[552,128]{1,0:T(8,128)} custom-call(s32[4,16]{1,0:T(4,128)} %bitcast.14, f32[17]{0:T(128)} %plan_ref.9, s32[4]{0:T(128)} %level_ref.9, f32[4,72,384]{2,1,0:T(8,128)S(1)} %get-tuple-element.38.own_ref, bf16[5,72,256]{2,1,0:T(8,128)(2,1)S(1)} %collective-permute-done.4.came_ref, bf16[72,384]{1,0:T(8,128)(2,1)S(1)} %collective-permute-done.5.far_ref, ...), custom_call_target="tpu_custom_call" | custom-call | tf_op jit(solution)/shard_map/second/pallas_call | solution.py:722
Async XLA Ops:
  2.3 16.2 %all-to-all-start = ((bf16[16,80,128]{2,1,0:T(8,128)(2,1)}), bf16[16,80,128]{2,1,0:T(8,128)(2,1)S(1)}, u32[]{:S(2)}, u32[]{:S(2)}) async-start(bf16[16,80,128]{2,1,0:T(8,128)(2,1)} %get-tuple-element.24), calls=%async_computation | async-start | bytes 655360 | tf_op jit(solution)/shard_map/all_to_all | solution.py:686
  8.4 24.3 %collective-permute-start = (bf16[4,72,256]{2,1,0:T(8,128)(2,1)S(1)}, bf16[4,72,256]{2,1,0:T(8,128)(2,1)S(1)}, u32[]{:S(2)}, u32[]{:S(2)}) collective-permute-start(bf16[4,72,256]{2,1,0:T(8,128)(2,1)S(1)} %get-tuple-element.29), channel_id=1, source_target_pairs={{16,0},{32,16},{48,32},{64,48},{80,64},{96,80},{112,96},{128,112},... | collective-permute-start | bytes 442376 | tf_op jit(solution)/shard_map/ppermute | solution.py:685
  19.6 13.3 %collective-permute-start.1 = (bf16[4,72,128]{2,1,0:T(8,128)(2,1)S(1)}, bf16[4,72,128]{2,1,0:T(8,128)(2,1)S(1)}, u32[]{:S(2)}, u32[]{:S(2)}) collective-permute-start(bf16[4,72,128]{2,1,0:T(8,128)(2,1)S(1)} %get-tuple-element.27.halo_ref), channel_id=1, source_target_pairs={{16,0},{32,16},{48,32},{64,48},{80,64},{96,80},{112,96},{128,112},... | collective-permute-start | bytes 221192 | tf_op jit(solution)/shard_map/ppermute | solution.py:694
  27.8 4.9 %collective-permute-start.2 = (bf16[72,256]{1,0:T(8,128)(2,1)S(1)}, bf16[72,256]{1,0:T(8,128)(2,1)S(1)}, u32[]{:S(2)}, u32[]{:S(2)}) collective-permute-start(bf16[72,256]{1,0:T(8,128)(2,1)S(1)} %get-tuple-element.30), channel_id=1, source_target_pairs={{32,0},{48,16},{64,32},{80,48},{96,64},{112,80},{128,96},{144,112}... | collective-permute-start | bytes 110600 | tf_op jit(solution)/shard_map/ppermute | solution.py:687
  27.8 5.1 %collective-permute-start.3 = (bf16[72,128]{1,0:T(8,128)(2,1)S(1)}, bf16[72,128]{1,0:T(8,128)(2,1)S(1)}, u32[]{:S(2)}, u32[]{:S(2)}) collective-permute-start(bf16[72,128]{1,0:T(8,128)(2,1)S(1)} %get-tuple-element.31), channel_id=1, source_target_pairs={{32,0},{48,16},{64,32},{80,48},{96,64},{112,80},{128,96},{144,112}... | collective-permute-start | bytes 55304 | tf_op jit(solution)/shard_map/ppermute | solution.py:695
  41.1 8.6 %collective-permute-start.4 = (bf16[5,72,256]{2,1,0:T(8,128)(2,1)S(1)}, bf16[5,72,256]{2,1,0:T(8,128)(2,1)S(1)}, u32[]{:S(2)}, u32[]{:S(2)}) collective-permute-start(bf16[5,72,256]{2,1,0:T(8,128)(2,1)S(1)} %get-tuple-element.39), channel_id=1, source_target_pairs={{16,0},{32,16},{48,32},{64,48},{80,64},{96,80},{112,96},{128,112},... | collective-permute-start | bytes 552968 | tf_op jit(solution)/shard_map/ppermute | solution.py:719
  43.8 5.9 %collective-permute-start.5 = (bf16[72,384]{1,0:T(8,128)(2,1)S(1)}, bf16[72,384]{1,0:T(8,128)(2,1)S(1)}, u32[]{:S(2)}, u32[]{:S(2)}) collective-permute-start(bf16[72,384]{1,0:T(8,128)(2,1)S(1)} %get-tuple-element.40), channel_id=1, source_target_pairs={{32,0},{48,16},{64,32},{80,48},{96,64},{112,80},{128,96},{144,112}... | collective-permute-start | bytes 165896 | tf_op jit(solution)/shard_map/ppermute | solution.py:720

commit v6 on v5

--- a/solution.py
+++ b/solution.py
@@ -431,29 +431,27 @@
 
 def denoise(
     lanes, near_ref, plan_ref, level_ref, weights, states, sigmas, scratch,
-    hidden_own, qkv_own, hidden_all, qkv_all, context_all, arrived, finished,
+    hidden_own, qkv_own, hidden_all, qkv_all, context_all, finished,
 ):
     taps_ref, lift_ref, qkv_ref, attend_ref, decode_ref = weights
     is_last = lax.axis_index("noise") == lax.axis_size("noise") - 1
     held = len(OWN)
-    copies = (
-        pltpu.make_async_copy(qkv_own, qkv_all.at[pl.ds(0, held)], arrived.at[0]),
-        pltpu.make_async_copy(hidden_own, hidden_all.at[pl.ds(0, held)], arrived.at[1]),
-    )
-    for copy in copies:
-        copy.start()
     features = features_of(REST, lanes, near_ref, taps_ref, lift_ref, states, sigmas, *scratch)
     for p in REST:
         hidden, normed = features(p)
         if p < FR_DEV:
-            hidden_all[p] = hidden
-            qkv_all[p] = mm(qkv_ref[...], normed).reshape(3 * HEAD, HEADS, lanes)
+            hidden_all[...] = hidden
+            qkv_all[p - held] = mm(qkv_ref[...], normed).reshape(3 * HEAD, HEADS, lanes)
         else:
-            qkv_all[p, HEAD : 3 * HEAD] = mm(qkv_ref[WIDTH : 3 * WIDTH, :], normed).reshape(
+            qkv_all[p - held, HEAD : 3 * HEAD] = mm(qkv_ref[WIDTH : 3 * WIDTH, :], normed).reshape(
                 2 * HEAD, HEADS, lanes
             )
-    for copy in copies:
-        copy.wait()
+
+    def every(row, at):
+        return jnp.concatenate([qkv_own[:, row, :, at], qkv_all[:, row, :, at]], axis=0)
+
+    def query(i, d, at):
+        return qkv_own[i, d, :, at] if i < held else qkv_all[i - held, d, :, at]
 
     hide = jnp.where(is_last, -jnp.inf, 0.0)
     for part in range(lanes // 128):
@@ -464,9 +462,9 @@
         for pair in range(0, FR_DEV, 2):
 
             def score(d, so_far, pair=pair):
-                keys = qkv_all[:, HEAD + d, :, at]
+                keys = every(HEAD + d, at)
                 return tuple(
-                    so_far[i] + qkv_all[pair + i, d, :, at][None] * keys for i in range(2)
+                    so_far[i] + query(pair + i, d, at)[None] * keys for i in range(2)
                 )
 
             sums.extend(lax.fori_loop(0, HEAD, score, (zero,) * 2, unroll=HEAD))
@@ -476,10 +474,10 @@
             scores = sums[i] * HEAD ** (-0.5) + jnp.where(second_half, hide, 0.0)
             top = jnp.max(scores, axis=0, keepdims=True)
             raised = jnp.exp(scores - top)
-            weights.append(raised / jnp.sum(raised, axis=0, keepdims=True))
+            weights.append(raised * (1.0 / jnp.sum(raised, axis=0, keepdims=True)))
 
         def combine(d, carry):
-            values = qkv_all[:, 2 * HEAD + d, :, at]
+            values = every(2 * HEAD + d, at)
             for i in range(FR_DEV):
                 context_all[i, d, :, at] = jnp.sum(weights[i] * values, axis=0)
             return carry
@@ -488,7 +486,8 @@
 
     for p in range(FR_DEV):
         context = context_all[p].reshape(WIDTH, lanes).astype(BF)
-        refined = (hidden_all[p] + mm(attend_ref[...], context)).astype(BF)
+        hidden = hidden_own[p] if p < held else hidden_all[...]
+        refined = (hidden + mm(attend_ref[...], context)).astype(BF)
         projected = mm(decode_ref[...], refined)
         sigma = wide(sigmas[p], lanes)
         sigma_next = jnp.full((1, lanes), plan_ref[level_ref[p] + 1], F32)
@@ -544,7 +543,7 @@
     next_halo_ref, far_ref, far_halo_ref, hidden_own, qkv_own,
     taps_ref, lift_ref, qkv_ref, attend_ref, decode_ref,
     own_out, near_out, far_out,
-    states, sigmas, scaled, images, ring_windows, hidden_all, qkv_all, context_all, arrived, message,
+    states, sigmas, scaled, images, ring_windows, hidden_all, qkv_all, context_all, message,
 ):
     own_sigmas(plan_ref, level_ref, sigmas)
     next_sigmas(next_frames_ref, sigmas)
@@ -568,7 +567,7 @@
         CELLS + 128, near_ref, plan_ref, level_ref,
         (taps_ref, lift_ref, qkv_ref, attend_ref, decode_ref),
         states, sigmas, (scaled, images, ring_windows), hidden_own, qkv_own,
-        hidden_all, qkv_all, context_all, arrived, finished,
+        hidden_all, qkv_all, context_all, finished,
     )
 
     @pl.when(lax.axis_index("noise") == 0)
@@ -608,7 +607,7 @@
 def second_kernel(
     near_ref, plan_ref, level_ref, own_ref, came_ref, far_ref, hidden_own, qkv_own,
     taps_ref, lift_ref, qkv_ref, attend_ref, decode_ref,
-    out_ref, states, sigmas, scaled, images, hidden_all, qkv_all, context_all, arrived,
+    out_ref, states, sigmas, scaled, images, hidden_all, qkv_all, context_all,
 ):
     own_sigmas(plan_ref, level_ref, sigmas)
     next_sigmas(came_ref, sigmas)
@@ -630,7 +629,7 @@
         CELLS, near_ref, plan_ref, level_ref,
         (taps_ref, lift_ref, qkv_ref, attend_ref, decode_ref),
         states, sigmas, (scaled, images, None), hidden_own, qkv_own,
-        hidden_all, qkv_all, context_all, arrived, finished,
+        hidden_all, qkv_all, context_all, finished,
     )
 
 
@@ -648,10 +647,9 @@
 
 def attention_scratch(lanes):
     return [
-        pltpu.VMEM((FR_DEV, WIDTH, lanes), F32),
-        pltpu.VMEM((2 * FR_DEV, 3 * HEAD, HEADS, lanes), F32),
+        pltpu.VMEM((WIDTH, lanes), F32),
+        pltpu.VMEM((len(REST), 3 * HEAD, HEADS, lanes), F32),
         pltpu.VMEM((FR_DEV, HEAD, HEADS, lanes), F32),
-        pltpu.SemaphoreType.DMA((2,)),
     ]
 
 
@@ -693,7 +691,7 @@
     halos, front_halo, later = halo_cells(near, slots, weights[1])
     next_halos = near_core(lax.ppermute(halos, "noise", from_next))
     far_halo = near_core(lax.ppermute(front_halo, "noise", from_second))
-    both = (pl.BlockSpec(memory_space=pl.ANY),) * 2
+    both = (VMEM,) * 2
     lanes = CELLS + 128
     own_part = own_call(first_own_kernel, lanes, near, plan, levels, queue, halos, *weights[:3])
     own, near_message, far_message = pl.pallas_call(

time: 56.7 us -> 56 us (0.988)
  Pallas kernels: 26.7 us -> 26.1 us
where the time goes in v6:
time: 56 us; the launch traced here: 55.3 us
  Pallas kernels  26.1 us (47%)
  starting transfers between devices  25.7 us (46%)
  waiting for transfers between devices  3.44 us (6%)
    ppermute x1, starting transfers between devices, shards(): next_halos = near_core(lax.ppermute(halos, 'noise', from_next))  8.24 us
    pallas_call x1, Pallas kernels, shards(): pl.pallas_call(first_kernel, out_shape=(jax.ShapeDtypeStruct((FR_DEV, ROW...  7.66 us
    ppermute x1, starting transfers between devices, shards(): next_frames = near_core(lax.ppermute(frames, 'noise', from_next))  6.72 us
    pallas_call x1, Pallas kernels, shards(): pl.pallas_call(second_kernel, out_shape=jax.ShapeDtypeStruct((FR_DEV * FI...  6.16 us
    all_to_all x1, starting transfers between devices, shards(): lax.all_to_all(slots, TILE_AXES, split_axis=0, concat_axis=0, tiled=True)  6.14 us
    pallas_call x2, Pallas kernels, own_call(): pl.pallas_call(kernel, out_shape=(pltpu.VMEM((len(OWN), WIDTH, lanes), F3...  6.11 us
    pallas_call x1, Pallas kernels, prepare_weights(): pl.pallas_call(weights_kernel, out_shape=(pltpu.VMEM((WIDTH, TAPS * ROWS)...  2.8 us
    ppermute x1, starting transfers between devices, shards(): came = near_core(lax.ppermute(near_message, 'noise', from_next))  2.74 us
  transfers between devices with their start and end apart: 7, of which 4 were waited for; matrix products, arithmetic and copies ran while one was open for 0% of the time, Pallas kernels for 18%

profile of v6, /device:TPU:8, one launch (start us, length us, event | category | flops | bytes accessed | tf_op | source)
XLA Modules:
  0.0 55.3 jit_solution(8035204635512589048)
XLA Ops:
  0.0 2.3 %border.1 = (bf16[4,72,256]{2,1,0:T(8,128)(2,1)S(1)}, bf16[72,256]{1,0:T(8,128)(2,1)S(1)}, bf16[16,80,128]{2,1,0:T(8,128)(2,1)}, s32[1]{0:T(128)}) custom-call(s32[4,16]{1,0:T(4,128)} %bitcast.9, f32[17]{0:T(128)} %plan_ref.9, s32[4]{0:T(128)} %level_ref.9, f32[552,128]{1,0:T(8,128)} %bitcast.6, f32[2,69,1,256]{3,2,1,0:T(1,128)} %fresh_ref.3), custom_call_target="tpu_custom_call" | custom-call | tf_op jit(solution)/shard_map/border/pallas_call | solution.py:201
  2.3 6.1 %all-to-all-start = ((bf16[16,80,128]{2,1,0:T(8,128)(2,1)}), bf16[16,80,128]{2,1,0:T(8,128)(2,1)S(1)}, u32[]{:S(2)}, u32[]{:S(2)}) async-start(bf16[16,80,128]{2,1,0:T(8,128)(2,1)} %get-tuple-element.24), calls=%async_computation | async-start | bytes 655360 | tf_op jit(solution)/shard_map/all_to_all | solution.py:684
  8.4 6.7 %collective-permute-start = (bf16[4,72,256]{2,1,0:T(8,128)(2,1)S(1)}, bf16[4,72,256]{2,1,0:T(8,128)(2,1)S(1)}, u32[]{:S(2)}, u32[]{:S(2)}) collective-permute-start(bf16[4,72,256]{2,1,0:T(8,128)(2,1)S(1)} %get-tuple-element.29), channel_id=1, source_target_pairs={{16,0},{32,16},{48,32},{64,48},{80,64},{96,80},{112,96},{128,112},... | collective-permute-start | bytes 442376 | tf_op jit(solution)/shard_map/ppermute | solution.py:683
  15.1 2.8 %weights.1 = (bf16[256,648]{1,0:T(8,128)(2,1)S(1)}, bf16[256,72]{1,0:T(8,128)(2,1)S(1)}, bf16[768,256]{1,0:T(8,128)(2,1)S(1)}, bf16[256,256]{1,0:T(8,128)(2,1)S(1)}, bf16[72,256]{1,0:T(8,128)(2,1)S(1)}) custom-call(bf16[69,256]{1,0:T(8,128)(2,1)} %bitcast.15, f32[1,256]{1,0:T(1,128)} %bitcast.16, bf16[9,256,256]{2,1,0:T(8,128)(2,1)} %conv_ref.1, ...), custom_call_target="tpu_custom_call" | custom-call | tf_op jit(solution)/shard_map/weights/pallas_call | solution.py:92
  17.9 0.5 all-to-all-done.slots_ref
  18.4 1.2 %ring.1 = (bf16[4,72,128]{2,1,0:T(8,128)(2,1)S(1)}, bf16[72,128]{1,0:T(8,128)(2,1)S(1)}, bf16[72,128]{1,0:T(8,128)(2,1)S(1)}) custom-call(s32[4,16]{1,0:T(4,128)} %bitcast.10, bf16[16,80,128]{2,1,0:T(8,128)(2,1)S(1)} %all-to-all-done.slots_ref, bf16[256,72]{1,0:T(8,128)(2,1)S(1)} %get-tuple-element.26.wait_ref.lift_ref), custom_call_target="tpu_custom_call" | custom-call | tf_op jit(solution)/shard_map/ring/pallas_call | solution.py:297
  19.6 8.2 %collective-permute-start.1 = (bf16[4,72,128]{2,1,0:T(8,128)(2,1)S(1)}, bf16[4,72,128]{2,1,0:T(8,128)(2,1)S(1)}, u32[]{:S(2)}, u32[]{:S(2)}) collective-permute-start(bf16[4,72,128]{2,1,0:T(8,128)(2,1)S(1)} %get-tuple-element.27.halo_ref), channel_id=1, source_target_pairs={{16,0},{32,16},{48,32},{64,48},{80,64},{96,80},{112,96},{128,112},... | collective-permute-start | bytes 221192 | tf_op jit(solution)/shard_map/ppermute | solution.py:692
  27.8 0.0 collective-permute-start.2
  27.8 0.5 collective-permute-start.3
  28.3 3.6 %shard_map.127 = (f32[3,256,384]{2,1,0:T(8,128)S(1)}, f32[3,96,8,384]{3,2,1,0:T(8,128)S(1)}) custom-call(s32[4,16]{1,0:T(4,128)} %bitcast.11, f32[17]{0:T(128)} %plan_ref.9, s32[4]{0:T(128)} %level_ref.9, f32[552,128]{1,0:T(8,128)} %bitcast.7, bf16[4,72,128]{2,1,0:T(8,128)(2,1)S(1)} %get-tuple-element.27.halo_ref, ...), custom_call_target="tpu_custom_call" | custom-call | tf_op jit(solution)/shard_map/pallas_call | solution.py:657
  31.9 0.8 %collective-permute-done.2.far_ref = bf16[72,256]{1,0:T(8,128)(2,1)S(1)} collective-permute-done((bf16[72,256]{1,0:T(8,128)(2,1)S(1)}, bf16[72,256]{1,0:T(8,128)(2,1)S(1)}, u32[]{:S(2)}, u32[]{:S(2)}) %collective-permute-start.2) | collective-permute-done | bytes 36896 | tf_op jit(solution)/shard_map/ppermute | solution.py:685
  32.7 0.0 collective-permute-done.next_frames_ref
  32.7 0.2 collective-permute-done.3.far_halo_ref
  32.9 0.0 collective-permute-done.1.next_halo_ref
  32.9 7.7 %first.1 = (f32[4,72,384]{2,1,0:T(8,128)S(1)}, bf16[5,72,256]{2,1,0:T(8,128)(2,1)S(1)}, bf16[72,384]{1,0:T(8,128)(2,1)S(1)}) custom-call(s32[4,16]{1,0:T(4,128)} %bitcast.12, f32[17]{0:T(128)} %plan_ref.9, s32[4]{0:T(128)} %level_ref.9, f32[552,128]{1,0:T(8,128)} %bitcast.8, f32[2,69,1,256]{3,2,1,0:T(1,128)} %fresh_ref.3, ...), custom_call_target="tpu_custom_call" | custom-call | tf_op jit(solution)/shard_map/first/pallas_call | solution.py:697
  40.5 2.7 %collective-permute-start.4 = (bf16[5,72,256]{2,1,0:T(8,128)(2,1)S(1)}, bf16[5,72,256]{2,1,0:T(8,128)(2,1)S(1)}, u32[]{:S(2)}, u32[]{:S(2)}) collective-permute-start(bf16[5,72,256]{2,1,0:T(8,128)(2,1)S(1)} %get-tuple-element.39), channel_id=1, source_target_pairs={{16,0},{32,16},{48,32},{64,48},{80,64},{96,80},{112,96},{128,112},... | collective-permute-start | bytes 552968 | tf_op jit(solution)/shard_map/ppermute | solution.py:717
  43.3 1.4 %collective-permute-start.5 = (bf16[72,384]{1,0:T(8,128)(2,1)S(1)}, bf16[72,384]{1,0:T(8,128)(2,1)S(1)}, u32[]{:S(2)}, u32[]{:S(2)}) collective-permute-start(bf16[72,384]{1,0:T(8,128)(2,1)S(1)} %get-tuple-element.40), channel_id=1, source_target_pairs={{32,0},{48,16},{64,32},{80,48},{96,64},{112,80},{128,96},{144,112}... | collective-permute-start | bytes 165896 | tf_op jit(solution)/shard_map/ppermute | solution.py:718
  44.7 2.5 %shard_map.128 = (f32[3,256,256]{2,1,0:T(8,128)S(1)}, f32[3,96,8,256]{3,2,1,0:T(8,128)S(1)}) custom-call(s32[4,16]{1,0:T(4,128)} %bitcast.13, f32[17]{0:T(128)} %plan_ref.9, s32[4]{0:T(128)} %level_ref.9, f32[4,72,384]{2,1,0:T(8,128)S(1)} %get-tuple-element.38.own_ref, bf16[256,648]{1,0:T(8,128)(2,1)S(1)} %get-tuple-element.32.taps_ref, ...), custom_call_target="tpu_custom_call" | custom-call | tf_op jit(solution)/shard_map/pallas_call | solution.py:657
  47.2 2.0 %collective-permute-done.5.far_ref = bf16[72,384]{1,0:T(8,128)(2,1)S(1)} collective-permute-done((bf16[72,384]{1,0:T(8,128)(2,1)S(1)}, bf16[72,384]{1,0:T(8,128)(2,1)S(1)}, u32[]{:S(2)}, u32[]{:S(2)}) %collective-permute-start.5) | collective-permute-done | bytes 55328 | tf_op jit(solution)/shard_map/ppermute | solution.py:718
  49.2 0.0 collective-permute-done.4.came_ref
  49.2 6.2 %second.1 = f32[552,128]{1,0:T(8,128)} custom-call(s32[4,16]{1,0:T(4,128)} %bitcast.14, f32[17]{0:T(128)} %plan_ref.9, s32[4]{0:T(128)} %level_ref.9, f32[4,72,384]{2,1,0:T(8,128)S(1)} %get-tuple-element.38.own_ref, bf16[5,72,256]{2,1,0:T(8,128)(2,1)S(1)} %collective-permute-done.4.came_ref, bf16[72,384]{1,0:T(8,128)(2,1)S(1)} %collective-permute-done.5.far_ref, ...), custom_call_target="tpu_custom_call" | custom-call | tf_op jit(solution)/shard_map/second/pallas_call | solution.py:720
Async XLA Ops:
  2.3 16.2 %all-to-all-start = ((bf16[16,80,128]{2,1,0:T(8,128)(2,1)}), bf16[16,80,128]{2,1,0:T(8,128)(2,1)S(1)}, u32[]{:S(2)}, u32[]{:S(2)}) async-start(bf16[16,80,128]{2,1,0:T(8,128)(2,1)} %get-tuple-element.24), calls=%async_computation | async-start | bytes 655360 | tf_op jit(solution)/shard_map/all_to_all | solution.py:684
  8.4 24.3 %collective-permute-start = (bf16[4,72,256]{2,1,0:T(8,128)(2,1)S(1)}, bf16[4,72,256]{2,1,0:T(8,128)(2,1)S(1)}, u32[]{:S(2)}, u32[]{:S(2)}) collective-permute-start(bf16[4,72,256]{2,1,0:T(8,128)(2,1)S(1)} %get-tuple-element.29), channel_id=1, source_target_pairs={{16,0},{32,16},{48,32},{64,48},{80,64},{96,80},{112,96},{128,112},... | collective-permute-start | bytes 442376 | tf_op jit(solution)/shard_map/ppermute | solution.py:683
  19.6 13.3 %collective-permute-start.1 = (bf16[4,72,128]{2,1,0:T(8,128)(2,1)S(1)}, bf16[4,72,128]{2,1,0:T(8,128)(2,1)S(1)}, u32[]{:S(2)}, u32[]{:S(2)}) collective-permute-start(bf16[4,72,128]{2,1,0:T(8,128)(2,1)S(1)} %get-tuple-element.27.halo_ref), channel_id=1, source_target_pairs={{16,0},{32,16},{48,32},{64,48},{80,64},{96,80},{112,96},{128,112},... | collective-permute-start | bytes 221192 | tf_op jit(solution)/shard_map/ppermute | solution.py:692
  27.8 4.9 %collective-permute-start.2 = (bf16[72,256]{1,0:T(8,128)(2,1)S(1)}, bf16[72,256]{1,0:T(8,128)(2,1)S(1)}, u32[]{:S(2)}, u32[]{:S(2)}) collective-permute-start(bf16[72,256]{1,0:T(8,128)(2,1)S(1)} %get-tuple-element.30), channel_id=1, source_target_pairs={{32,0},{48,16},{64,32},{80,48},{96,64},{112,80},{128,96},{144,112}... | collective-permute-start | bytes 110600 | tf_op jit(solution)/shard_map/ppermute | solution.py:685
  27.8 5.1 %collective-permute-start.3 = (bf16[72,128]{1,0:T(8,128)(2,1)S(1)}, bf16[72,128]{1,0:T(8,128)(2,1)S(1)}, u32[]{:S(2)}, u32[]{:S(2)}) collective-permute-start(bf16[72,128]{1,0:T(8,128)(2,1)S(1)} %get-tuple-element.31), channel_id=1, source_target_pairs={{32,0},{48,16},{64,32},{80,48},{96,64},{112,80},{128,96},{144,112}... | collective-permute-start | bytes 55304 | tf_op jit(solution)/shard_map/ppermute | solution.py:693
  40.5 8.6 %collective-permute-start.4 = (bf16[5,72,256]{2,1,0:T(8,128)(2,1)S(1)}, bf16[5,72,256]{2,1,0:T(8,128)(2,1)S(1)}, u32[]{:S(2)}, u32[]{:S(2)}) collective-permute-start(bf16[5,72,256]{2,1,0:T(8,128)(2,1)S(1)} %get-tuple-element.39), channel_id=1, source_target_pairs={{16,0},{32,16},{48,32},{64,48},{80,64},{96,80},{112,96},{128,112},... | collective-permute-start | bytes 552968 | tf_op jit(solution)/shard_map/ppermute | solution.py:717
  43.3 5.9 %collective-permute-start.5 = (bf16[72,384]{1,0:T(8,128)(2,1)S(1)}, bf16[72,384]{1,0:T(8,128)(2,1)S(1)}, u32[]{:S(2)}, u32[]{:S(2)}) collective-permute-start(bf16[72,384]{1,0:T(8,128)(2,1)S(1)} %get-tuple-element.40), channel_id=1, source_target_pairs={{32,0},{48,16},{64,32},{80,48},{96,64},{112,80},{128,96},{144,112}... | collective-permute-start | bytes 165896 | tf_op jit(solution)/shard_map/ppermute | solution.py:718

commit v7 on v6

--- a/solution.py
+++ b/solution.py
@@ -51,9 +51,10 @@
 
 
 def weights_kernel(
-    in_ref, embed_ref, conv_ref, gain_ref, query_ref, memory_ref, out_ref, decode_ref, after_ref,
-    taps_out, lift_out, qkv_out, attend_out, decode_out, folded,
-):
+    in_ref, embed_ref, conv_ref, gain_ref, query_ref, memory_ref, out_ref, decode_ref, near_ref,
+    after_ref, taps_out, lift_out, spread_out, pick_out, qkv_out, attend_out, decode_out, folded,
+):
+    selections(near_ref[2, lax.axis_index(TILE_AXES)] >= 0, spread_out, pick_out)
     rows = iota((ROWS, WIDTH), 0)
     unit = (iota((ROWS, FIELDS), 0) == iota((ROWS, FIELDS), 1)).astype(BF)
     lift_t = mm(unit, in_ref[...])
@@ -88,18 +89,20 @@
     decode_out[...] = mm(unit, decode_ref[...]).astype(BF)
 
 
-def prepare_weights(in_weight, embed, conv, gain, query, memory, attend, decode, after):
+def prepare_weights(in_weight, embed, conv, gain, query, memory, attend, decode, near, after):
     return pl.pallas_call(
         weights_kernel,
         out_shape=(
             pltpu.VMEM((WIDTH, TAPS * ROWS), BF),
             pltpu.VMEM((WIDTH, ROWS), BF),
+            pltpu.VMEM((128, 4 * CELLS), BF),
+            pltpu.VMEM((CELLS + 128, 5 * 128), BF),
             pltpu.VMEM((3 * WIDTH, WIDTH), BF),
             pltpu.VMEM((WIDTH, WIDTH), BF),
             pltpu.VMEM((ROWS, WIDTH), BF),
         ),
-        in_specs=[VMEM] * 8 + [SMEM],
-        out_specs=(VMEM,) * 5,
+        in_specs=[VMEM] * 8 + [SMEM] * 2,
+        out_specs=(VMEM,) * 7,
         scratch_shapes=[pltpu.VMEM((TAPS * ROWS, WIDTH), F32)],
         compiler_params=pltpu.CompilerParams(vmem_limit_bytes=40 << 20),
         name="weights",
@@ -111,6 +114,7 @@
                 attend, decode,
             ),
         ),
+        near,
         after,
     )
 
@@ -320,8 +324,47 @@
     return jnp.concatenate([row] * (lanes // 128), axis=1)
 
 
+def selections(at_north, spread_out, pick_out):
+    ring_row = iota((128, 4 * CELLS), 0)
+    column = iota((8, 4 * CELLS), 1)
+    shift = column // CELLS - 2
+    cell_x = column % TILE
+    cell_y = (column % CELLS) // TILE
+    line_x = cell_x + shift
+    from_line = jnp.where(
+        line_x < 0, 3 * TILE, jnp.where(line_x >= TILE, 3 * TILE + 1, 2 * TILE + line_x)
+    )
+    from_side = jnp.where(cell_x == 0, cell_y, TILE + cell_y)
+    spot = jnp.where(column < CELLS, from_side, from_line)
+    spread_out[...] = (ring_row == spot[0:1]).astype(BF)
+    near_row = jnp.where(at_north, -1, TILE)
+    far_row = jnp.where(at_north, -2, TILE + 1)
+    column = iota((8, 5 * 128), 1)
+    tap = column // 64
+    cell = column % 64
+    block = cell // TILE
+    along = cell % TILE
+    row = jnp.where(block < 2, along, near_row) + tap // 3 - 1
+    col = jnp.where(
+        block == 0,
+        -1,
+        jnp.where(block == 1, TILE, jnp.where(block == 2, along, jnp.where(along == 0, -1, TILE))),
+    )
+    col = col + tap % 3 - 1
+    in_tile = jnp.logical_and(
+        jnp.logical_and(row >= 0, row < TILE), jnp.logical_and(col >= 0, col < TILE)
+    )
+    halo = halo_lane(row, col, near_row, far_row)
+    spot = jnp.where(
+        in_tile, row * TILE + col, jnp.where(halo >= 0, CELLS + halo, -1)
+    )
+    spot = jnp.where(cell < 50, spot, -1)
+    pick_out[...] = (iota((CELLS + 128, 5 * 128), 0) == spot[0:1]).astype(BF)
+
+
 def features_of(
-    frames, lanes, near_ref, taps_ref, lift_ref, states, sigmas, scaled, images, ring_windows
+    frames, lanes, near_ref, taps_ref, lift_ref, spread_ref, pick_ref, states, sigmas, scaled,
+    images, ring_windows,
 ):
     me = lax.axis_index(TILE_AXES)
     at_north = near_ref[2, me] >= 0
@@ -339,45 +382,10 @@
         scaled[p] = with_log_rows(
             states[p] * wide(scale, total), wide(log_hi, total), wide(log_lo, total), total
         )
-    ring_row = iota((128, 4 * CELLS), 0)
-    column = iota((8, 4 * CELLS), 1)
-    shift = column // CELLS - 2
-    cell_x = column % TILE
-    cell_y = (column % CELLS) // TILE
-    line_x = cell_x + shift
-    from_line = jnp.where(
-        line_x < 0, 3 * TILE, jnp.where(line_x >= TILE, 3 * TILE + 1, 2 * TILE + line_x)
-    )
-    from_side = jnp.where(cell_x == 0, cell_y, TILE + cell_y)
-    spot = jnp.where(column < CELLS, from_side, from_line)
-    spread = (ring_row == spot[0:1]).astype(BF)
     low = scaled[begin : begin + count].reshape(count * ROWS, total).astype(BF)
-    images[begin : begin + count] = mm(low[:, CELLS:], spread).reshape(count, ROWS, 4 * CELLS)
+    images[begin : begin + count] = mm(low[:, CELLS:], spread_ref[...]).reshape(count, ROWS, 4 * CELLS)
     if extended:
-        near_row = jnp.where(at_north, -1, TILE)
-        far_row = jnp.where(at_north, -2, TILE + 1)
-        column = iota((8, 5 * 128), 1)
-        tap = column // 64
-        cell = column % 64
-        block = cell // TILE
-        along = cell % TILE
-        row = jnp.where(block < 2, along, near_row) + tap // 3 - 1
-        col = jnp.where(
-            block == 0,
-            -1,
-            jnp.where(block == 1, TILE, jnp.where(block == 2, along, jnp.where(along == 0, -1, TILE))),
-        )
-        col = col + tap % 3 - 1
-        in_tile = jnp.logical_and(
-            jnp.logical_and(row >= 0, row < TILE), jnp.logical_and(col >= 0, col < TILE)
-        )
-        halo = halo_lane(row, col, near_row, far_row)
-        spot = jnp.where(
-            in_tile, row * TILE + col, jnp.where(halo >= 0, CELLS + halo, -1)
-        )
-        spot = jnp.where(cell < 50, spot, -1)
-        pick = (iota((CELLS + 128, 5 * 128), 0) == spot[0:1]).astype(BF)
-        ring_windows[begin : begin + count] = mm(low, pick).reshape(count, ROWS, 5 * 128)
+        ring_windows[begin : begin + count] = mm(low, pick_ref[...]).reshape(count, ROWS, 5 * 128)
 
     across = iota((ROWS, CELLS), 1) % TILE
     down = iota((ROWS, CELLS), 1) // TILE
@@ -421,8 +429,10 @@
 
 
 def own_frames(lanes, near_ref, weights, states, sigmas, scratch, hidden_out, qkv_out):
-    taps_ref, lift_ref, qkv_ref = weights
-    features = features_of(OWN, lanes, near_ref, taps_ref, lift_ref, states, sigmas, *scratch)
+    taps_ref, lift_ref, spread_ref, pick_ref, qkv_ref = weights
+    features = features_of(
+        OWN, lanes, near_ref, taps_ref, lift_ref, spread_ref, pick_ref, states, sigmas, *scratch
+    )
     for p in OWN:
         hidden, normed = features(p)
         hidden_out[p] = hidden
@@ -433,10 +443,12 @@
     lanes, near_ref, plan_ref, level_ref, weights, states, sigmas, scratch,
     hidden_own, qkv_own, hidden_all, qkv_all, context_all, finished,
 ):
-    taps_ref, lift_ref, qkv_ref, attend_ref, decode_ref = weights
+    taps_ref, lift_ref, spread_ref, pick_ref, qkv_ref, attend_ref, decode_ref = weights
     is_last = lax.axis_index("noise") == lax.axis_size("noise") - 1
     held = len(OWN)
-    features = features_of(REST, lanes, near_ref, taps_ref, lift_ref, states, sigmas, *scratch)
+    features = features_of(
+        REST, lanes, near_ref, taps_ref, lift_ref, spread_ref, pick_ref, states, sigmas, *scratch
+    )
     for p in REST:
         hidden, normed = features(p)
         if p < FR_DEV:
@@ -527,13 +539,13 @@
 
 
 def first_own_kernel(
-    near_ref, plan_ref, level_ref, queue_ref, halo_ref, taps_ref, lift_ref, qkv_ref,
+    near_ref, plan_ref, level_ref, queue_ref, halo_ref, taps_ref, lift_ref, spread_ref, pick_ref, qkv_ref,
     hidden_out, qkv_out, states, sigmas, *scratch,
 ):
     own_sigmas(plan_ref, level_ref, sigmas)
     first_own_states(queue_ref, halo_ref, states)
     own_frames(
-        CELLS + 128, near_ref, (taps_ref, lift_ref, qkv_ref), states, sigmas, scratch,
+        CELLS + 128, near_ref, (taps_ref, lift_ref, spread_ref, pick_ref, qkv_ref), states, sigmas, scratch,
         hidden_out, qkv_out,
     )
 
@@ -541,7 +553,7 @@
 def first_kernel(
     near_ref, plan_ref, level_ref, queue_ref, fresh_ref, halo_ref, later_ref, next_frames_ref,
     next_halo_ref, far_ref, far_halo_ref, hidden_own, qkv_own,
-    taps_ref, lift_ref, qkv_ref, attend_ref, decode_ref,
+    taps_ref, lift_ref, spread_ref, pick_ref, qkv_ref, attend_ref, decode_ref,
     own_out, near_out, far_out,
     states, sigmas, scaled, images, ring_windows, hidden_all, qkv_all, context_all, message,
 ):
@@ -565,7 +577,7 @@
 
     denoise(
         CELLS + 128, near_ref, plan_ref, level_ref,
-        (taps_ref, lift_ref, qkv_ref, attend_ref, decode_ref),
+        (taps_ref, lift_ref, spread_ref, pick_ref, qkv_ref, attend_ref, decode_ref),
         states, sigmas, (scaled, images, ring_windows), hidden_own, qkv_own,
         hidden_all, qkv_all, context_all, finished,
     )
@@ -593,20 +605,20 @@
 
 
 def second_own_kernel(
-    near_ref, plan_ref, level_ref, own_ref, taps_ref, lift_ref, qkv_ref,
+    near_ref, plan_ref, level_ref, own_ref, taps_ref, lift_ref, spread_ref, pick_ref, qkv_ref,
     hidden_out, qkv_out, states, sigmas, *scratch,
 ):
     own_sigmas(plan_ref, level_ref, sigmas)
     second_own_states(own_ref, states)
     own_frames(
-        CELLS, near_ref, (taps_ref, lift_ref, qkv_ref), states, sigmas, (*scratch, None),
+        CELLS, near_ref, (taps_ref, lift_ref, spread_ref, pick_ref, qkv_ref), states, sigmas, (*scratch, None),
         hidden_out, qkv_out,
     )
 
 
 def second_kernel(
     near_ref, plan_ref, level_ref, own_ref, came_ref, far_ref, hidden_own, qkv_own,
-    taps_ref, lift_ref, qkv_ref, attend_ref, decode_ref,
+    taps_ref, lift_ref, spread_ref, pick_ref, qkv_ref, attend_ref, decode_ref,
     out_ref, states, sigmas, scaled, images, hidden_all, qkv_all, context_all,
 ):
     own_sigmas(plan_ref, level_ref, sigmas)
@@ -627,7 +639,7 @@
 
     denoise(
         CELLS, near_ref, plan_ref, level_ref,
-        (taps_ref, lift_ref, qkv_ref, attend_ref, decode_ref),
+        (taps_ref, lift_ref, spread_ref, pick_ref, qkv_ref, attend_ref, decode_ref),
         states, sigmas, (scaled, images, None), hidden_own, qkv_own,
         hidden_all, qkv_all, context_all, finished,
     )
@@ -685,7 +697,7 @@
     far = lax.ppermute(front, "noise", from_second)
     weights = prepare_weights(
         in_weight, level_embed, conv_weight, norm_gain, query_weight, memory_weight,
-        attend_out, decode_weight, after,
+        attend_out, decode_weight, near, after,
     )
     far = near_core(far)
     halos, front_halo, later = halo_cells(near, slots, weights[1])
@@ -693,7 +705,7 @@
     far_halo = near_core(lax.ppermute(front_halo, "noise", from_second))
     both = (VMEM,) * 2
     lanes = CELLS + 128
-    own_part = own_call(first_own_kernel, lanes, near, plan, levels, queue, halos, *weights[:3])
+    own_part = own_call(first_own_kernel, lanes, near, plan, levels, queue, halos, *weights[:5])
     own, near_message, far_message = pl.pallas_call(
         first_kernel,
         out_shape=(
@@ -701,7 +713,7 @@
             jax.ShapeDtypeStruct((FR_DEV + 1, ROWS, CELLS), BF),
             jax.ShapeDtypeStruct((ROWS, lanes), BF),
         ),
-        in_specs=[*([SMEM] * 3 + [VMEM] * 8), *both, *([VMEM] * 5)],
+        in_specs=[*([SMEM] * 3 + [VMEM] * 8), *both, *([VMEM] * 7)],
         out_specs=(VMEM,) * 3,
         scratch_shapes=[
             *window_scratch(lanes, 2 * FR_DEV),
@@ -716,11 +728,11 @@
     )
     came = near_core(lax.ppermute(near_message, "noise", from_next))
     far = near_core(lax.ppermute(far_message, "noise", from_second))
-    own_part = own_call(second_own_kernel, CELLS, near, plan, levels, own, *weights[:3])
+    own_part = own_call(second_own_kernel, CELLS, near, plan, levels, own, *weights[:5])
     moved = pl.pallas_call(
         second_kernel,
         out_shape=jax.ShapeDtypeStruct((FR_DEV * FIELDS * 2, 128), F32),
-        in_specs=[*([SMEM] * 3 + [VMEM] * 3), *both, *([VMEM] * 5)],
+        in_specs=[*([SMEM] * 3 + [VMEM] * 3), *both, *([VMEM] * 7)],
         out_specs=VMEM,
         scratch_shapes=[*window_scratch(CELLS, 2 * FR_DEV), *attention_scratch(CELLS)],
         compiler_params=pltpu.CompilerParams(vmem_limit_bytes=40 << 20),

time: 56 us -> 55.9 us (level)
  no operation moved by 1% of the time
where the time goes in v7:
time: 55.9 us; the launch traced here: 55.3 us
  Pallas kernels  26.1 us (47%)
  starting transfers between devices  25.7 us (46%)
  waiting for transfers between devices  3.45 us (6%)
    ppermute x1, starting transfers between devices, shards(): next_halos = near_core(lax.ppermute(halos, 'noise', from_next))  8.24 us
    pallas_call x1, Pallas kernels, shards(): pl.pallas_call(first_kernel, out_shape=(jax.ShapeDtypeStruct((FR_DEV, ROW...  7.61 us
    ppermute x1, starting transfers between devices, shards(): next_frames = near_core(lax.ppermute(frames, 'noise', from_next))  6.72 us
    pallas_call x1, Pallas kernels, shards(): pl.pallas_call(second_kernel, out_shape=jax.ShapeDtypeStruct((FR_DEV * FI...  6.15 us
    all_to_all x1, starting transfers between devices, shards(): lax.all_to_all(slots, TILE_AXES, split_axis=0, concat_axis=0, tiled=True)  6.14 us
    pallas_call x2, Pallas kernels, own_call(): pl.pallas_call(kernel, out_shape=(pltpu.VMEM((len(OWN), WIDTH, lanes), F3...  5.94 us
    pallas_call x1, Pallas kernels, prepare_weights(): pl.pallas_call(weights_kernel, out_shape=(pltpu.VMEM((WIDTH, TAPS * ROWS)...  2.97 us
    ppermute x1, starting transfers between devices, shards(): came = near_core(lax.ppermute(near_message, 'noise', from_next))  2.74 us
  transfers between devices with their start and end apart: 7, of which 4 were waited for; matrix products, arithmetic and copies ran while one was open for 0% of the time, Pallas kernels for 18%

profile of v7, /device:TPU:8, one launch (start us, length us, event | category | flops | bytes accessed | tf_op | source)
XLA Modules:
  0.0 55.3 jit_solution(6114297451004876889)
XLA Ops:
  0.0 2.3 %border.1 = (bf16[4,72,256]{2,1,0:T(8,128)(2,1)S(1)}, bf16[72,256]{1,0:T(8,128)(2,1)S(1)}, bf16[16,80,128]{2,1,0:T(8,128)(2,1)}, s32[1]{0:T(128)}) custom-call(s32[4,16]{1,0:T(4,128)} %bitcast.9, f32[17]{0:T(128)} %plan_ref.9, s32[4]{0:T(128)} %level_ref.9, f32[552,128]{1,0:T(8,128)} %bitcast.6, f32[2,69,1,256]{3,2,1,0:T(1,128)} %fresh_ref.3), custom_call_target="tpu_custom_call" | custom-call | tf_op jit(solution)/shard_map/border/pallas_call | solution.py:205
  2.3 6.1 %all-to-all-start = ((bf16[16,80,128]{2,1,0:T(8,128)(2,1)}), bf16[16,80,128]{2,1,0:T(8,128)(2,1)S(1)}, u32[]{:S(2)}, u32[]{:S(2)}) async-start(bf16[16,80,128]{2,1,0:T(8,128)(2,1)} %get-tuple-element.26), calls=%async_computation | async-start | bytes 655360 | tf_op jit(solution)/shard_map/all_to_all | solution.py:696
  8.4 6.7 %collective-permute-start = (bf16[4,72,256]{2,1,0:T(8,128)(2,1)S(1)}, bf16[4,72,256]{2,1,0:T(8,128)(2,1)S(1)}, u32[]{:S(2)}, u32[]{:S(2)}) collective-permute-start(bf16[4,72,256]{2,1,0:T(8,128)(2,1)S(1)} %get-tuple-element.31), channel_id=1, source_target_pairs={{16,0},{32,16},{48,32},{64,48},{80,64},{96,80},{112,96},{128,112},... | collective-permute-start | bytes 442376 | tf_op jit(solution)/shard_map/ppermute | solution.py:695
  15.1 3.0 %weights.1 = (bf16[256,648]{1,0:T(8,128)(2,1)S(1)}, bf16[256,72]{1,0:T(8,128)(2,1)S(1)}, bf16[128,1024]{1,0:T(8,128)(2,1)S(1)}, bf16[384,640]{1,0:T(8,128)(2,1)S...) custom-call(bf16[69,256]{1,0:T(8,128)(2,1)} %bitcast.16, ...), custom_call_target="tpu_custom_call" | custom-call | tf_op jit(solution)/shard_map/weights/pallas_call | solution.py:93
  18.1 0.3 all-to-all-done.slots_ref
  18.4 1.2 %ring.1 = (bf16[4,72,128]{2,1,0:T(8,128)(2,1)S(1)}, bf16[72,128]{1,0:T(8,128)(2,1)S(1)}, bf16[72,128]{1,0:T(8,128)(2,1)S(1)}) custom-call(s32[4,16]{1,0:T(4,128)} %bitcast.11, bf16[16,80,128]{2,1,0:T(8,128)(2,1)S(1)} %all-to-all-done.slots_ref, bf16[256,72]{1,0:T(8,128)(2,1)S(1)} %get-tuple-element.28.wait_ref.lift_ref), custom_call_target="tpu_custom_call" | custom-call | tf_op jit(solution)/shard_map/ring/pallas_call | solution.py:301
  19.6 8.2 %collective-permute-start.1 = (bf16[4,72,128]{2,1,0:T(8,128)(2,1)S(1)}, bf16[4,72,128]{2,1,0:T(8,128)(2,1)S(1)}, u32[]{:S(2)}, u32[]{:S(2)}) collective-permute-start(bf16[4,72,128]{2,1,0:T(8,128)(2,1)S(1)} %get-tuple-element.29.halo_ref), channel_id=1, source_target_pairs={{16,0},{32,16},{48,32},{64,48},{80,64},{96,80},{112,96},{128,112},... | collective-permute-start | bytes 221192 | tf_op jit(solution)/shard_map/ppermute | solution.py:704
  27.8 0.0 collective-permute-start.2
  27.8 0.5 collective-permute-start.3
  28.3 3.4 %shard_map.127 = (f32[3,256,384]{2,1,0:T(8,128)S(1)}, f32[3,96,8,384]{3,2,1,0:T(8,128)S(1)}) custom-call(s32[4,16]{1,0:T(4,128)} %bitcast.12, f32[17]{0:T(128)} %plan_ref.9, s32[4]{0:T(128)} %level_ref.9, f32[552,128]{1,0:T(8,128)} %bitcast.7, bf16[4,72,128]{2,1,0:T(8,128)(2,1)S(1)} %get-tuple-element.29.halo_ref, ...), custom_call_target="tpu_custom_call" | custom-call | tf_op jit(solution)/shard_map/pallas_call | solution.py:669
  31.7 0.9 %collective-permute-done.2.far_ref = bf16[72,256]{1,0:T(8,128)(2,1)S(1)} collective-permute-done((bf16[72,256]{1,0:T(8,128)(2,1)S(1)}, bf16[72,256]{1,0:T(8,128)(2,1)S(1)}, u32[]{:S(2)}, u32[]{:S(2)}) %collective-permute-start.2) | collective-permute-done | bytes 36896 | tf_op jit(solution)/shard_map/ppermute | solution.py:697
  32.7 0.0 collective-permute-done.next_frames_ref
  32.7 0.2 collective-permute-done.3.far_halo_ref
  32.9 0.0 collective-permute-done.1.next_halo_ref
  32.9 7.6 %first.1 = (f32[4,72,384]{2,1,0:T(8,128)S(1)}, bf16[5,72,256]{2,1,0:T(8,128)(2,1)S(1)}, bf16[72,384]{1,0:T(8,128)(2,1)S(1)}) custom-call(s32[4,16]{1,0:T(4,128)} %bitcast.13, f32[17]{0:T(128)} %plan_ref.9, s32[4]{0:T(128)} %level_ref.9, f32[552,128]{1,0:T(8,128)} %bitcast.8, f32[2,69,1,256]{3,2,1,0:T(1,128)} %fresh_ref.3, ...), custom_call_target="tpu_custom_call" | custom-call | tf_op jit(solution)/shard_map/first/pallas_call | solution.py:709
  40.5 2.7 %collective-permute-start.4 = (bf16[5,72,256]{2,1,0:T(8,128)(2,1)S(1)}, bf16[5,72,256]{2,1,0:T(8,128)(2,1)S(1)}, u32[]{:S(2)}, u32[]{:S(2)}) collective-permute-start(bf16[5,72,256]{2,1,0:T(8,128)(2,1)S(1)} %get-tuple-element.43), channel_id=1, source_target_pairs={{16,0},{32,16},{48,32},{64,48},{80,64},{96,80},{112,96},{128,112},... | collective-permute-start | bytes 552968 | tf_op jit(solution)/shard_map/ppermute | solution.py:729
  43.2 1.4 %collective-permute-start.5 = (bf16[72,384]{1,0:T(8,128)(2,1)S(1)}, bf16[72,384]{1,0:T(8,128)(2,1)S(1)}, u32[]{:S(2)}, u32[]{:S(2)}) collective-permute-start(bf16[72,384]{1,0:T(8,128)(2,1)S(1)} %get-tuple-element.44), channel_id=1, source_target_pairs={{32,0},{48,16},{64,32},{80,48},{96,64},{112,80},{128,96},{144,112}... | collective-permute-start | bytes 165896 | tf_op jit(solution)/shard_map/ppermute | solution.py:730
  44.6 2.5 %shard_map.128 = (f32[3,256,256]{2,1,0:T(8,128)S(1)}, f32[3,96,8,256]{3,2,1,0:T(8,128)S(1)}) custom-call(s32[4,16]{1,0:T(4,128)} %bitcast.14, f32[17]{0:T(128)} %plan_ref.9, s32[4]{0:T(128)} %level_ref.9, f32[4,72,384]{2,1,0:T(8,128)S(1)} %get-tuple-element.42.own_ref, bf16[256,648]{1,0:T(8,128)(2,1)S(1)} %get-tuple-element.34.taps_ref, ...), custom_call_target="tpu_custom_call" | custom-call | tf_op jit(solution)/shard_map/pallas_call | solution.py:669
  47.1 2.0 %collective-permute-done.5.far_ref = bf16[72,384]{1,0:T(8,128)(2,1)S(1)} collective-permute-done((bf16[72,384]{1,0:T(8,128)(2,1)S(1)}, bf16[72,384]{1,0:T(8,128)(2,1)S(1)}, u32[]{:S(2)}, u32[]{:S(2)}) %collective-permute-start.5) | collective-permute-done | bytes 55328 | tf_op jit(solution)/shard_map/ppermute | solution.py:730
  49.1 0.0 collective-permute-done.4.came_ref
  49.1 6.2 %second.1 = f32[552,128]{1,0:T(8,128)} custom-call(s32[4,16]{1,0:T(4,128)} %bitcast.15, f32[17]{0:T(128)} %plan_ref.9, s32[4]{0:T(128)} %level_ref.9, f32[4,72,384]{2,1,0:T(8,128)S(1)} %get-tuple-element.42.own_ref, bf16[5,72,256]{2,1,0:T(8,128)(2,1)S(1)} %collective-permute-done.4.came_ref, bf16[72,384]{1,0:T(8,128)(2,1)S(1)} %collective-permute-done.5.far_ref, ...), custom_call_target="tpu_custom_call" | custom-call | tf_op jit(solution)/shard_map/second/pallas_call | solution.py:732
Async XLA Ops:
  2.3 16.2 %all-to-all-start = ((bf16[16,80,128]{2,1,0:T(8,128)(2,1)}), bf16[16,80,128]{2,1,0:T(8,128)(2,1)S(1)}, u32[]{:S(2)}, u32[]{:S(2)}) async-start(bf16[16,80,128]{2,1,0:T(8,128)(2,1)} %get-tuple-element.26), calls=%async_computation | async-start | bytes 655360 | tf_op jit(solution)/shard_map/all_to_all | solution.py:696
  8.4 24.3 %collective-permute-start = (bf16[4,72,256]{2,1,0:T(8,128)(2,1)S(1)}, bf16[4,72,256]{2,1,0:T(8,128)(2,1)S(1)}, u32[]{:S(2)}, u32[]{:S(2)}) collective-permute-start(bf16[4,72,256]{2,1,0:T(8,128)(2,1)S(1)} %get-tuple-element.31), channel_id=1, source_target_pairs={{16,0},{32,16},{48,32},{64,48},{80,64},{96,80},{112,96},{128,112},... | collective-permute-start | bytes 442376 | tf_op jit(solution)/shard_map/ppermute | solution.py:695
  19.6 13.3 %collective-permute-start.1 = (bf16[4,72,128]{2,1,0:T(8,128)(2,1)S(1)}, bf16[4,72,128]{2,1,0:T(8,128)(2,1)S(1)}, u32[]{:S(2)}, u32[]{:S(2)}) collective-permute-start(bf16[4,72,128]{2,1,0:T(8,128)(2,1)S(1)} %get-tuple-element.29.halo_ref), channel_id=1, source_target_pairs={{16,0},{32,16},{48,32},{64,48},{80,64},{96,80},{112,96},{128,112},... | collective-permute-start | bytes 221192 | tf_op jit(solution)/shard_map/ppermute | solution.py:704
  27.8 4.9 %collective-permute-start.2 = (bf16[72,256]{1,0:T(8,128)(2,1)S(1)}, bf16[72,256]{1,0:T(8,128)(2,1)S(1)}, u32[]{:S(2)}, u32[]{:S(2)}) collective-permute-start(bf16[72,256]{1,0:T(8,128)(2,1)S(1)} %get-tuple-element.32), channel_id=1, source_target_pairs={{32,0},{48,16},{64,32},{80,48},{96,64},{112,80},{128,96},{144,112}... | collective-permute-start | bytes 110600 | tf_op jit(solution)/shard_map/ppermute | solution.py:697
  27.8 5.1 %collective-permute-start.3 = (bf16[72,128]{1,0:T(8,128)(2,1)S(1)}, bf16[72,128]{1,0:T(8,128)(2,1)S(1)}, u32[]{:S(2)}, u32[]{:S(2)}) collective-permute-start(bf16[72,128]{1,0:T(8,128)(2,1)S(1)} %get-tuple-element.33), channel_id=1, source_target_pairs={{32,0},{48,16},{64,32},{80,48},{96,64},{112,80},{128,96},{144,112}... | collective-permute-start | bytes 55304 | tf_op jit(solution)/shard_map/ppermute | solution.py:705
  40.5 8.6 %collective-permute-start.4 = (bf16[5,72,256]{2,1,0:T(8,128)(2,1)S(1)}, bf16[5,72,256]{2,1,0:T(8,128)(2,1)S(1)}, u32[]{:S(2)}, u32[]{:S(2)}) collective-permute-start(bf16[5,72,256]{2,1,0:T(8,128)(2,1)S(1)} %get-tuple-element.43), channel_id=1, source_target_pairs={{16,0},{32,16},{48,32},{64,48},{80,64},{96,80},{112,96},{128,112},... | collective-permute-start | bytes 552968 | tf_op jit(solution)/shard_map/ppermute | solution.py:729
  43.2 5.9 %collective-permute-start.5 = (bf16[72,384]{1,0:T(8,128)(2,1)S(1)}, bf16[72,384]{1,0:T(8,128)(2,1)S(1)}, u32[]{:S(2)}, u32[]{:S(2)}) collective-permute-start(bf16[72,384]{1,0:T(8,128)(2,1)S(1)} %get-tuple-element.44), channel_id=1, source_target_pairs={{32,0},{48,16},{64,32},{80,48},{96,64},{112,80},{128,96},{144,112}... | collective-permute-start | bytes 165896 | tf_op jit(solution)/shard_map/ppermute | solution.py:730
